TPU v7x, 32 devices: a whole 2x2x4 slice. The times are simulated.
32 devices in a mesh: dp: 16 (over z, y, x), tensor: 2 (over core).
Axes of the slice: x: 2, y: 2, z: 4, core: 2. Of those that a mesh axis runs over, the one named last changes fastest.
Arguments:
- block_input: bfloat16 [4096, 1024], P(('dp', 'tensor')), may hold values from -32 to 32
- segments: int32 [16, 256], P('dp'), may hold values from 0 to 31, as said below
- positions: int32 [16, 256], P('dp'), may hold values from 0 to 2302, as said below
- norm1_gain: bfloat16 [1024], replicated, may hold values from 0.5 to 1.5
- w_query: bfloat16 [1024, 1024], P('dp', 'tensor'), may hold values from -0.1875 to 0.1875
- w_key: bfloat16 [1024, 512], P('dp', 'tensor'), may hold values from -0.1875 to 0.1875
- w_value: bfloat16 [1024, 512], P('dp', 'tensor'), may hold values from -0.1875 to 0.1875
- w_out: bfloat16 [1024, 1024], P('tensor', 'dp'), may hold values from -0.5 to 0.5
- query_gain: bfloat16 [64], replicated, may hold values from 0.5 to 2
- key_gain: bfloat16 [64], replicated, may hold values from 0.5 to 2
- norm2_gain: bfloat16 [1024], replicated, may hold values from 0.5 to 1.5
- w_gate: bfloat16 [1024, 4608], P('dp', 'tensor'), may hold values from -0.1875 to 0.1875
- w_up: bfloat16 [1024, 4608], P('dp', 'tensor'), may hold values from -0.1875 to 0.1875
- w_down: bfloat16 [4608, 1024], P('tensor', 'dp'), may hold values from -0.1875 to 0.1875
- grad_out: bfloat16 [4096, 1024], P(('dp', 'tensor')), may hold values from -6 to 6
Outputs:
- block_out: bfloat16 [4096, 1024], P(('dp', 'tensor'))
- grad_input: float32 [4096, 1024], P(('dp', 'tensor'))
- grad_norm1_gain: float32 [1024], replicated
- grad_w_query: float32 [1024, 1024], P('dp', 'tensor')
- grad_w_key: float32 [1024, 512], P('dp', 'tensor')
- grad_w_value: float32 [1024, 512], P('dp', 'tensor')
- grad_w_out: float32 [1024, 1024], P('tensor', 'dp')
- grad_query_gain: float32 [64], replicated
- grad_key_gain: float32 [64], replicated
- grad_norm2_gain: float32 [1024], replicated
- grad_w_gate: float32 [1024, 4608], P('dp', 'tensor')
- grad_w_up: float32 [1024, 4608], P('dp', 'tensor')
- grad_w_down: float32 [4608, 1024], P('tensor', 'dp')
Inputs may be any that keep to these rules, and one draw needn't show every extreme that they name: `segments`: in every sequence of 256 tokens the segment numbers start at 0 and never fall; each number is one document, and documents begin only at token indices that are multiples of 8. Within a document positions rise by one from token to token; every document but a sequence's first starts at position 0.
All inputs are finite; a program needn't handle non-finite values.
Results may differ from a plain program's by a relative error of at most 0.013.
The roundings to bfloat16 on the way count: a program that leaves them out, or rounds other values in their place, can miss the bound.
Values may be sent and summed in bfloat16 or wider, within the bound.
No kernel may reach another device: no remote copies, remote signals or barrier semaphores. Data moves between devices by JAX's collectives and lax.ppermute only.
A program may use at most 128 MiB of HBM per device.

v0:
```python
import jax
import jax.numpy as jnp
from jax import lax
from jax.experimental import pallas as pl
from jax.experimental.pallas import tpu as pltpu
from jax.sharding import PartitionSpec as P

HD = 64
PLANE = 4

epsilon = 1e-05
rope_base = 1000000.0
masked_score = -1e30

f32 = jnp.float32
bf16 = jnp.bfloat16

SMALL_COST = pl.CostEstimate(flops=1_000_000, transcendentals=0, bytes_accessed=100_000)


def inverse_rms(values):
    return lax.rsqrt(jnp.mean(values * values, axis=-1, keepdims=True) + epsilon)


def dot_nn(a, b):
    return lax.dot_general(a, b, (((1,), (0,)), ((), ())), preferred_element_type=f32)


def dot_nt(a, b):
    return lax.dot_general(a, b, (((1,), (1,)), ((), ())), preferred_element_type=f32)


def dot_tn(a, b):
    return lax.dot_general(a, b, (((0,), (0,)), ((), ())), preferred_element_type=f32)


def swap_halves(values):
    half = values.shape[-1] // 2
    return jnp.concatenate([values[:, half:], values[:, :half]], axis=-1)


def rope_tables(positions, head_width):
    half_width = head_width // 2
    freq_index = jnp.arange(half_width).astype(f32)
    frequency = rope_base ** (-(2.0 * freq_index) / head_width)
    angles = positions.astype(f32)[..., None] * frequency
    cosine, sine = jnp.cos(angles), jnp.sin(angles)
    return (
        jnp.concatenate([cosine, cosine], axis=-1),
        jnp.concatenate([-sine, sine], axis=-1),
    )


def attention_forward_kernel(
    core_ref,
    own_ref,
    other_ref,
    cos_ref,
    sin_ref,
    seg_col_ref,
    seg_row_ref,
    gain_ref,
    o_own_ref,
    o_other_ref,
    p_ref,
    qkv_ref,
    o_ref,
):
    length = cos_ref.shape[1]
    half = length // 2
    own_rows = pl.ds(pl.multiple_of(core_ref[0] * half, half), half)
    other_rows = pl.ds(pl.multiple_of((1 - core_ref[0]) * half, half), half)
    qkv_ref[own_rows, :] = own_ref[0]
    qkv_ref[other_rows, :] = other_ref[0]
    qkv = qkv_ref[...]
    cosine, sine = cos_ref[0], sin_ref[0]
    row = lax.broadcasted_iota(jnp.int32, (length, length), 0)
    col = lax.broadcasted_iota(jnp.int32, (length, length), 1)
    allowed = (col <= row) & (seg_col_ref[0] == seg_row_ref[0])

    def rotated(lo, gain):
        raw = qkv[:, lo : lo + HD]
        normed = raw * inverse_rms(raw) * gain
        return (normed * cosine + swap_halves(normed) * sine).astype(bf16)

    key = rotated(2 * HD, gain_ref[1:2, :])
    value = qkv[:, 3 * HD : 4 * HD].astype(bf16)
    outs = []
    for head in range(2):
        query = rotated(head * HD, gain_ref[0:1, :])
        scores = jnp.where(allowed, dot_nt(query, key) * HD**-0.5, masked_score)
        row_max = jnp.max(scores, axis=-1, keepdims=True)
        raised = jnp.exp(scores - row_max)
        total = jnp.sum(raised, axis=-1, keepdims=True)
        weights = (raised * (1.0 / total)).astype(bf16)
        p_ref[0, head] = weights
        outs.append(dot_nn(weights, value))
    o_ref[...] = jnp.concatenate(outs, axis=-1)
    o_own_ref[0] = o_ref[own_rows, :].astype(bf16)
    o_other_ref[0] = o_ref[other_rows, :].astype(bf16)


def attention_backward_kernel(
    core_ref,
    own_ref,
    other_ref,
    do_own_ref,
    do_other_ref,
    cos_ref,
    sin_ref,
    gain_ref,
    p_ref,
    d_own_ref,
    d_other_ref,
    dgain_ref,
    qkv_ref,
    do_ref,
):
    length = cos_ref.shape[1]
    half = length // 2
    own_rows = pl.ds(pl.multiple_of(core_ref[0] * half, half), half)
    other_rows = pl.ds(pl.multiple_of((1 - core_ref[0]) * half, half), half)
    qkv_ref[own_rows, :] = own_ref[0]
    qkv_ref[other_rows, :] = other_ref[0]
    do_ref[own_rows, :] = do_own_ref[0].astype(f32)
    do_ref[other_rows, :] = do_other_ref[0].astype(f32)
    qkv = qkv_ref[...]
    cosine, sine = cos_ref[0], sin_ref[0]
    grad_o = do_ref[...].astype(bf16)

    def forward(lo, gain):
        raw = qkv[:, lo : lo + HD]
        scale = inverse_rms(raw)
        unit = raw * scale
        normed = unit * gain
        return unit, scale, (normed * cosine + swap_halves(normed) * sine).astype(bf16)

    def backward(grad_rot, unit, scale, gain):
        grad_normed = grad_rot * cosine - swap_halves(grad_rot) * sine
        gain_part = jnp.sum(unit * grad_normed, axis=0, keepdims=True)
        weighted = grad_normed * gain
        mean = jnp.mean(weighted * unit, axis=-1, keepdims=True)
        return scale * (weighted - unit * mean), gain_part

    query_gain, key_gain = gain_ref[0:1, :], gain_ref[1:2, :]
    key_unit, key_scale, key = forward(2 * HD, key_gain)
    value = qkv[:, 3 * HD : 4 * HD].astype(bf16)
    grad_key = jnp.zeros((length, HD), f32)
    grad_value = jnp.zeros((length, HD), f32)
    query_gain_part = jnp.zeros((1, HD), f32)
    parts = []
    for head in range(2):
        query_unit, query_scale, query = forward(head * HD, query_gain)
        low = p_ref[0, head]
        wide = low.astype(f32)
        grad_head = grad_o[:, head * HD : (head + 1) * HD]
        grad_weights = dot_nt(grad_head, value)
        delta = jnp.sum(wide * grad_weights, axis=-1, keepdims=True)
        grad_scores = (wide * (grad_weights - delta) * HD**-0.5).astype(bf16)
        grad_value += dot_tn(low, grad_head)
        grad_key += dot_tn(grad_scores, query)
        part, gain_part = backward(dot_nn(grad_scores, key), query_unit, query_scale, query_gain)
        query_gain_part += gain_part
        parts.append(part)
    part, key_gain_part = backward(grad_key, key_unit, key_scale, key_gain)
    parts += [part, grad_value]
    qkv_ref[...] = jnp.concatenate(parts, axis=-1)
    d_own_ref[0] = qkv_ref[own_rows, :].astype(bf16)
    d_other_ref[0] = qkv_ref[other_rows, :].astype(bf16)
    dgain_ref[0] = jnp.concatenate([query_gain_part, key_gain_part], axis=-1)


def seq_block(*shape):
    return pl.BlockSpec((1,) + shape, lambda s, c: (s,) + (0,) * len(shape))


def attention_forward(core, own, other, cosine, sine, seg_col, seg_row, gains):
    seqs, half, width = own.shape
    length = 2 * half
    return pl.pallas_call(
        attention_forward_kernel,
        grid_spec=pltpu.PrefetchScalarGridSpec(
            num_scalar_prefetch=1,
            grid=(seqs,),
            in_specs=[
                seq_block(half, width),
                seq_block(half, width),
                seq_block(length, HD),
                seq_block(length, HD),
                seq_block(length, 1),
                seq_block(1, length),
                pl.BlockSpec((2, HD), lambda s, c: (0, 0)),
            ],
            out_specs=[
                seq_block(half, 2 * HD),
                seq_block(half, 2 * HD),
                seq_block(2, length, length),
            ],
            scratch_shapes=[
                pltpu.VMEM((length, width), f32),
                pltpu.VMEM((length, 2 * HD), f32),
            ],
        ),
        out_shape=[
            jax.ShapeDtypeStruct((seqs, half, 2 * HD), bf16),
            jax.ShapeDtypeStruct((seqs, half, 2 * HD), bf16),
            jax.ShapeDtypeStruct((seqs, 2, length, length), bf16),
        ],
        cost_estimate=SMALL_COST,
        name="attention_forward",
    )(core, own, other, cosine, sine, seg_col, seg_row, gains)


def attention_backward(core, own, other, do_own, do_other, cosine, sine, gains, weights):
    seqs, half, width = own.shape
    length = 2 * half
    return pl.pallas_call(
        attention_backward_kernel,
        grid_spec=pltpu.PrefetchScalarGridSpec(
            num_scalar_prefetch=1,
            grid=(seqs,),
            in_specs=[
                seq_block(half, width),
                seq_block(half, width),
                seq_block(half, 2 * HD),
                seq_block(half, 2 * HD),
                seq_block(length, HD),
                seq_block(length, HD),
                pl.BlockSpec((2, HD), lambda s, c: (0, 0)),
                seq_block(2, length, length),
            ],
            out_specs=[
                seq_block(half, width),
                seq_block(half, width),
                seq_block(1, 2 * HD),
            ],
            scratch_shapes=[
                pltpu.VMEM((length, width), f32),
                pltpu.VMEM((length, 2 * HD), f32),
            ],
        ),
        out_shape=[
            jax.ShapeDtypeStruct((seqs, half, width), bf16),
            jax.ShapeDtypeStruct((seqs, half, width), bf16),
            jax.ShapeDtypeStruct((seqs, 1, 2 * HD), f32),
        ],
        cost_estimate=SMALL_COST,
        name="attention_backward",
    )(core, own, other, do_own, do_other, cosine, sine, gains, weights)


def ffn_kernel(n_ref, g_ref, w_ref, dn_ref, y_ref, z_ref, gate_ref, up_ref):
    depth, _, band = w_ref.shape
    units = z_ref.shape[1]

    def over_width(x_ref, lo):
        total = None
        for i in range(depth):
            part = dot_nt(x_ref[:, i * band : (i + 1) * band], w_ref[i, lo : lo + units, :])
            total = part if total is None else total + part
        return total

    gate = over_width(n_ref, 0)
    up = over_width(n_ref, units)
    grad_act = over_width(g_ref, 2 * units)
    sigmoid = 1.0 / (1.0 + jnp.exp(-gate))
    silu = gate * sigmoid
    activated = (silu * up).astype(bf16)
    grad_gate = (grad_act * up * sigmoid * (1.0 + gate * (1.0 - sigmoid))).astype(bf16)
    grad_up = (grad_act * silu).astype(bf16)
    for i in range(depth):
        dn_ref[:, i * band : (i + 1) * band] = (
            dot_nn(grad_gate, w_ref[i, :units, :]) + dot_nn(grad_up, w_ref[i, units : 2 * units, :])
        ).astype(dn_ref.dtype)
    z_ref[...] = activated
    gate_ref[...] = grad_gate
    up_ref[...] = grad_up
    for i in range(depth):
        y_ref[:, i * band : (i + 1) * band] = dot_nn(
            activated, w_ref[i, 2 * units :, :]
        ).astype(y_ref.dtype)


def ffn_half(normed, grads, weights, kind):
    tokens, width = normed.shape
    if weights.shape[2] % 128:
        weights = jnp.moveaxis(weights, 0, 1).reshape(1, weights.shape[1], width)
    units = weights.shape[1] // 3
    tile = tokens // 2

    def rows_of(n):
        return pl.BlockSpec((tile, n), lambda i: (i, 0))

    return pl.pallas_call(
        ffn_kernel,
        grid=(tokens // tile,),
        in_specs=[
            rows_of(width),
            rows_of(width),
            pl.BlockSpec(weights.shape, lambda i: (0, 0, 0)),
        ],
        out_specs=[rows_of(width)] * 2 + [rows_of(units)] * 3,
        out_shape=[jax.ShapeDtypeStruct((tokens, width), kind)] * 2
        + [jax.ShapeDtypeStruct((tokens, units), bf16)] * 3,
        compiler_params=pltpu.CompilerParams(vmem_limit_bytes=48 << 20),
        cost_estimate=SMALL_COST,
        name="ffn_half",
    )(normed, grads, weights)


def ffn_grads_kernel(
    n0_ref, n1_ref, g0_ref, g1_ref, a0_ref, a1_ref, u0_ref, u1_ref, z0_ref, z1_ref, out_ref
):
    units = z0_ref.shape[1]

    def product(x0, x1, y0, y1):
        return (dot_tn(x0[...], y0[...]) + dot_tn(x1[...], y1[...])).astype(bf16)

    out_ref[:, :units] = product(n0_ref, n1_ref, a0_ref, a1_ref)
    out_ref[:, units : 2 * units] = product(n0_ref, n1_ref, u0_ref, u1_ref)
    out_ref[:, 2 * units :] = product(g0_ref, g1_ref, z0_ref, z1_ref)


def ffn_grads_call(normed, grads, gates, ups, activated):
    tokens, width = normed[0].shape
    units = activated[0].shape[1]
    tile = width // 4
    slab = pl.BlockSpec((tokens, tile), lambda i: (0, i))
    whole = pl.BlockSpec((tokens, units), lambda i: (0, 0))
    return pl.pallas_call(
        ffn_grads_kernel,
        grid=(width // tile,),
        in_specs=[slab] * 4 + [whole] * 6,
        out_specs=pl.BlockSpec((tile, 3 * units), lambda i: (i, 0)),
        out_shape=jax.ShapeDtypeStruct((width, 3 * units), bf16),
        compiler_params=pltpu.CompilerParams(vmem_limit_bytes=48 << 20),
        cost_estimate=SMALL_COST,
        name="ffn_grads",
    )(*normed, *grads, *gates, *ups, *activated)


def unxor(blocks, index):
    step = 1
    while step < len(blocks):
        odd = (index & step) != 0
        blocks = [
            jnp.where(odd, blocks[k ^ step], blocks[k]) for k in range(len(blocks))
        ]
        step *= 2
    return blocks


def pick(stacked, index):
    return lax.dynamic_index_in_dim(stacked, index, 0, keepdims=False)


def after(value, *others):
    return lax.optimization_barrier((value,) + others)[0]


def solution(mesh):
    devices = mesh.shape["dp"]
    depth = devices // PLANE
    lines = [[place + PLANE * k for k in range(depth)] for place in range(PLANE)]

    def dp_swap(value, mask):
        return lax.ppermute(value, "dp", [(i, i ^ mask) for i in range(devices)])

    def core_swap(value):
        return lax.ppermute(value, "tensor", [(0, 1), (1, 0)])

    def body(
        block_input,
        segments,
        positions,
        norm1_gain,
        w_query,
        w_key,
        w_value,
        w_out,
        query_gain,
        key_gain,
        norm2_gain,
        w_gate,
        w_up,
        w_down,
        grad_out,
    ):
        me = lax.axis_index("dp")
        core = lax.axis_index("tensor")
        place, level = me % PLANE, me // PLANE
        half, width = block_input.shape
        length = 2 * half
        rows = w_query.shape[0]
        band = PLANE * rows
        units = w_gate.shape[1] // PLANE

        def quarters(*arrays):
            parts = [jnp.moveaxis(a.reshape(rows, PLANE, -1), 1, 0) for a in arrays]
            return jnp.concatenate(parts, axis=-1)

        def plane_exchange(stacked):
            received = [pick(stacked, place)]
            for k in range(1, PLANE):
                received.append(dp_swap(pick(stacked, place ^ k), k))
            return jnp.stack(unxor(received, place))

        def gather_chips(block):
            return jnp.concatenate([block] + [dp_swap(block, k) for k in range(1, PLANE)], axis=0)

        def reduce_chips(mine):
            mine = mine.reshape(PLANE, half, width)
            total = mine[0]
            for k in range(1, PLANE):
                total += dp_swap(mine[k].astype(bf16), k).astype(f32)
            return total

        gain_one = norm1_gain.astype(f32)
        gain_two = norm2_gain.astype(f32)
        head_gains = jnp.stack([query_gain, key_gain]).astype(f32)
        core_index = core.astype(jnp.int32).reshape(1)

        own_x = gather_chips(block_input)
        attn_stack = quarters(w_query, w_key, w_value, w_out.T)
        attn_width = attn_stack.shape[-1]
        layout = jnp.concatenate([segments[0], positions[0] // 256, positions[0] % 256])
        layout_rows = -(-layout.shape[0] // attn_width)
        layout = jnp.pad(layout, (0, layout_rows * attn_width - layout.shape[0]))
        layout = layout.astype(bf16).reshape(layout_rows, attn_width)
        layout_all = jnp.broadcast_to(layout, (PLANE,) + layout.shape)
        attn_stack = jnp.concatenate([attn_stack, layout_all], axis=1)
        received = [pick(attn_stack, place)]
        for k in range(1, PLANE):
            received.append(dp_swap(pick(attn_stack, place ^ k), k))
        layouts = jnp.stack([r[rows:] for r in received]).reshape(PLANE, -1)
        layouts = layouts[:, : 3 * length].astype(f32).reshape(PLANE, 3, length)
        attn_band = jnp.concatenate(unxor([r[:rows] for r in received], place), axis=0)
        attn_band = after(attn_band, own_x)
        ffn_stack = after(quarters(w_gate, w_up, w_down.T), own_x)
        ffn_band = plane_exchange(ffn_stack).reshape(band, 3 * units).T
        bands = [attn_band] + [dp_swap(attn_band, k * PLANE) for k in range(1, depth)]
        attn_weights = jnp.concatenate(unxor(bands, level), axis=0)
        other_x = core_swap(own_x)

        attn_weights = after(attn_weights, ffn_band)
        ffn_weights = lax.all_gather(ffn_band, "dp", axis_index_groups=lines)
        own_go = gather_chips(after(grad_out, ffn_band))

        w_qkv, w_out_t = attn_weights[:, : 4 * HD], attn_weights[:, 4 * HD :]

        def units_of(block):
            wide = block.astype(f32)
            return wide * inverse_rms(wide)

        x_pair = (own_x, other_x)
        n1_pair = [(units_of(x) * gain_one).astype(bf16) for x in x_pair]
        qkv_pair = [dot_nn(n, w_qkv).reshape(PLANE, half, 4 * HD) for n in n1_pair]
        cosine, sine = rope_tables(layouts[:, 1] * 256.0 + layouts[:, 2], HD)
        seg_row, seg_col = layouts[:, 0:1], layouts[:, 0, :, None]
        o_own, o_other, weights = attention_forward(
            core_index, *qkv_pair, cosine, sine, seg_col, seg_row, head_gains
        )
        o_own, o_other = o_own.reshape(-1, 2 * HD), o_other.reshape(-1, 2 * HD)
        o_other = after(o_other, own_go)
        own_go = after(own_go, o_own)
        other_go = core_swap(own_go)

        own_input = block_input.astype(f32)
        scale_one = inverse_rms(own_input)
        unit_one = own_input * scale_one
        sent = core_swap(dot_nt(o_other, w_out_t).astype(bf16))
        hidden = own_input + reduce_chips(dot_nt(o_own, w_out_t) + sent.astype(f32))
        scale_two = inverse_rms(hidden)
        unit_two = hidden * scale_two
        normed_two = (unit_two * gain_two).astype(bf16)
        own_n2 = gather_chips(normed_two)
        other_n2 = core_swap(own_n2)

        dn_other, y_other, z_other, a_other, u_other = ffn_half(
            other_n2, other_go, ffn_weights, bf16
        )
        sent = core_swap(dn_other)
        dn_own, y_own, z_own, a_own, u_own = ffn_half(own_n2, own_go, ffn_weights, f32)
        grad_normed_two = reduce_chips(dn_own + sent.astype(f32))

        ffn_partial = ffn_grads_call(
            (own_n2, other_n2),
            (own_go, other_go),
            (a_own, a_other),
            (u_own, u_other),
            (z_own, z_other),
        )
        ffn_total = lax.psum_scatter(
            ffn_partial.reshape(depth, band, 3 * units), "dp", axis_index_groups=lines
        )

        gain_two_part = jnp.sum(unit_two * grad_normed_two, axis=0)
        weighted_two = grad_normed_two * gain_two
        grad_hidden = grad_out.astype(f32) + scale_two * (
            weighted_two - unit_two * jnp.mean(weighted_two * unit_two, axis=-1, keepdims=True)
        )
        grad_hidden = after(grad_hidden, ffn_partial)
        own_dh = gather_chips(grad_hidden.astype(bf16))
        other_dh = core_swap(own_dh)

        y_sum = after(y_own + core_swap(y_other).astype(f32), own_dh)
        block_out = (hidden + reduce_chips(y_sum)).astype(bf16)

        do_pair = [
            dot_nn(dh, w_out_t).astype(bf16).reshape(PLANE, half, 2 * HD)
            for dh in (own_dh, other_dh)
        ]
        dqkv_own, dqkv_other, head_gain_parts = attention_backward(
            core_index, *qkv_pair, *do_pair, cosine, sine, head_gains, weights
        )
        dqkv_own = after(dqkv_own, block_out).reshape(-1, 4 * HD)
        dqkv_other = dqkv_other.reshape(-1, 4 * HD)

        ffn_total = after(ffn_total, dqkv_own).reshape(PLANE, rows, 3 * units)
        ffn_grads = jnp.moveaxis(plane_exchange(ffn_total), 0, 1).astype(f32)


        sent = core_swap(dot_nt(dqkv_other, w_qkv).astype(bf16))
        dn1_own = dot_nt(dqkv_own, w_qkv)
        dn1_sum = dn1_own + sent.astype(f32)
        grad_normed_one = reduce_chips(dn1_sum)
        attn_partial = jnp.concatenate(
            [
                dot_tn(n1_pair[0], dqkv_own) + dot_tn(n1_pair[1], dqkv_other),
                dot_tn(own_dh, o_own) + dot_tn(other_dh, o_other),
            ],
            axis=-1,
        ).astype(bf16).reshape(depth, band, attn_width)

        gain_one_part = jnp.sum(units_of(own_x) * dn1_sum, axis=0)
        gain_parts = jnp.concatenate(
            [gain_one_part, gain_two_part, jnp.sum(head_gain_parts, axis=(0, 1))]
        )
        gain_count = gain_parts.shape[0]
        gain_rows = -(-gain_count // attn_width)

        def two_parts(sums):
            high = sums.astype(bf16)
            return jnp.concatenate([high, (sums - high.astype(f32)).astype(bf16)], axis=0)

        def joined(extra):
            extra = extra.astype(f32)
            return extra[:gain_rows] + extra[gain_rows:]

        gain_sum = jnp.pad(gain_parts, (0, gain_rows * attn_width - gain_count))
        gain_sum = gain_sum.reshape(gain_rows, attn_width)
        extra = two_parts(gain_sum)
        total = pick(attn_partial, level).astype(f32)
        for k in range(1, depth):
            message = jnp.concatenate([pick(attn_partial, level ^ k), extra], axis=0)
            message = dp_swap(message, k * PLANE)
            total += message[:band].astype(f32)
            gain_sum += joined(message[band:])
        total = total.astype(bf16).reshape(PLANE, rows, attn_width)
        extra = two_parts(gain_sum)
        received = [pick(total, place)]
        for k in range(1, PLANE):
            message = jnp.concatenate([pick(total, place ^ k), extra], axis=0)
            message = dp_swap(message, k)
            received.append(message[:rows])
            gain_sum += joined(message[rows:])
        attn_grads = jnp.stack(unxor(received, place), axis=1).astype(f32)
        gain_sum = (gain_sum + core_swap(gain_sum)).reshape(-1)

        weighted_one = grad_normed_one * gain_one
        grad_input = grad_hidden + scale_one * (
            weighted_one - unit_one * jnp.mean(weighted_one * unit_one, axis=-1, keepdims=True)
        )

        def columns(grads, lo, hi):
            return grads[:, :, lo:hi].reshape(rows, -1)

        return (
            block_out,
            grad_input,
            gain_sum[:width],
            columns(attn_grads, 0, 2 * HD),
            columns(attn_grads, 2 * HD, 3 * HD),
            columns(attn_grads, 3 * HD, 4 * HD),
            columns(attn_grads, 4 * HD, 6 * HD).T,
            gain_sum[2 * width : 2 * width + HD],
            gain_sum[2 * width + HD : 2 * width + 2 * HD],
            gain_sum[width : 2 * width],
            columns(ffn_grads, 0, units),
            columns(ffn_grads, units, 2 * units),
            columns(ffn_grads, 2 * units, 3 * units).T,
        )

    in_specs = (
        P(("dp", "tensor"), None),
        P("dp", None),
        P("dp", None),
        P(),
        P("dp", "tensor"),
        P("dp", "tensor"),
        P("dp", "tensor"),
        P("tensor", "dp"),
        P(),
        P(),
        P(),
        P("dp", "tensor"),
        P("dp", "tensor"),
        P("tensor", "dp"),
        P(("dp", "tensor"), None),
    )
    out_specs = (
        P(("dp", "tensor"), None),
        P(("dp", "tensor"), None),
        P(),
        P("dp", "tensor"),
        P("dp", "tensor"),
        P("dp", "tensor"),
        P("tensor", "dp"),
        P(),
        P(),
        P(),
        P("dp", "tensor"),
        P("dp", "tensor"),
        P("tensor", "dp"),
    )
    return jax.shard_map(body, mesh=mesh, in_specs=in_specs, out_specs=out_specs, check_vma=False)
```

profile of v0, /device:TPU:0, one launch (start us, length us, event | category | flops | bytes accessed | tf_op | source)
XLA Modules:
  0.0 317.9 jit_solution(1260810625229714033)
XLA Ops:
  7.3 3.0 collective-permute-start
  26.8 1.9 fusion.58
  35.6 4.1 %collective-permute-start.6 = (bf16[256,384]{1,0:T(8,128)(2,1)S(1)}, bf16[256,384]{1,0:T(8,128)(2,1)S(1)}, u32[]{:S(2)}, u32[]{:S(2)}) collective-permute-start(bf16[256,384]{1,0:T(8,128)(2,1)S(1)} %pad_maximum_fusion.13), channel_id=1, source_target_pairs={{0,24},{2,26},{4,28},{6,30},{8,16},{10,18},{12,20},{14,22},{16,8},... | collective-permute-start | bytes 589832 | tf_op jit(solution)/shard_map/ppermute | solution.py:367
  40.7 1.9 constant_dynamic-slice_fusion
  42.7 2.7 collective-permute-start.9
  45.5 1.7 collective-permute-start.10
  47.3 7.5 %collective-permute-done.7 = bf16[256,384]{1,0:T(8,128)(2,1)S(1)} collective-permute-done((bf16[256,384]{1,0:T(8,128)(2,1)S(1)}, bf16[256,384]{1,0:T(8,128)(2,1)S(1)}, u32[]{:S(2)}, u32[]{:S(2)}) %collective-permute-start.7) | collective-permute-done | bytes 196640 | tf_op jit(solution)/shard_map/ppermute | solution.py:367
  56.5 4.8 %collective-permute-done.11 = bf16[64,1728]{1,0:T(8,128)(2,1)S(1)} collective-permute-done((bf16[64,1728]{1,0:T(8,128)(2,1)S(1)}, bf16[64,1728]{1,0:T(8,128)(2,1)S(1)}, u32[]{:S(2)}, u32[]{:S(2)}) %collective-permute-start.11) | collective-permute-done | bytes 221216 | tf_op jit(solution)/shard_map/ppermute | solution.py:367
  68.7 3.0 collective-permute-done.13
  72.6 3.1 collective-permute-done.14
  77.7 1.9 fusion.5
  79.6 2.5 fusion.29
  82.1 12.9 %attention_forward.1 = (bf16[4,128,128]{2,1,0:T(8,128)(2,1)}, bf16[4,128,128]{2,1,0:T(8,128)(2,1)}, bf16[4,2,256,256]{3,2,1,0:T(8,128)(2,1)}) custom-call(s32[1]{0:T(128)} %bitcast.core_ref, f32[4,128,256]{2,1,0:T(8,128)} %bitcast.188, f32[4,128,256]{2,1,0:T(8,128)} %bitcast.190, f32[4,256,64]{2,1,0:T(8,128)} %pad_maximum_fusion.4.cos_ref, ...), custom_call_target="tpu_custom_call" | custom-call | flops 1000000 | bytes 100000 | tf_op jit(solution)/shard_map/attention_forward/pallas_call | solution.py:180
  96.4 2.6 collective-permute-done.16
  100.5 1.6 collective-permute-start.19
  102.3 1.8 collective-permute-start.17
  104.1 6.6 %collective-permute-done.19 = bf16[128,1024]{1,0:T(8,128)(2,1)S(1)} collective-permute-done((bf16[128,1024]{1,0:T(8,128)(2,1)S(1)}, bf16[128,1024]{1,0:T(8,128)(2,1)S(1)}, u32[]{:S(2)}, u32[]{:S(2)}) %collective-permute-start.19) | collective-permute-done | bytes 262176 | tf_op jit(solution)/shard_map/ppermute | solution.py:367
  110.7 4.8 %collective-permute-done.18 = bf16[128,1024]{1,0:T(8,128)(2,1)S(1)} collective-permute-done((bf16[128,1024]{1,0:T(8,128)(2,1)S(1)}, bf16[128,1024]{1,0:T(8,128)(2,1)S(1)}, u32[]{:S(2)}, u32[]{:S(2)}) %collective-permute-start.18) | collective-permute-done | bytes 262176 | tf_op jit(solution)/shard_map/ppermute | solution.py:367
  119.5 6.6 %collective-permute-done.22 = bf16[128,1024]{1,0:T(8,128)(2,1)S(1)} collective-permute-done((bf16[128,1024]{1,0:T(8,128)(2,1)S(1)}, bf16[128,1024]{1,0:T(8,128)(2,1)S(1)}, u32[]{:S(2)}, u32[]{:S(2)}) %collective-permute-start.22) | collective-permute-done | bytes 262176 | tf_op jit(solution)/shard_map/ppermute | solution.py:367
  126.2 4.6 %collective-permute-done.21 = bf16[128,1024]{1,0:T(8,128)(2,1)S(1)} collective-permute-done((bf16[128,1024]{1,0:T(8,128)(2,1)S(1)}, bf16[128,1024]{1,0:T(8,128)(2,1)S(1)}, u32[]{:S(2)}, u32[]{:S(2)}) %collective-permute-start.21) | collective-permute-done | bytes 262176 | tf_op jit(solution)/shard_map/ppermute | solution.py:367
  131.0 2.5 collective-permute-done.23.n_ref.n1_ref
  134.6 2.3 all-gather.3.cloned.1.call-done
  138.1 8.9 %ffn_half.3 = (bf16[512,1024]{1,0:T(8,128)(2,1)S(1)}, bf16[512,1024]{1,0:T(8,128)(2,1)}, bf16[512,576]{1,0:T(8,128)(2,1)S(1)}, bf16[512,576]{1,0:T(8,128)(2,1)S(1)}, bf16[512,576]{1,0:T(8,128)(2,1)S(1)}) custom-call(bf16[512,1024]{1,0:T(8,128)(2,1)S(1)} %copy-done.5, bf16[512,1024]{1,0:T(8,128)(2,1)S(1)} %collective-permute-done.24.g_ref.g1_ref, ...), custom_call_target="tpu_custom_call" | custom-call | flops 1000000 | bytes 100000 | tf_op jit(solution)/shard_map/ffn_half/pallas_call | solution.py:294
  146.9 9.0 %ffn_half.2 = (f32[512,1024]{1,0:T(8,128)S(1)}, f32[512,1024]{1,0:T(8,128)}, bf16[512,576]{1,0:T(8,128)(2,1)S(1)}, bf16[512,576]{1,0:T(8,128)(2,1)S(1)}, bf16[512,576]{1,0:T(8,128)(2,1)S(1)}) custom-call(bf16[512,1024]{1,0:T(8,128)(2,1)S(1)} %pad_maximum_fusion.n_ref.n0_ref, bf16[512,1024]{1,0:T(8,128)(2,1)S(1)} %constant_dynamic-update-slice_fusion.4.g_ref.g0_ref, ...), custom_call_target="tpu_custom_call" | custom-call | flops 1000000 | bytes 100000 | tf_op jit(solution)/shard_map/ffn_half/pallas_call | solution.py:294
  156.6 2.4 collective-permute-start.29
  160.1 8.0 %ffn_grads.1 = bf16[1024,1728]{1,0:T(8,128)(2,1)} custom-call(bf16[512,1024]{1,0:T(8,128)(2,1)S(1)} %pad_maximum_fusion.n_ref.n0_ref, bf16[512,1024]{1,0:T(8,128)(2,1)S(1)} %copy-done.5, bf16[512,1024]{1,0:T(8,128)(2,1)} %copy-done.2, bf16[512,1024]{1,0:T(8,128)(2,1)} %copy-done.3, bf16[512,576]{1,0:T(8,128)(2,1)S(1)} %get-tuple-element.51.a0_ref, ...), custom_call_target="tpu_custom_call" | custom-call | flops 1000000 | bytes 100000 | tf_op jit(solution)/shard_map/ffn_grads/pallas_call | solution.py:330
  168.1 3.7 %collective-permute-done.28 = bf16[128,1024]{1,0:T(8,128)(2,1)S(1)} collective-permute-done((bf16[128,1024]{1,0:T(8,128)(2,1)S(1)}, bf16[128,1024]{1,0:T(8,128)(2,1)S(1)}, u32[]{:S(2)}, u32[]{:S(2)}) %collective-permute-start.28) | collective-permute-done | bytes 262176 | tf_op jit(solution)/shard_map/ppermute | solution.py:367
  173.3 1.8 collective-permute-start.32
  176.8 6.6 %collective-permute-done.32 = bf16[128,1024]{1,0:T(8,128)(2,1)S(1)} collective-permute-done((bf16[128,1024]{1,0:T(8,128)(2,1)S(1)}, bf16[128,1024]{1,0:T(8,128)(2,1)S(1)}, u32[]{:S(2)}, u32[]{:S(2)}) %collective-permute-start.32) | collective-permute-done | bytes 262176 | tf_op jit(solution)/shard_map/ppermute | solution.py:367
  183.4 4.6 %collective-permute-done.31 = bf16[128,1024]{1,0:T(8,128)(2,1)S(1)} collective-permute-done((bf16[128,1024]{1,0:T(8,128)(2,1)S(1)}, bf16[128,1024]{1,0:T(8,128)(2,1)S(1)}, u32[]{:S(2)}, u32[]{:S(2)}) %collective-permute-start.31) | collective-permute-done | bytes 262176 | tf_op jit(solution)/shard_map/ppermute | solution.py:367
  189.2 2.1 convert_add_fusion.2
  195.9 2.3 convolution_convert_fusion.3
  198.2 4.5 %collective-permute-done.35 = bf16[128,1024]{1,0:T(8,128)(2,1)} collective-permute-done((bf16[128,1024]{1,0:T(8,128)(2,1)}, bf16[128,1024]{1,0:T(8,128)(2,1)}, u32[]{:S(2)}, u32[]{:S(2)}) %collective-permute-start.35) | collective-permute-done | bytes 262176 | tf_op jit(solution)/shard_map/ppermute | solution.py:367
  202.7 5.2 %collective-permute-done.34 = bf16[128,1024]{1,0:T(8,128)(2,1)} collective-permute-done((bf16[128,1024]{1,0:T(8,128)(2,1)}, bf16[128,1024]{1,0:T(8,128)(2,1)}, u32[]{:S(2)}, u32[]{:S(2)}) %collective-permute-start.34) | collective-permute-done | bytes 262176 | tf_op jit(solution)/shard_map/ppermute | solution.py:367
  207.9 2.0 add_convert_fusion.1
  209.9 2.3 convolution_convert_fusion.2
  212.3 13.0 %attention_backward.1 = (bf16[4,128,256]{2,1,0:T(8,128)(2,1)}, bf16[4,128,256]{2,1,0:T(8,128)(2,1)}, f32[4,1,128]{2,1,0:T(1,128)}) custom-call(s32[1]{0:T(128)} %bitcast.core_ref, f32[4,128,256]{2,1,0:T(8,128)} %bitcast.189, f32[4,128,256]{2,1,0:T(8,128)} %bitcast.191, bf16[4,128,128]{2,1,0:T(8,128)(2,1)} %bitcast.214, bf16[4,128,128]{2,1,0:T(8,128)(2,1)} %bitcast.215, ...), custom_call_target="tpu_custom_call" | custom-call | flops 1000000 | bytes 100000 | tf_op jit(solution)/shard_map/attention_backward/pallas_call | solution.py:217
  226.8 1.7 fusion.80
  228.6 1.8 fusion.8
  230.4 1.8 fusion.35
  234.0 2.9 fusion.3
  240.3 1.6 collective-permute-start.40
  243.9 8.6 %collective-permute-done.43 = bf16[268,384]{1,0:T(8,128)(2,1)S(1)} collective-permute-done((bf16[268,384]{1,0:T(8,128)(2,1)S(1)}, bf16[268,384]{1,0:T(8,128)(2,1)S(1)}, u32[]{:S(2)}, u32[]{:S(2)}) %collective-permute-start.43) | collective-permute-done | bytes 205856 | tf_op jit(solution)/shard_map/ppermute | solution.py:367
  252.5 14.3 %collective-permute-start.41 = (bf16[268,384]{1,0:T(8,128)(2,1)S(1)}, bf16[268,384]{1,0:T(8,128)(2,1)S(1)}, u32[]{:S(2)}, u32[]{:S(2)}) collective-permute-start(bf16[268,384]{1,0:T(8,128)(2,1)S(1)} %get-tuple-element.146), channel_id=1, source_target_pairs={{0,8},{2,10},{4,12},{6,14},{8,0},{10,2},{12,4},{14,6},{16,24},{18,... | collective-permute-start | bytes 617480 | tf_op jit(solution)/shard_map/ppermute | solution.py:367
  266.8 10.8 %collective-permute-done.42 = bf16[268,384]{1,0:T(8,128)(2,1)S(1)} collective-permute-done((bf16[268,384]{1,0:T(8,128)(2,1)S(1)}, bf16[268,384]{1,0:T(8,128)(2,1)S(1)}, u32[]{:S(2)}, u32[]{:S(2)}) %collective-permute-start.42) | collective-permute-done | bytes 205856 | tf_op jit(solution)/shard_map/ppermute | solution.py:367
  278.3 2.5 collective-permute-start.46
  294.8 5.3 %collective-permute-done.48 = bf16[64,1728]{1,0:T(8,128)(2,1)S(1)} collective-permute-done((bf16[64,1728]{1,0:T(8,128)(2,1)S(1)}, bf16[64,1728]{1,0:T(8,128)(2,1)S(1)}, u32[]{:S(2)}, u32[]{:S(2)}) %collective-permute-start.48) | collective-permute-done | bytes 221216 | tf_op jit(solution)/shard_map/ppermute | solution.py:367
  300.1 4.5 %collective-permute-done.49 = bf16[64,1728]{1,0:T(8,128)(2,1)S(1)} collective-permute-done((bf16[64,1728]{1,0:T(8,128)(2,1)S(1)}, bf16[64,1728]{1,0:T(8,128)(2,1)S(1)}, u32[]{:S(2)}, u32[]{:S(2)}) %collective-permute-start.49) | collective-permute-done | bytes 221216 | tf_op jit(solution)/shard_map/ppermute | solution.py:367
  (261 shorter events, 86.5 us)
Async XLA Ops:
  7.3 129.6 %all-gather.3.cloned.1.call-start = ((), (), s32[]{:S(2)}) async-start(), calls=%async_computation.2 | async-start | bytes 4423680 | tf_op jit(solution)/shard_map/all_gather | solution.py:446
  7.3 25.3 %collective-permute-start = (bf16[128,1024]{1,0:T(8,128)(2,1)}, bf16[128,1024]{1,0:T(8,128)(2,1)}, u32[]{:S(2)}, u32[]{:S(2)}) collective-permute-start(bf16[128,1024]{1,0:T(8,128)(2,1)} %param.15), channel_id=1, source_target_pairs={{0,2},{2,0},{4,6},{6,4},{8,10},{10,8},{12,14},{14,12},{16,18},{18,... | collective-permute-start | bytes 786440 | tf_op jit(solution)/shard_map/ppermute | solution.py:367
  10.3 23.3 %collective-permute-start.1 = (bf16[128,1024]{1,0:T(8,128)(2,1)}, bf16[128,1024]{1,0:T(8,128)(2,1)}, u32[]{:S(2)}, u32[]{:S(2)}) collective-permute-start(bf16[128,1024]{1,0:T(8,128)(2,1)} %param.15), channel_id=1, source_target_pairs={{0,4},{2,6},{4,0},{6,2},{8,12},{10,14},{12,8},{14,10},{16,20},{18,... | collective-permute-start | bytes 786440 | tf_op jit(solution)/shard_map/ppermute | solution.py:367
  16.7 8.6 %collective-permute-start.4 = (bf16[66,384]{1,0:T(8,128)(2,1)}, bf16[66,384]{1,0:T(8,128)(2,1)}, u32[]{:S(2)}, u32[]{:S(2)}) collective-permute-start(bf16[66,384]{1,0:T(8,128)(2,1)} %get-tuple-element.134), channel_id=1, source_target_pairs={{0,4},{2,6},{4,0},{6,2},{8,12},{10,14},{12,8},{14,10},{16,20},{18,... | collective-permute-start | bytes 152072 | tf_op jit(solution)/shard_map/ppermute | solution.py:367
  17.2 7.3 %collective-permute-start.3 = (bf16[66,384]{1,0:T(8,128)(2,1)}, bf16[66,384]{1,0:T(8,128)(2,1)}, u32[]{:S(2)}, u32[]{:S(2)}) collective-permute-start(bf16[66,384]{1,0:T(8,128)(2,1)} %get-tuple-element.135), channel_id=1, source_target_pairs={{0,6},{2,4},{4,2},{6,0},{8,14},{10,12},{12,10},{14,8},{16,22},{18,... | collective-permute-start | bytes 152072 | tf_op jit(solution)/shard_map/ppermute | solution.py:367
  18.7 7.3 %collective-permute-start.5 = (bf16[66,384]{1,0:T(8,128)(2,1)S(1)}, bf16[66,384]{1,0:T(8,128)(2,1)}, u32[]{:S(2)}, u32[]{:S(2)}) collective-permute-start(bf16[66,384]{1,0:T(8,128)(2,1)S(1)} %get-tuple-element.133), channel_id=1, source_target_pairs={{0,2},{2,0},{4,6},{6,4},{8,10},{10,8},{12,14},{14,12},{16,18},{18,... | collective-permute-start | bytes 152072 | tf_op jit(solution)/shard_map/ppermute | solution.py:367
  24.5 10.1 %collective-permute-start.2 = (bf16[128,1024]{1,0:T(8,128)(2,1)S(1)}, bf16[128,1024]{1,0:T(8,128)(2,1)}, u32[]{:S(2)}, u32[]{:S(2)}) collective-permute-start(bf16[128,1024]{1,0:T(8,128)(2,1)S(1)} %copy-done.14), channel_id=1, source_target_pairs={{0,6},{2,4},{4,2},{6,0},{8,14},{10,12},{12,10},{14,8},{16,22},{18,... | collective-permute-start | bytes 786440 | tf_op jit(solution)/shard_map/ppermute | solution.py:367
  35.6 9.9 %collective-permute-start.6 = (bf16[256,384]{1,0:T(8,128)(2,1)S(1)}, bf16[256,384]{1,0:T(8,128)(2,1)S(1)}, u32[]{:S(2)}, u32[]{:S(2)}) collective-permute-start(bf16[256,384]{1,0:T(8,128)(2,1)S(1)} %pad_maximum_fusion.13), channel_id=1, source_target_pairs={{0,24},{2,26},{4,28},{6,30},{8,16},{10,18},{12,20},{14,22},{16,8},... | collective-permute-start | bytes 589832 | tf_op jit(solution)/shard_map/ppermute | solution.py:367
  39.7 15.0 %collective-permute-start.7 = (bf16[256,384]{1,0:T(8,128)(2,1)S(1)}, bf16[256,384]{1,0:T(8,128)(2,1)S(1)}, u32[]{:S(2)}, u32[]{:S(2)}) collective-permute-start(bf16[256,384]{1,0:T(8,128)(2,1)S(1)} %pad_maximum_fusion.13), channel_id=1, source_target_pairs={{0,16},{2,18},{4,20},{6,22},{8,24},{10,26},{12,28},{14,30},{16,0},... | collective-permute-start | bytes 589832 | tf_op jit(solution)/shard_map/ppermute | solution.py:367
  39.7 16.5 %collective-permute-start.8 = (bf16[256,384]{1,0:T(8,128)(2,1)S(1)}, bf16[256,384]{1,0:T(8,128)(2,1)S(1)}, u32[]{:S(2)}, u32[]{:S(2)}) collective-permute-start(bf16[256,384]{1,0:T(8,128)(2,1)S(1)} %pad_maximum_fusion.13), channel_id=1, source_target_pairs={{0,8},{2,10},{4,12},{6,14},{8,0},{10,2},{12,4},{14,6},{16,24},{18,... | collective-permute-start | bytes 589832 | tf_op jit(solution)/shard_map/ppermute | solution.py:367
  40.6 37.1 %collective-permute-start.12 = (bf16[512,1024]{1,0:T(8,128)(2,1)S(1)}, bf16[512,1024]{1,0:T(8,128)(2,1)}, u32[]{:S(2)}, u32[]{:S(2)}) collective-permute-start(bf16[512,1024]{1,0:T(8,128)(2,1)S(1)} %constant_dynamic-update-slice_fusion), channel_id=1, source_target_pairs={{0,1},{1,0},{2,3},{3,2},{4,5},{5,4},{6,7},{7,6},{8,9},{9,8},{10,11... | collective-permute-start | bytes 3145736 | tf_op jit(solution)/shard_map/ppermute | solution.py:370
  42.7 13.8 %collective-permute-start.9 = (bf16[64,1728]{1,0:T(8,128)(2,1)S(1)}, bf16[64,1728]{1,0:T(8,128)(2,1)S(1)}, u32[]{:S(2)}, u32[]{:S(2)}) collective-permute-start(bf16[64,1728]{1,0:T(8,128)(2,1)S(1)} %bitcast.209), channel_id=1, source_target_pairs={{0,6},{2,4},{4,2},{6,0},{8,14},{10,12},{12,10},{14,8},{16,22},{18,... | collective-permute-start | bytes 663560 | tf_op jit(solution)/shard_map/ppermute | solution.py:367
  45.5 11.0 %collective-permute-start.10 = (bf16[64,1728]{1,0:T(8,128)(2,1)S(1)}, bf16[64,1728]{1,0:T(8,128)(2,1)S(1)}, u32[]{:S(2)}, u32[]{:S(2)}) collective-permute-start(bf16[64,1728]{1,0:T(8,128)(2,1)S(1)} %bitcast.211), channel_id=1, source_target_pairs={{0,4},{2,6},{4,0},{6,2},{8,12},{10,14},{12,8},{14,10},{16,20},{18,... | collective-permute-start | bytes 663560 | tf_op jit(solution)/shard_map/ppermute | solution.py:367
  54.7 6.6 %collective-permute-start.11 = (bf16[64,1728]{1,0:T(8,128)(2,1)S(1)}, bf16[64,1728]{1,0:T(8,128)(2,1)S(1)}, u32[]{:S(2)}, u32[]{:S(2)}) collective-permute-start(bf16[64,1728]{1,0:T(8,128)(2,1)S(1)} %bitcast.210), channel_id=1, source_target_pairs={{0,2},{2,0},{4,6},{6,4},{8,10},{10,8},{12,14},{14,12},{16,18},{18,... | collective-permute-start | bytes 663560 | tf_op jit(solution)/shard_map/ppermute | solution.py:367
  62.4 9.3 %collective-permute-start.13 = (bf16[128,1024]{1,0:T(8,128)(2,1)S(1)}, bf16[128,1024]{1,0:T(8,128)(2,1)}, u32[]{:S(2)}, u32[]{:S(2)}) collective-permute-start(bf16[128,1024]{1,0:T(8,128)(2,1)S(1)} %copy-done.18), channel_id=1, source_target_pairs={{0,2},{2,0},{4,6},{6,4},{8,10},{10,8},{12,14},{14,12},{16,18},{18,... | collective-permute-start | bytes 786440 | tf_op jit(solution)/shard_map/ppermute | solution.py:367
  63.9 11.8 %collective-permute-start.14 = (bf16[128,1024]{1,0:T(8,128)(2,1)S(1)}, bf16[128,1024]{1,0:T(8,128)(2,1)}, u32[]{:S(2)}, u32[]{:S(2)}) collective-permute-start(bf16[128,1024]{1,0:T(8,128)(2,1)S(1)} %copy-done.18), channel_id=1, source_target_pairs={{0,4},{2,6},{4,0},{6,2},{8,12},{10,14},{12,8},{14,10},{16,20},{18,... | collective-permute-start | bytes 786440 | tf_op jit(solution)/shard_map/ppermute | solution.py:367
  65.4 11.3 %collective-permute-start.15 = (bf16[128,1024]{1,0:T(8,128)(2,1)S(1)}, bf16[128,1024]{1,0:T(8,128)(2,1)}, u32[]{:S(2)}, u32[]{:S(2)}) collective-permute-start(bf16[128,1024]{1,0:T(8,128)(2,1)S(1)} %copy-done.18), channel_id=1, source_target_pairs={{0,6},{2,4},{4,2},{6,0},{8,14},{10,12},{12,10},{14,8},{16,22},{18,... | collective-permute-start | bytes 786440 | tf_op jit(solution)/shard_map/ppermute | solution.py:367
  67.2 222.3 %reduce-scatter.2.cloned.1.call-start = ((), (), s32[]{:S(2)}) async-start(), calls=%async_computation.1 | async-start | bytes 4587520 | tf_op jit(solution)/shard_map/reduce_scatter | solution.py:493
  100.5 10.2 %collective-permute-start.19 = (bf16[128,1024]{1,0:T(8,128)(2,1)S(1)}, bf16[128,1024]{1,0:T(8,128)(2,1)S(1)}, u32[]{:S(2)}, u32[]{:S(2)}) collective-permute-start(bf16[128,1024]{1,0:T(8,128)(2,1)S(1)} %get-tuple-element.102), channel_id=1, source_target_pairs={{0,6},{2,4},{4,2},{6,0},{8,14},{10,12},{12,10},{14,8},{16,22},{18,... | collective-permute-start | bytes 786440 | tf_op jit(solution)/shard_map/ppermute | solution.py:367
  102.1 13.4 %collective-permute-start.18 = (bf16[128,1024]{1,0:T(8,128)(2,1)S(1)}, bf16[128,1024]{1,0:T(8,128)(2,1)S(1)}, u32[]{:S(2)}, u32[]{:S(2)}) collective-permute-start(bf16[128,1024]{1,0:T(8,128)(2,1)S(1)} %get-tuple-element.103), channel_id=1, source_target_pairs={{0,4},{2,6},{4,0},{6,2},{8,12},{10,14},{12,8},{14,10},{16,20},{18,... | collective-permute-start | bytes 786440 | tf_op jit(solution)/shard_map/ppermute | solution.py:367
  102.3 13.3 %collective-permute-start.17 = (bf16[128,1024]{1,0:T(8,128)(2,1)S(1)}, bf16[128,1024]{1,0:T(8,128)(2,1)S(1)}, u32[]{:S(2)}, u32[]{:S(2)}) collective-permute-start(bf16[128,1024]{1,0:T(8,128)(2,1)S(1)} %get-tuple-element.101), channel_id=1, source_target_pairs={{0,2},{2,0},{4,6},{6,4},{8,10},{10,8},{12,14},{14,12},{16,18},{18,... | collective-permute-start | bytes 786440 | tf_op jit(solution)/shard_map/ppermute | solution.py:367
  116.0 10.2 %collective-permute-start.22 = (bf16[128,1024]{1,0:T(8,128)(2,1)S(1)}, bf16[128,1024]{1,0:T(8,128)(2,1)S(1)}, u32[]{:S(2)}, u32[]{:S(2)}) collective-permute-start(bf16[128,1024]{1,0:T(8,128)(2,1)S(1)} %multiply_convert_fusion), channel_id=1, source_target_pairs={{0,6},{2,4},{4,2},{6,0},{8,14},{10,12},{12,10},{14,8},{16,22},{18,... | collective-permute-start | bytes 786440 | tf_op jit(solution)/shard_map/ppermute | solution.py:367
  117.4 13.3 %collective-permute-start.21 = (bf16[128,1024]{1,0:T(8,128)(2,1)S(1)}, bf16[128,1024]{1,0:T(8,128)(2,1)S(1)}, u32[]{:S(2)}, u32[]{:S(2)}) collective-permute-start(bf16[128,1024]{1,0:T(8,128)(2,1)S(1)} %multiply_convert_fusion), channel_id=1, source_target_pairs={{0,4},{2,6},{4,0},{6,2},{8,12},{10,14},{12,8},{14,10},{16,20},{18,... | collective-permute-start | bytes 786440 | tf_op jit(solution)/shard_map/ppermute | solution.py:367
  118.0 12.7 %collective-permute-start.20 = (bf16[128,1024]{1,0:T(8,128)(2,1)S(1)}, bf16[128,1024]{1,0:T(8,128)(2,1)S(1)}, u32[]{:S(2)}, u32[]{:S(2)}) collective-permute-start(bf16[128,1024]{1,0:T(8,128)(2,1)S(1)} %multiply_convert_fusion), channel_id=1, source_target_pairs={{0,2},{2,0},{4,6},{6,4},{8,10},{10,8},{12,14},{14,12},{16,18},{18,... | collective-permute-start | bytes 786440 | tf_op jit(solution)/shard_map/ppermute | solution.py:367
  119.5 11.5 %collective-permute-start.24 = (bf16[512,1024]{1,0:T(8,128)(2,1)S(1)}, bf16[512,1024]{1,0:T(8,128)(2,1)S(1)}, u32[]{:S(2)}, u32[]{:S(2)}) collective-permute-start(bf16[512,1024]{1,0:T(8,128)(2,1)S(1)} %constant_dynamic-update-slice_fusion.4.g_ref.g0_ref), channel_id=1, source_target_pairs={{0,1},{1,0},{2,3},{3,2},{4,5},{5,4},{6,7},{7,6},{8,9},{9,8},{10,11... | collective-permute-start | bytes 3145736 | tf_op jit(solution)/shard_map/ppermute | solution.py:370
  146.9 9.0 %collective-permute-start.26 = (bf16[512,1024]{1,0:T(8,128)(2,1)S(1)}, bf16[512,1024]{1,0:T(8,128)(2,1)S(1)}, u32[]{:S(2)}, u32[]{:S(2)}) collective-permute-start(bf16[512,1024]{1,0:T(8,128)(2,1)S(1)} %get-tuple-element.50), channel_id=1, source_target_pairs={{0,1},{1,0},{2,3},{3,2},{4,5},{5,4},{6,7},{7,6},{8,9},{9,8},{10,11... | collective-permute-start | bytes 3145736 | tf_op jit(solution)/shard_map/ppermute | solution.py:370
  156.6 11.6 %collective-permute-start.29 = (bf16[128,1024]{1,0:T(8,128)(2,1)S(1)}, bf16[128,1024]{1,0:T(8,128)(2,1)S(1)}, u32[]{:S(2)}, u32[]{:S(2)}) collective-permute-start(bf16[128,1024]{1,0:T(8,128)(2,1)S(1)} %get-tuple-element.99), channel_id=1, source_target_pairs={{0,6},{2,4},{4,2},{6,0},{8,14},{10,12},{12,10},{14,8},{16,22},{18,... | collective-permute-start | bytes 786440 | tf_op jit(solution)/shard_map/ppermute | solution.py:367
  159.0 12.8 %collective-permute-start.28 = (bf16[128,1024]{1,0:T(8,128)(2,1)S(1)}, bf16[128,1024]{1,0:T(8,128)(2,1)S(1)}, u32[]{:S(2)}, u32[]{:S(2)}) collective-permute-start(bf16[128,1024]{1,0:T(8,128)(2,1)S(1)} %get-tuple-element.100), channel_id=1, source_target_pairs={{0,4},{2,6},{4,0},{6,2},{8,12},{10,14},{12,8},{14,10},{16,20},{18,... | collective-permute-start | bytes 786440 | tf_op jit(solution)/shard_map/ppermute | solution.py:367
  159.6 12.3 %collective-permute-start.27 = (bf16[128,1024]{1,0:T(8,128)(2,1)S(1)}, bf16[128,1024]{1,0:T(8,128)(2,1)S(1)}, u32[]{:S(2)}, u32[]{:S(2)}) collective-permute-start(bf16[128,1024]{1,0:T(8,128)(2,1)S(1)} %get-tuple-element.98), channel_id=1, source_target_pairs={{0,2},{2,0},{4,6},{6,4},{8,10},{10,8},{12,14},{14,12},{16,18},{18,... | collective-permute-start | bytes 786440 | tf_op jit(solution)/shard_map/ppermute | solution.py:367
  160.1 29.0 %collective-permute-start.25 = (bf16[512,1024]{1,0:T(8,128)(2,1)}, bf16[512,1024]{1,0:T(8,128)(2,1)}, u32[]{:S(2)}, u32[]{:S(2)}) collective-permute-start(bf16[512,1024]{1,0:T(8,128)(2,1)} %get-tuple-element.48), channel_id=1, source_target_pairs={{0,1},{1,0},{2,3},{3,2},{4,5},{5,4},{6,7},{7,6},{8,9},{9,8},{10,11... | collective-permute-start | bytes 3145736 | tf_op jit(solution)/shard_map/ppermute | solution.py:370
  173.3 10.2 %collective-permute-start.32 = (bf16[128,1024]{1,0:T(8,128)(2,1)S(1)}, bf16[128,1024]{1,0:T(8,128)(2,1)S(1)}, u32[]{:S(2)}, u32[]{:S(2)}) collective-permute-start(bf16[128,1024]{1,0:T(8,128)(2,1)S(1)} %convert_element_type.215), channel_id=1, source_target_pairs={{0,6},{2,4},{4,2},{6,0},{8,14},{10,12},{12,10},{14,8},{16,22},{18,... | collective-permute-start | bytes 786440 | tf_op jit(solution)/shard_map/ppermute | solution.py:367
  175.0 13.0 %collective-permute-start.31 = (bf16[128,1024]{1,0:T(8,128)(2,1)S(1)}, bf16[128,1024]{1,0:T(8,128)(2,1)S(1)}, u32[]{:S(2)}, u32[]{:S(2)}) collective-permute-start(bf16[128,1024]{1,0:T(8,128)(2,1)S(1)} %convert_element_type.215), channel_id=1, source_target_pairs={{0,4},{2,6},{4,0},{6,2},{8,12},{10,14},{12,8},{14,10},{16,20},{18,... | collective-permute-start | bytes 786440 | tf_op jit(solution)/shard_map/ppermute | solution.py:367
  176.3 11.8 %collective-permute-start.30 = (bf16[128,1024]{1,0:T(8,128)(2,1)S(1)}, bf16[128,1024]{1,0:T(8,128)(2,1)S(1)}, u32[]{:S(2)}, u32[]{:S(2)}) collective-permute-start(bf16[128,1024]{1,0:T(8,128)(2,1)S(1)} %convert_element_type.215), channel_id=1, source_target_pairs={{0,2},{2,0},{4,6},{6,4},{8,10},{10,8},{12,14},{14,12},{16,18},{18,... | collective-permute-start | bytes 786440 | tf_op jit(solution)/shard_map/ppermute | solution.py:367
  189.1 20.8 %collective-permute-start.36 = (bf16[512,1024]{1,0:T(8,128)(2,1)}, bf16[512,1024]{1,0:T(8,128)(2,1)}, u32[]{:S(2)}, u32[]{:S(2)}) collective-permute-start(bf16[512,1024]{1,0:T(8,128)(2,1)} %pad_maximum_fusion.1), channel_id=1, source_target_pairs={{0,1},{1,0},{2,3},{3,2},{4,5},{5,4},{6,7},{7,6},{8,9},{9,8},{10,11... | collective-permute-start | bytes 3145736 | tf_op jit(solution)/shard_map/ppermute | solution.py:370
  192.4 10.4 %collective-permute-start.35 = (bf16[128,1024]{1,0:T(8,128)(2,1)}, bf16[128,1024]{1,0:T(8,128)(2,1)}, u32[]{:S(2)}, u32[]{:S(2)}) collective-permute-start(bf16[128,1024]{1,0:T(8,128)(2,1)} %get-tuple-element.96), channel_id=1, source_target_pairs={{0,6},{2,4},{4,2},{6,0},{8,14},{10,12},{12,10},{14,8},{16,22},{18,... | collective-permute-start | bytes 786440 | tf_op jit(solution)/shard_map/ppermute | solution.py:367
  193.8 14.1 %collective-permute-start.34 = (bf16[128,1024]{1,0:T(8,128)(2,1)}, bf16[128,1024]{1,0:T(8,128)(2,1)}, u32[]{:S(2)}, u32[]{:S(2)}) collective-permute-start(bf16[128,1024]{1,0:T(8,128)(2,1)} %get-tuple-element.97), channel_id=1, source_target_pairs={{0,4},{2,6},{4,0},{6,2},{8,12},{10,14},{12,8},{14,10},{16,20},{18,... | collective-permute-start | bytes 786440 | tf_op jit(solution)/shard_map/ppermute | solution.py:367
  195.3 12.7 %collective-permute-start.33 = (bf16[128,1024]{1,0:T(8,128)(2,1)}, bf16[128,1024]{1,0:T(8,128)(2,1)}, u32[]{:S(2)}, u32[]{:S(2)}) collective-permute-start(bf16[128,1024]{1,0:T(8,128)(2,1)} %get-tuple-element.95), channel_id=1, source_target_pairs={{0,2},{2,0},{4,6},{6,4},{8,10},{10,8},{12,14},{14,12},{16,18},{18,... | collective-permute-start | bytes 786440 | tf_op jit(solution)/shard_map/ppermute | solution.py:367
  226.7 7.2 %collective-permute-start.37 = (bf16[512,1024]{1,0:T(8,128)(2,1)S(1)}, bf16[512,1024]{1,0:T(8,128)(2,1)}, u32[]{:S(2)}, u32[]{:S(2)}) collective-permute-start(bf16[512,1024]{1,0:T(8,128)(2,1)S(1)} %convolution_convert_fusion.1), channel_id=1, source_target_pairs={{0,1},{1,0},{2,3},{3,2},{4,5},{5,4},{6,7},{7,6},{8,9},{9,8},{10,11... | collective-permute-start | bytes 3145736 | tf_op jit(solution)/shard_map/ppermute | solution.py:370
  238.2 14.4 %collective-permute-start.43 = (bf16[268,384]{1,0:T(8,128)(2,1)S(1)}, bf16[268,384]{1,0:T(8,128)(2,1)S(1)}, u32[]{:S(2)}, u32[]{:S(2)}) collective-permute-start(bf16[268,384]{1,0:T(8,128)(2,1)S(1)} %get-tuple-element.148), channel_id=1, source_target_pairs={{0,24},{2,26},{4,28},{6,30},{8,16},{10,18},{12,20},{14,22},{16,8},... | collective-permute-start | bytes 617480 | tf_op jit(solution)/shard_map/ppermute | solution.py:367
  240.3 41.0 %collective-permute-start.40 = (bf16[128,1024]{1,0:T(8,128)(2,1)S(1)}, bf16[128,1024]{1,0:T(8,128)(2,1)S(1)}, u32[]{:S(2)}, u32[]{:S(2)}) collective-permute-start(bf16[128,1024]{1,0:T(8,128)(2,1)S(1)} %get-tuple-element.93), channel_id=1, source_target_pairs={{0,6},{2,4},{4,2},{6,0},{8,14},{10,12},{12,10},{14,8},{16,22},{18,... | collective-permute-start | bytes 786440 | tf_op jit(solution)/shard_map/ppermute | solution.py:367
  241.8 40.0 %collective-permute-start.39 = (bf16[128,1024]{1,0:T(8,128)(2,1)S(1)}, bf16[128,1024]{1,0:T(8,128)(2,1)S(1)}, u32[]{:S(2)}, u32[]{:S(2)}) collective-permute-start(bf16[128,1024]{1,0:T(8,128)(2,1)S(1)} %get-tuple-element.94), channel_id=1, source_target_pairs={{0,4},{2,6},{4,0},{6,2},{8,12},{10,14},{12,8},{14,10},{16,20},{18,... | collective-permute-start | bytes 786440 | tf_op jit(solution)/shard_map/ppermute | solution.py:367
  243.2 38.6 %collective-permute-start.38 = (bf16[128,1024]{1,0:T(8,128)(2,1)S(1)}, bf16[128,1024]{1,0:T(8,128)(2,1)S(1)}, u32[]{:S(2)}, u32[]{:S(2)}) collective-permute-start(bf16[128,1024]{1,0:T(8,128)(2,1)S(1)} %get-tuple-element.92), channel_id=1, source_target_pairs={{0,2},{2,0},{4,6},{6,4},{8,10},{10,8},{12,14},{14,12},{16,18},{18,... | collective-permute-start | bytes 786440 | tf_op jit(solution)/shard_map/ppermute | solution.py:367
  243.8 33.8 %collective-permute-start.42 = (bf16[268,384]{1,0:T(8,128)(2,1)S(1)}, bf16[268,384]{1,0:T(8,128)(2,1)S(1)}, u32[]{:S(2)}, u32[]{:S(2)}) collective-permute-start(bf16[268,384]{1,0:T(8,128)(2,1)S(1)} %get-tuple-element.147), channel_id=1, source_target_pairs={{0,16},{2,18},{4,20},{6,22},{8,24},{10,26},{12,28},{14,30},{16,0},... | collective-permute-start | bytes 617480 | tf_op jit(solution)/shard_map/ppermute | solution.py:367
  252.5 25.5 %collective-permute-start.41 = (bf16[268,384]{1,0:T(8,128)(2,1)S(1)}, bf16[268,384]{1,0:T(8,128)(2,1)S(1)}, u32[]{:S(2)}, u32[]{:S(2)}) collective-permute-start(bf16[268,384]{1,0:T(8,128)(2,1)S(1)} %get-tuple-element.146), channel_id=1, source_target_pairs={{0,8},{2,10},{4,12},{6,14},{8,0},{10,2},{12,4},{14,6},{16,24},{18,... | collective-permute-start | bytes 617480 | tf_op jit(solution)/shard_map/ppermute | solution.py:367
  278.3 5.2 %collective-permute-start.46 = (bf16[76,384]{1,0:T(8,128)(2,1)S(1)}, bf16[76,384]{1,0:T(8,128)(2,1)S(1)}, u32[]{:S(2)}, u32[]{:S(2)}) collective-permute-start(bf16[76,384]{1,0:T(8,128)(2,1)S(1)} %get-tuple-element.145), channel_id=1, source_target_pairs={{0,6},{2,4},{4,2},{6,0},{8,14},{10,12},{12,10},{14,8},{16,22},{18,... | collective-permute-start | bytes 175112 | tf_op jit(solution)/shard_map/ppermute | solution.py:367
  290.7 9.4 %collective-permute-start.48 = (bf16[64,1728]{1,0:T(8,128)(2,1)S(1)}, bf16[64,1728]{1,0:T(8,128)(2,1)S(1)}, u32[]{:S(2)}, u32[]{:S(2)}) collective-permute-start(bf16[64,1728]{1,0:T(8,128)(2,1)S(1)} %get-tuple-element.106), channel_id=1, source_target_pairs={{0,6},{2,4},{4,2},{6,0},{8,14},{10,12},{12,10},{14,8},{16,22},{18,... | collective-permute-start | bytes 663560 | tf_op jit(solution)/shard_map/ppermute | solution.py:367
  292.2 12.3 %collective-permute-start.49 = (bf16[64,1728]{1,0:T(8,128)(2,1)S(1)}, bf16[64,1728]{1,0:T(8,128)(2,1)S(1)}, u32[]{:S(2)}, u32[]{:S(2)}) collective-permute-start(bf16[64,1728]{1,0:T(8,128)(2,1)S(1)} %get-tuple-element.105), channel_id=1, source_target_pairs={{0,4},{2,6},{4,0},{6,2},{8,12},{10,14},{12,8},{14,10},{16,20},{18,... | collective-permute-start | bytes 663560 | tf_op jit(solution)/shard_map/ppermute | solution.py:367
  292.8 11.9 %collective-permute-start.50 = (bf16[64,1728]{1,0:T(8,128)(2,1)S(1)}, bf16[64,1728]{1,0:T(8,128)(2,1)S(1)}, u32[]{:S(2)}, u32[]{:S(2)}) collective-permute-start(bf16[64,1728]{1,0:T(8,128)(2,1)S(1)} %get-tuple-element.104), channel_id=1, source_target_pairs={{0,2},{2,0},{4,6},{6,4},{8,10},{10,8},{12,14},{14,12},{16,18},{18,... | collective-permute-start | bytes 663560 | tf_op jit(solution)/shard_map/ppermute | solution.py:367
  (37 other events, 491.6 us)
Sparse Core Ops, SparseCore 0:
  67.3 69.5 all-gather.2
  196.0 74.9 reduce-scatter.1
where the time goes:
time: 319 us; the launch traced here: 318 us
  waiting for transfers between devices  105 us (33%)
  starting transfers between devices  66.7 us (21%)
  Pallas kernels  51.7 us (16%)
  local copies, waits for them, and re-layouts  36.1 us (11%)
  other arithmetic  21.5 us (7%)
  matrix products  21.5 us (7%)
  between operations  14.9 us (5%)
    ppermute x42, waiting for transfers between devices, dp_swap(): return lax.ppermute(value, 'dp', [(i, i ^ mask) for i in range(devices)])  97.9 us
    ppermute x42, starting transfers between devices, dp_swap(): return lax.ppermute(value, 'dp', [(i, i ^ mask) for i in range(devices)])  65.9 us
    pallas_call x2, Pallas kernels, ffn_half(): pl.pallas_call(ffn_kernel, grid=(tokens // tile,), in_specs=[rows_of(widt...  17.9 us
    pallas_call x1, Pallas kernels, attention_backward(): pl.pallas_call(attention_backward_kernel, grid_spec=pltpu.PrefetchScalarG...  13 us
    pallas_call x1, Pallas kernels, attention_forward(): pl.pallas_call(attention_forward_kernel, grid_spec=pltpu.PrefetchScalarGr...  12.9 us
    unnamed x75, local copies, waits for them, and re-layouts  8.99 us
    dot_general x4, matrix products, dot_nn(): lax.dot_general(a, b, (((1,), (0,)), ((), ())), preferred_element_type=f32)  8.44 us
    pallas_call x1, Pallas kernels, ffn_grads_call(): pl.pallas_call(ffn_grads_kernel, grid=(width // tile,), in_specs=[slab] *...  7.99 us
  transfers between devices with their start and end apart: 53, of which 30 were waited for; matrix products, arithmetic and copies ran while one was open for 21% of the time, Pallas kernels for 13%

commit v1 on v0

--- a/solution.py
+++ b/solution.py
@@ -1,6 +1,7 @@
 import jax
 import jax.numpy as jnp
 from jax import lax
+from jax.experimental.layout import Layout, with_layout_constraint
 from jax.experimental import pallas as pl
 from jax.experimental.pallas import tpu as pltpu
 from jax.sharding import PartitionSpec as P
@@ -249,43 +250,26 @@
     )(core, own, other, do_own, do_other, cosine, sine, gains, weights)
 
 
-def ffn_kernel(n_ref, g_ref, w_ref, dn_ref, y_ref, z_ref, gate_ref, up_ref):
-    depth, _, band = w_ref.shape
+def ffn_kernel(n_ref, g_ref, w_ref, dn_ref, y_ref, z_ref, d_ref):
     units = z_ref.shape[1]
-
-    def over_width(x_ref, lo):
-        total = None
-        for i in range(depth):
-            part = dot_nt(x_ref[:, i * band : (i + 1) * band], w_ref[i, lo : lo + units, :])
-            total = part if total is None else total + part
-        return total
-
-    gate = over_width(n_ref, 0)
-    up = over_width(n_ref, units)
-    grad_act = over_width(g_ref, 2 * units)
+    gate_up = dot_nn(n_ref[...], w_ref[:, : 2 * units])
+    grad_act = dot_nn(g_ref[...], w_ref[:, 2 * units :])
+    gate, up = gate_up[:, :units], gate_up[:, units:]
     sigmoid = 1.0 / (1.0 + jnp.exp(-gate))
     silu = gate * sigmoid
     activated = (silu * up).astype(bf16)
-    grad_gate = (grad_act * up * sigmoid * (1.0 + gate * (1.0 - sigmoid))).astype(bf16)
-    grad_up = (grad_act * silu).astype(bf16)
-    for i in range(depth):
-        dn_ref[:, i * band : (i + 1) * band] = (
-            dot_nn(grad_gate, w_ref[i, :units, :]) + dot_nn(grad_up, w_ref[i, units : 2 * units, :])
-        ).astype(dn_ref.dtype)
+    grad_gate = grad_act * up * sigmoid * (1.0 + gate * (1.0 - sigmoid))
+    grad = jnp.concatenate([grad_gate, grad_act * silu], axis=-1).astype(bf16)
+    d_ref[...] = grad
     z_ref[...] = activated
-    gate_ref[...] = grad_gate
-    up_ref[...] = grad_up
-    for i in range(depth):
-        y_ref[:, i * band : (i + 1) * band] = dot_nn(
-            activated, w_ref[i, 2 * units :, :]
-        ).astype(y_ref.dtype)
+    dn_ref[...] = dot_nt(grad, w_ref[:, : 2 * units]).astype(dn_ref.dtype)
+    y_ref[...] = dot_nt(activated, w_ref[:, 2 * units :]).astype(y_ref.dtype)
 
 
 def ffn_half(normed, grads, weights, kind):
     tokens, width = normed.shape
-    if weights.shape[2] % 128:
-        weights = jnp.moveaxis(weights, 0, 1).reshape(1, weights.shape[1], width)
-    units = weights.shape[1] // 3
+    columns = weights.shape[1]
+    units = columns // 3
     tile = tokens // 2
 
     def rows_of(n):
@@ -297,46 +281,53 @@
         in_specs=[
             rows_of(width),
             rows_of(width),
-            pl.BlockSpec(weights.shape, lambda i: (0, 0, 0)),
+            pl.BlockSpec((width, columns), lambda i: (0, 0)),
         ],
-        out_specs=[rows_of(width)] * 2 + [rows_of(units)] * 3,
+        out_specs=[rows_of(width)] * 2 + [rows_of(units), rows_of(2 * units)],
         out_shape=[jax.ShapeDtypeStruct((tokens, width), kind)] * 2
-        + [jax.ShapeDtypeStruct((tokens, units), bf16)] * 3,
+        + [
+            jax.ShapeDtypeStruct((tokens, units), bf16),
+            jax.ShapeDtypeStruct((tokens, 2 * units), bf16),
+        ],
         compiler_params=pltpu.CompilerParams(vmem_limit_bytes=48 << 20),
         cost_estimate=SMALL_COST,
         name="ffn_half",
     )(normed, grads, weights)
 
 
-def ffn_grads_kernel(
-    n0_ref, n1_ref, g0_ref, g1_ref, a0_ref, a1_ref, u0_ref, u1_ref, z0_ref, z1_ref, out_ref
-):
-    units = z0_ref.shape[1]
+def ffn_grads_kernel(n0_ref, n1_ref, g0_ref, g1_ref, d0_ref, d1_ref, z0_ref, z1_ref, out_ref):
+    pair = d0_ref.shape[1]
 
     def product(x0, x1, y0, y1):
         return (dot_tn(x0[...], y0[...]) + dot_tn(x1[...], y1[...])).astype(bf16)
 
-    out_ref[:, :units] = product(n0_ref, n1_ref, a0_ref, a1_ref)
-    out_ref[:, units : 2 * units] = product(n0_ref, n1_ref, u0_ref, u1_ref)
-    out_ref[:, 2 * units :] = product(g0_ref, g1_ref, z0_ref, z1_ref)
-
-
-def ffn_grads_call(normed, grads, gates, ups, activated):
+    out_ref[:, :pair] = product(n0_ref, n1_ref, d0_ref, d1_ref)
+    out_ref[:, pair:] = product(g0_ref, g1_ref, z0_ref, z1_ref)
+
+
+def ffn_grads_call(normed, grads, grad_pairs, activated):
     tokens, width = normed[0].shape
     units = activated[0].shape[1]
     tile = width // 4
     slab = pl.BlockSpec((tokens, tile), lambda i: (0, i))
-    whole = pl.BlockSpec((tokens, units), lambda i: (0, 0))
+
+    def whole(n):
+        return pl.BlockSpec((tokens, n), lambda i: (0, 0))
+
     return pl.pallas_call(
         ffn_grads_kernel,
         grid=(width // tile,),
-        in_specs=[slab] * 4 + [whole] * 6,
+        in_specs=[slab] * 4 + [whole(2 * units)] * 2 + [whole(units)] * 2,
         out_specs=pl.BlockSpec((tile, 3 * units), lambda i: (i, 0)),
         out_shape=jax.ShapeDtypeStruct((width, 3 * units), bf16),
         compiler_params=pltpu.CompilerParams(vmem_limit_bytes=48 << 20),
-        cost_estimate=SMALL_COST,
+        cost_estimate=pl.CostEstimate(
+            flops=4 * tokens * width * 3 * units,
+            transcendentals=0,
+            bytes_accessed=4 * tokens * (2 * width + 3 * units) + 6 * width * units,
+        ),
         name="ffn_grads",
-    )(*normed, *grads, *gates, *ups, *activated)
+    )(*normed, *grads, *grad_pairs, *activated)
 
 
 def unxor(blocks, index):
@@ -399,20 +390,21 @@
             parts = [jnp.moveaxis(a.reshape(rows, PLANE, -1), 1, 0) for a in arrays]
             return jnp.concatenate(parts, axis=-1)
 
-        def plane_exchange(stacked):
+        def plane_exchange(stacked, *marks):
             received = [pick(stacked, place)]
             for k in range(1, PLANE):
-                received.append(dp_swap(pick(stacked, place ^ k), k))
+                received.append(after(dp_swap(pick(stacked, place ^ k), k), *marks))
             return jnp.stack(unxor(received, place))
 
-        def gather_chips(block):
-            return jnp.concatenate([block] + [dp_swap(block, k) for k in range(1, PLANE)], axis=0)
-
-        def reduce_chips(mine):
+        def gather_chips(block, *marks):
+            chips = [block] + [after(dp_swap(block, k), *marks) for k in range(1, PLANE)]
+            return jnp.concatenate(chips, axis=0)
+
+        def reduce_chips(mine, *marks):
             mine = mine.reshape(PLANE, half, width)
             total = mine[0]
             for k in range(1, PLANE):
-                total += dp_swap(mine[k].astype(bf16), k).astype(f32)
+                total += after(dp_swap(mine[k].astype(bf16), k), *marks).astype(f32)
             return total
 
         gain_one = norm1_gain.astype(f32)
@@ -420,7 +412,6 @@
         head_gains = jnp.stack([query_gain, key_gain]).astype(f32)
         core_index = core.astype(jnp.int32).reshape(1)
 
-        own_x = gather_chips(block_input)
         attn_stack = quarters(w_query, w_key, w_value, w_out.T)
         attn_width = attn_stack.shape[-1]
         layout = jnp.concatenate([segments[0], positions[0] // 256, positions[0] % 256])
@@ -435,16 +426,18 @@
         layouts = jnp.stack([r[rows:] for r in received]).reshape(PLANE, -1)
         layouts = layouts[:, : 3 * length].astype(f32).reshape(PLANE, 3, length)
         attn_band = jnp.concatenate(unxor([r[:rows] for r in received], place), axis=0)
-        attn_band = after(attn_band, own_x)
-        ffn_stack = after(quarters(w_gate, w_up, w_down.T), own_x)
-        ffn_band = plane_exchange(ffn_stack).reshape(band, 3 * units).T
-        bands = [attn_band] + [dp_swap(attn_band, k * PLANE) for k in range(1, depth)]
+        ffn_stack = after(quarters(w_gate, w_up, w_down.T), attn_stack)
+        ffn_stack = with_layout_constraint(ffn_stack, Layout(major_to_minor=(0, 1, 2)))
+        ffn_band = plane_exchange(ffn_stack).reshape(band, 3 * units)
+        ffn_weights = lax.all_gather(ffn_band, "dp", axis_index_groups=lines)
+        ffn_weights = ffn_weights.reshape(width, 3 * units)
+
+        bands = [attn_band]
+        for k in range(1, depth):
+            bands.append(dp_swap(attn_band, k * PLANE))
         attn_weights = jnp.concatenate(unxor(bands, level), axis=0)
+        own_x = gather_chips(after(block_input, ffn_band))
         other_x = core_swap(own_x)
-
-        attn_weights = after(attn_weights, ffn_band)
-        ffn_weights = lax.all_gather(ffn_band, "dp", axis_index_groups=lines)
-        own_go = gather_chips(after(grad_out, ffn_band))
 
         w_qkv, w_out_t = attn_weights[:, : 4 * HD], attn_weights[:, 4 * HD :]
 
@@ -455,14 +448,15 @@
         x_pair = (own_x, other_x)
         n1_pair = [(units_of(x) * gain_one).astype(bf16) for x in x_pair]
         qkv_pair = [dot_nn(n, w_qkv).reshape(PLANE, half, 4 * HD) for n in n1_pair]
+        layouts = after(layouts, ffn_band)
         cosine, sine = rope_tables(layouts[:, 1] * 256.0 + layouts[:, 2], HD)
         seg_row, seg_col = layouts[:, 0:1], layouts[:, 0, :, None]
         o_own, o_other, weights = attention_forward(
             core_index, *qkv_pair, cosine, sine, seg_col, seg_row, head_gains
         )
         o_own, o_other = o_own.reshape(-1, 2 * HD), o_other.reshape(-1, 2 * HD)
+        own_go = gather_chips(after(grad_out, attn_weights, own_x), o_own)
         o_other = after(o_other, own_go)
-        own_go = after(own_go, o_own)
         other_go = core_swap(own_go)
 
         own_input = block_input.astype(f32)
@@ -476,18 +470,19 @@
         own_n2 = gather_chips(normed_two)
         other_n2 = core_swap(own_n2)
 
-        dn_other, y_other, z_other, a_other, u_other = ffn_half(
+        dn_other, y_other, z_other, d_other = ffn_half(
             other_n2, other_go, ffn_weights, bf16
         )
         sent = core_swap(dn_other)
-        dn_own, y_own, z_own, a_own, u_own = ffn_half(own_n2, own_go, ffn_weights, f32)
-        grad_normed_two = reduce_chips(dn_own + sent.astype(f32))
+        dn_own, y_own, z_own, d_own = ffn_half(after(own_n2, dn_other), own_go, ffn_weights, f32)
+        dn_sum = dn_own + sent.astype(f32)
+        grad_normed_two = reduce_chips(dn_sum)
+        d_own = after(d_own, dn_sum)
 
         ffn_partial = ffn_grads_call(
             (own_n2, other_n2),
             (own_go, other_go),
-            (a_own, a_other),
-            (u_own, u_other),
+            (d_own, d_other),
             (z_own, z_other),
         )
         ffn_total = lax.psum_scatter(
@@ -516,14 +511,10 @@
         dqkv_own = after(dqkv_own, block_out).reshape(-1, 4 * HD)
         dqkv_other = dqkv_other.reshape(-1, 4 * HD)
 
-        ffn_total = after(ffn_total, dqkv_own).reshape(PLANE, rows, 3 * units)
-        ffn_grads = jnp.moveaxis(plane_exchange(ffn_total), 0, 1).astype(f32)
-
-
+        ffn_total = after(ffn_total, dqkv_own)
         sent = core_swap(dot_nt(dqkv_other, w_qkv).astype(bf16))
         dn1_own = dot_nt(dqkv_own, w_qkv)
         dn1_sum = dn1_own + sent.astype(f32)
-        grad_normed_one = reduce_chips(dn1_sum)
         attn_partial = jnp.concatenate(
             [
                 dot_tn(n1_pair[0], dqkv_own) + dot_tn(n1_pair[1], dqkv_other),
@@ -551,11 +542,18 @@
         gain_sum = gain_sum.reshape(gain_rows, attn_width)
         extra = two_parts(gain_sum)
         total = pick(attn_partial, level).astype(f32)
+        messages = []
         for k in range(1, depth):
             message = jnp.concatenate([pick(attn_partial, level ^ k), extra], axis=0)
-            message = dp_swap(message, k * PLANE)
+            message = dp_swap(after(message, ffn_total), k * PLANE)
+            messages.append(message)
             total += message[:band].astype(f32)
             gain_sum += joined(message[band:])
+        ffn_grads = plane_exchange(ffn_total.reshape(PLANE, rows, 3 * units), *messages)
+        ffn_grads = jnp.moveaxis(ffn_grads, 0, 1).astype(f32)
+
+
+        grad_normed_one = reduce_chips(dn1_sum, ffn_grads)
         total = total.astype(bf16).reshape(PLANE, rows, attn_width)
         extra = two_parts(gain_sum)
         received = [pick(total, place)]

time: 319 us -> 286 us (0.90)
  waiting for transfers between devices: 105 us -> 86.5 us
  starting transfers between devices: 66.7 us -> 54.9 us
  other arithmetic: 21.5 us -> 30 us
  matrix products: 21.5 us -> 14.6 us
    ppermute x42, waiting for transfers between devices: 97.9 us -> 80.2 us  [dp_swap(): return lax.ppermute(value, 'dp', [(i, i ^ mask) for i in range(devices)])]
    ppermute x42, starting transfers between devices: 65.9 us -> 54.2 us  [dp_swap(): return lax.ppermute(value, 'dp', [(i, i ^ mask) for i in range(devices)])]
    all_gather x0 -> x1, local copies, waits for them, and re-layouts: none -> 5.84 us  [body(): ffn_weights = lax.all_gather(ffn_band, 'dp', axis_index_groups=lines)]
    dot_general x4, matrix products: 8.44 us -> 4.78 us  [dot_nn(): lax.dot_general(a, b, (((1,), (0,)), ((), ())), preferred_element_type=f32)]
    unnamed x75 -> x97, local copies, waits for them, and re-layouts: 8.99 us -> 5.95 us
  transfers between devices with their start and end apart: 53 -> 53, of which waited for: 30 -> 25; matrix products, arithmetic and copies ran while one was open for 21% -> 22% of each run, Pallas kernels for 13% -> 12%
where the time goes in v1:
time: 286 us; the launch traced here: 284 us
  waiting for transfers between devices  86.5 us (30%)
  starting transfers between devices  54.9 us (19%)
  Pallas kernels  49.3 us (17%)
  local copies, waits for them, and re-layouts  34.2 us (12%)
  other arithmetic  30 us (10%)
  between operations  15 us (5%)
  matrix products  14.6 us (5%)
    ppermute x42, waiting for transfers between devices, dp_swap(): return lax.ppermute(value, 'dp', [(i, i ^ mask) for i in range(devices)])  80.2 us
    ppermute x42, starting transfers between devices, dp_swap(): return lax.ppermute(value, 'dp', [(i, i ^ mask) for i in range(devices)])  54.2 us
    pallas_call x2, Pallas kernels, ffn_half(): pl.pallas_call(ffn_kernel, grid=(tokens // tile,), in_specs=[rows_of(widt...  15.3 us
    pallas_call x1, Pallas kernels, attention_backward(): pl.pallas_call(attention_backward_kernel, grid_spec=pltpu.PrefetchScalarG...  13 us
    pallas_call x1, Pallas kernels, attention_forward(): pl.pallas_call(attention_forward_kernel, grid_spec=pltpu.PrefetchScalarGr...  12.9 us
    pallas_call x1, Pallas kernels, ffn_grads_call(): pl.pallas_call(ffn_grads_kernel, grid=(width // tile,), in_specs=[slab] *...  8.11 us
    reshape x7, local copies, waits for them, and re-layouts, columns(): return grads[:, :, lo:hi].reshape(rows, -1)  6.57 us
    dot_general x4, matrix products, dot_nt(): lax.dot_general(a, b, (((1,), (1,)), ((), ())), preferred_element_type=f32)  6.17 us
  transfers between devices with their start and end apart: 53, of which 25 were waited for; matrix products, arithmetic and copies ran while one was open for 22% of the time, Pallas kernels for 12%

profile of v1, /device:TPU:0, one launch (start us, length us, event | category | flops | bytes accessed | tf_op | source)
XLA Modules:
  0.0 284.5 jit_solution(7832493346382817881)
XLA Ops:
  12.2 3.0 %collective-permute-start.7 = (bf16[66,384]{1,0:T(8,128)(2,1)}, bf16[66,384]{1,0:T(8,128)(2,1)}, u32[]{:S(2)}, u32[]{:S(2)}) collective-permute-start(bf16[66,384]{1,0:T(8,128)(2,1)} %get-tuple-element.152), channel_id=1, source_target_pairs={{0,4},{2,6},{4,0},{6,2},{8,12},{10,14},{12,8},{14,10},{16,20},{18,... | collective-permute-start | bytes 152072 | tf_op jit(solution)/shard_map/ppermute | solution.py:358
  15.2 1.4 collective-permute-start.6
  19.5 3.0 %collective-permute-start = (bf16[64,1728]{1,0:T(8,128)(2,1)S(1)}, bf16[64,1728]{1,0:T(8,128)(2,1)S(1)}, u32[]{:S(2)}, u32[]{:S(2)}) collective-permute-start(bf16[64,1728]{1,0:T(8,128)(2,1)S(1)} %get-tuple-element.131), channel_id=1, source_target_pairs={{0,6},{2,4},{4,2},{6,0},{8,14},{10,12},{12,10},{14,8},{16,22},{18,... | collective-permute-start | bytes 663560 | tf_op jit(solution)/shard_map/ppermute | solution.py:358
  25.4 3.0 %collective-permute-start.10 = (bf16[256,384]{1,0:T(8,128)(2,1)}, bf16[256,384]{1,0:T(8,128)(2,1)S(1)}, u32[]{:S(2)}, u32[]{:S(2)}) collective-permute-start(bf16[256,384]{1,0:T(8,128)(2,1)} %pad_maximum_fusion.14), channel_id=1, source_target_pairs={{0,16},{2,18},{4,20},{6,22},{8,24},{10,26},{12,28},{14,30},{16,0},... | collective-permute-start | bytes 589832 | tf_op jit(solution)/shard_map/ppermute | solution.py:358
  33.8 1.9 collective-permute-start.5
  39.3 1.9 fusion.58
  42.2 1.8 collective-permute-done.5
  44.0 1.5 collective-permute-start.11
  50.4 1.4 collective-permute-start.13
  57.6 12.9 %attention_forward.1 = (bf16[4,128,128]{2,1,0:T(8,128)(2,1)}, bf16[4,128,128]{2,1,0:T(8,128)(2,1)}, bf16[4,2,256,256]{3,2,1,0:T(8,128)(2,1)}) custom-call(s32[1]{0:T(128)} %bitcast.core_ref, f32[4,128,256]{2,1,0:T(8,128)} %bitcast.195, f32[4,128,256]{2,1,0:T(8,128)} %bitcast.197, f32[4,256,64]{2,1,0:T(8,128)} %pad_maximum_fusion.5.cos_ref, ...), custom_call_target="tpu_custom_call" | custom-call | flops 1000000 | bytes 100000 | tf_op jit(solution)/shard_map/attention_forward/pallas_call | solution.py:181
  72.1 2.6 collective-permute-done.16
  75.2 1.7 collective-permute-start.19
  78.8 6.6 %collective-permute-done.19 = bf16[128,1024]{1,0:T(8,128)(2,1)S(1)} collective-permute-done((bf16[128,1024]{1,0:T(8,128)(2,1)S(1)}, bf16[128,1024]{1,0:T(8,128)(2,1)S(1)}, u32[]{:S(2)}, u32[]{:S(2)}) %collective-permute-start.19) | collective-permute-done | bytes 262176 | tf_op jit(solution)/shard_map/ppermute | solution.py:358
  85.4 4.8 %collective-permute-done.18 = bf16[128,1024]{1,0:T(8,128)(2,1)S(1)} collective-permute-done((bf16[128,1024]{1,0:T(8,128)(2,1)S(1)}, bf16[128,1024]{1,0:T(8,128)(2,1)S(1)}, u32[]{:S(2)}, u32[]{:S(2)}) %collective-permute-start.18) | collective-permute-done | bytes 262176 | tf_op jit(solution)/shard_map/ppermute | solution.py:358
  91.1 1.7 collective-permute-start.22
  94.6 6.6 %collective-permute-done.22 = bf16[128,1024]{1,0:T(8,128)(2,1)S(1)} collective-permute-done((bf16[128,1024]{1,0:T(8,128)(2,1)S(1)}, bf16[128,1024]{1,0:T(8,128)(2,1)S(1)}, u32[]{:S(2)}, u32[]{:S(2)}) %collective-permute-start.22) | collective-permute-done | bytes 262176 | tf_op jit(solution)/shard_map/ppermute | solution.py:358
  101.2 4.8 %collective-permute-done.21 = bf16[128,1024]{1,0:T(8,128)(2,1)S(1)} collective-permute-done((bf16[128,1024]{1,0:T(8,128)(2,1)S(1)}, bf16[128,1024]{1,0:T(8,128)(2,1)S(1)}, u32[]{:S(2)}, u32[]{:S(2)}) %collective-permute-start.21) | collective-permute-done | bytes 262176 | tf_op jit(solution)/shard_map/ppermute | solution.py:358
  106.3 3.5 %all-gather.2.cloned.1.call-done = bf16[4,256,1728]{1,2,0:T(8,128)(2,1)} async-done(((bf16[1,256,1728]{1,2,0:T(8,128)(2,1)}), bf16[4,256,1728]{1,2,0:T(8,128)(2,1)}) %all-gather.2.cloned.1.call-update) | async-done | bytes 3538960 | tf_op jit(solution)/shard_map/all_gather | solution.py:432
  109.8 5.8 %copy.98 = bf16[4,256,1728]{2,1,0:T(8,128)(2,1)} copy(bf16[4,256,1728]{1,2,0:T(8,128)(2,1)} %all-gather.2.cloned.1.call-done) | data formatting | bytes 7077888 | tf_op jit(solution)/shard_map/all_gather | solution.py:432
  115.6 7.3 %ffn_half.2 = (bf16[512,1024]{1,0:T(8,128)(2,1)S(1)}, bf16[512,1024]{1,0:T(8,128)(2,1)S(1)}, bf16[512,576]{1,0:T(8,128)(2,1)S(1)}, bf16[512,1152]{1,0:T(8,128)(2,1)S(1)}) custom-call(bf16[512,1024]{1,0:T(8,128)(2,1)} %collective-permute-done.23.n_ref.n1_ref, bf16[512,1024]{1,0:T(8,128)(2,1)S(1)} %collective-permute-done.24.g_ref.g1_ref, ...), custom_call_target="tpu_custom_call" | custom-call | flops 1000000 | bytes 100000 | tf_op jit(solution)/shard_map/ffn_half/pallas_call | solution.py:278
  124.9 8.0 %ffn_half.3 = (f32[512,1024]{1,0:T(8,128)S(1)}, f32[512,1024]{1,0:T(8,128)}, bf16[512,576]{1,0:T(8,128)(2,1)S(1)}, bf16[512,1152]{1,0:T(8,128)(2,1)S(1)}) custom-call(bf16[512,1024]{1,0:T(8,128)(2,1)S(1)} %pad_maximum_fusion.1.n_ref.n0_ref, bf16[512,1024]{1,0:T(8,128)(2,1)S(1)} %constant_dynamic-update-slice_fusion.g_ref.g0_ref, bf16[1024,1728]{1,0:T(8,128)(2,1)} %bitcast.188), custom_call_target="tpu_custom_call" | custom-call | flops 1000000 | bytes 100000 | tf_op jit(solution)/shard_map/ffn_half/pallas_call | solution.py:278
  133.0 2.2 fusion.69
  135.2 8.1 %ffn_grads.1 = bf16[1024,1728]{1,0:T(8,128)(2,1)} custom-call(bf16[512,1024]{1,0:T(8,128)(2,1)S(1)} %pad_maximum_fusion.1.n_ref.n0_ref, bf16[512,1024]{1,0:T(8,128)(2,1)} %collective-permute-done.23.n_ref.n1_ref, bf16[512,1024]{1,0:T(8,128)(2,1)S(1)} %constant_dynamic-update-slice_fusion.g_ref.g0_ref, ...), custom_call_target="tpu_custom_call" | custom-call | flops 3623878656 | bytes 11272192 | tf_op jit(solution)/shard_map/ffn_grads/pallas_call | solution.py:317
  144.6 2.4 collective-permute-start.29
  148.2 6.6 %collective-permute-done.29 = bf16[128,1024]{1,0:T(8,128)(2,1)S(1)} collective-permute-done((bf16[128,1024]{1,0:T(8,128)(2,1)S(1)}, bf16[128,1024]{1,0:T(8,128)(2,1)S(1)}, u32[]{:S(2)}, u32[]{:S(2)}) %collective-permute-start.29) | collective-permute-done | bytes 262176 | tf_op jit(solution)/shard_map/ppermute | solution.py:358
  154.7 5.2 %collective-permute-done.28 = bf16[128,1024]{1,0:T(8,128)(2,1)S(1)} collective-permute-done((bf16[128,1024]{1,0:T(8,128)(2,1)S(1)}, bf16[128,1024]{1,0:T(8,128)(2,1)S(1)}, u32[]{:S(2)}, u32[]{:S(2)}) %collective-permute-start.28) | collective-permute-done | bytes 262176 | tf_op jit(solution)/shard_map/ppermute | solution.py:358
  161.6 1.8 collective-permute-start.32
  165.1 6.6 %collective-permute-done.32 = bf16[128,1024]{1,0:T(8,128)(2,1)S(1)} collective-permute-done((bf16[128,1024]{1,0:T(8,128)(2,1)S(1)}, bf16[128,1024]{1,0:T(8,128)(2,1)S(1)}, u32[]{:S(2)}, u32[]{:S(2)}) %collective-permute-start.32) | collective-permute-done | bytes 262176 | tf_op jit(solution)/shard_map/ppermute | solution.py:358
  171.8 4.7 %collective-permute-done.31 = bf16[128,1024]{1,0:T(8,128)(2,1)S(1)} collective-permute-done((bf16[128,1024]{1,0:T(8,128)(2,1)S(1)}, bf16[128,1024]{1,0:T(8,128)(2,1)S(1)}, u32[]{:S(2)}, u32[]{:S(2)}) %collective-permute-start.31) | collective-permute-done | bytes 262176 | tf_op jit(solution)/shard_map/ppermute | solution.py:358
  178.6 1.7 convert_add_fusion.2
  181.8 1.8 collective-permute-start.34
  185.7 5.0 %collective-permute-done.35 = bf16[128,1024]{1,0:T(8,128)(2,1)S(1)} collective-permute-done((bf16[128,1024]{1,0:T(8,128)(2,1)S(1)}, bf16[128,1024]{1,0:T(8,128)(2,1)S(1)}, u32[]{:S(2)}, u32[]{:S(2)}) %collective-permute-start.35) | collective-permute-done | bytes 262176 | tf_op jit(solution)/shard_map/ppermute | solution.py:358
  190.7 5.0 %collective-permute-done.34 = bf16[128,1024]{1,0:T(8,128)(2,1)S(1)} collective-permute-done((bf16[128,1024]{1,0:T(8,128)(2,1)S(1)}, bf16[128,1024]{1,0:T(8,128)(2,1)S(1)}, u32[]{:S(2)}, u32[]{:S(2)}) %collective-permute-start.34) | collective-permute-done | bytes 262176 | tf_op jit(solution)/shard_map/ppermute | solution.py:358
  198.7 13.0 %attention_backward.1 = (bf16[4,128,256]{2,1,0:T(8,128)(2,1)}, bf16[4,128,256]{2,1,0:T(8,128)(2,1)}, f32[4,1,128]{2,1,0:T(1,128)}) custom-call(s32[1]{0:T(128)} %bitcast.core_ref, f32[4,128,256]{2,1,0:T(8,128)} %bitcast.196, f32[4,128,256]{2,1,0:T(8,128)} %bitcast.198, bf16[4,128,128]{2,1,0:T(8,128)(2,1)} %bitcast.216, bf16[4,128,128]{2,1,0:T(8,128)(2,1)} %bitcast.217, ...), custom_call_target="tpu_custom_call" | custom-call | flops 1000000 | bytes 100000 | tf_op jit(solution)/shard_map/attention_backward/pallas_call | solution.py:218
  211.7 2.5 convolution_convert_fusion.1
  215.9 2.0 fusion.35
  219.6 1.9 fusion.3
  222.4 1.4 collective-permute-start.46
  223.8 1.6 collective-permute-start.45
  225.4 2.0 pad_maximum_fusion.7
  229.7 1.4 collective-permute-start.39
  231.8 5.7 %collective-permute-done.42 = bf16[268,384]{1,0:T(8,128)(2,1)S(1)} collective-permute-done((bf16[268,384]{1,0:T(8,128)(2,1)}, bf16[268,384]{1,0:T(8,128)(2,1)S(1)}, u32[]{:S(2)}, u32[]{:S(2)}) %collective-permute-start.42) | collective-permute-done | bytes 205856 | tf_op jit(solution)/shard_map/ppermute | solution.py:358
  237.5 2.5 collective-permute-start.41
  240.0 9.2 %collective-permute-done.41 = bf16[268,384]{1,0:T(8,128)(2,1)S(1)} collective-permute-done((bf16[268,384]{1,0:T(8,128)(2,1)}, bf16[268,384]{1,0:T(8,128)(2,1)S(1)}, u32[]{:S(2)}, u32[]{:S(2)}) %collective-permute-start.41) | collective-permute-done | bytes 205856 | tf_op jit(solution)/shard_map/ppermute | solution.py:358
  249.9 1.4 collective-permute-start.44
  252.8 2.9 %collective-permute-done.43 = bf16[64,1728]{1,0:T(8,128)(2,1)S(1)} collective-permute-done((bf16[64,1728]{1,0:T(8,128)(2,1)S(1)}, bf16[64,1728]{1,0:T(8,128)(2,1)S(1)}, u32[]{:S(2)}, u32[]{:S(2)}) %collective-permute-start.43) | collective-permute-done | bytes 221216 | tf_op jit(solution)/shard_map/ppermute | solution.py:358
  255.7 1.6 collective-permute-start.49
  264.2 2.1 fusion.14
  (285 shorter events, 82.0 us)
Async XLA Ops:
  7.2 102.6 %all-gather.2.cloned.1.call-start = ((), (), s32[]{:S(2)}) async-start(), calls=%async_computation.1 | async-start | bytes 4423680 | tf_op jit(solution)/shard_map/all_gather | solution.py:432
  12.2 11.4 %collective-permute-start.7 = (bf16[66,384]{1,0:T(8,128)(2,1)}, bf16[66,384]{1,0:T(8,128)(2,1)}, u32[]{:S(2)}, u32[]{:S(2)}) collective-permute-start(bf16[66,384]{1,0:T(8,128)(2,1)} %get-tuple-element.152), channel_id=1, source_target_pairs={{0,4},{2,6},{4,0},{6,2},{8,12},{10,14},{12,8},{14,10},{16,20},{18,... | collective-permute-start | bytes 152072 | tf_op jit(solution)/shard_map/ppermute | solution.py:358
  15.2 8.6 %collective-permute-start.6 = (bf16[66,384]{1,0:T(8,128)(2,1)}, bf16[66,384]{1,0:T(8,128)(2,1)}, u32[]{:S(2)}, u32[]{:S(2)}) collective-permute-start(bf16[66,384]{1,0:T(8,128)(2,1)} %get-tuple-element.153), channel_id=1, source_target_pairs={{0,6},{2,4},{4,2},{6,0},{8,14},{10,12},{12,10},{14,8},{16,22},{18,... | collective-permute-start | bytes 152072 | tf_op jit(solution)/shard_map/ppermute | solution.py:358
  16.6 7.2 %collective-permute-start.8 = (bf16[66,384]{1,0:T(8,128)(2,1)S(1)}, bf16[66,384]{1,0:T(8,128)(2,1)}, u32[]{:S(2)}, u32[]{:S(2)}) collective-permute-start(bf16[66,384]{1,0:T(8,128)(2,1)S(1)} %get-tuple-element.151), channel_id=1, source_target_pairs={{0,2},{2,0},{4,6},{6,4},{8,10},{10,8},{12,14},{14,12},{16,18},{18,... | collective-permute-start | bytes 152072 | tf_op jit(solution)/shard_map/ppermute | solution.py:358
  19.5 12.4 %collective-permute-start = (bf16[64,1728]{1,0:T(8,128)(2,1)S(1)}, bf16[64,1728]{1,0:T(8,128)(2,1)S(1)}, u32[]{:S(2)}, u32[]{:S(2)}) collective-permute-start(bf16[64,1728]{1,0:T(8,128)(2,1)S(1)} %get-tuple-element.131), channel_id=1, source_target_pairs={{0,6},{2,4},{4,2},{6,0},{8,14},{10,12},{12,10},{14,8},{16,22},{18,... | collective-permute-start | bytes 663560 | tf_op jit(solution)/shard_map/ppermute | solution.py:358
  22.5 9.7 %collective-permute-start.1 = (bf16[64,1728]{1,0:T(8,128)(2,1)S(1)}, bf16[64,1728]{1,0:T(8,128)(2,1)S(1)}, u32[]{:S(2)}, u32[]{:S(2)}) collective-permute-start(bf16[64,1728]{1,0:T(8,128)(2,1)S(1)} %get-tuple-element.130), channel_id=1, source_target_pairs={{0,4},{2,6},{4,0},{6,2},{8,12},{10,14},{12,8},{14,10},{16,20},{18,... | collective-permute-start | bytes 663560 | tf_op jit(solution)/shard_map/ppermute | solution.py:358
  23.6 9.0 %collective-permute-start.2 = (bf16[64,1728]{1,0:T(8,128)(2,1)S(1)}, bf16[64,1728]{1,0:T(8,128)(2,1)}, u32[]{:S(2)}, u32[]{:S(2)}) collective-permute-start(bf16[64,1728]{1,0:T(8,128)(2,1)S(1)} %get-tuple-element.129), channel_id=1, source_target_pairs={{0,2},{2,0},{4,6},{6,4},{8,10},{10,8},{12,14},{14,12},{16,18},{18,... | collective-permute-start | bytes 663560 | tf_op jit(solution)/shard_map/ppermute | solution.py:358
  25.4 23.4 %collective-permute-start.10 = (bf16[256,384]{1,0:T(8,128)(2,1)}, bf16[256,384]{1,0:T(8,128)(2,1)S(1)}, u32[]{:S(2)}, u32[]{:S(2)}) collective-permute-start(bf16[256,384]{1,0:T(8,128)(2,1)} %pad_maximum_fusion.14), channel_id=1, source_target_pairs={{0,16},{2,18},{4,20},{6,22},{8,24},{10,26},{12,28},{14,30},{16,0},... | collective-permute-start | bytes 589832 | tf_op jit(solution)/shard_map/ppermute | solution.py:358
  28.4 20.5 %collective-permute-start.9 = (bf16[256,384]{1,0:T(8,128)(2,1)}, bf16[256,384]{1,0:T(8,128)(2,1)S(1)}, u32[]{:S(2)}, u32[]{:S(2)}) collective-permute-start(bf16[256,384]{1,0:T(8,128)(2,1)} %pad_maximum_fusion.14), channel_id=1, source_target_pairs={{0,24},{2,26},{4,28},{6,30},{8,16},{10,18},{12,20},{14,22},{16,8},... | collective-permute-start | bytes 589832 | tf_op jit(solution)/shard_map/ppermute | solution.py:358
  33.8 10.2 %collective-permute-start.5 = (bf16[128,1024]{1,0:T(8,128)(2,1)S(1)}, bf16[128,1024]{1,0:T(8,128)(2,1)S(1)}, u32[]{:S(2)}, u32[]{:S(2)}) collective-permute-start(bf16[128,1024]{1,0:T(8,128)(2,1)S(1)} %copy-done.12), channel_id=1, source_target_pairs={{0,6},{2,4},{4,2},{6,0},{8,14},{10,12},{12,10},{14,8},{16,22},{18,... | collective-permute-start | bytes 786440 | tf_op jit(solution)/shard_map/ppermute | solution.py:358
  35.6 12.5 %collective-permute-start.4 = (bf16[128,1024]{1,0:T(8,128)(2,1)S(1)}, bf16[128,1024]{1,0:T(8,128)(2,1)S(1)}, u32[]{:S(2)}, u32[]{:S(2)}) collective-permute-start(bf16[128,1024]{1,0:T(8,128)(2,1)S(1)} %copy-done.12), channel_id=1, source_target_pairs={{0,4},{2,6},{4,0},{6,2},{8,12},{10,14},{12,8},{14,10},{16,20},{18,... | collective-permute-start | bytes 786440 | tf_op jit(solution)/shard_map/ppermute | solution.py:358
  36.8 11.7 %collective-permute-start.3 = (bf16[128,1024]{1,0:T(8,128)(2,1)S(1)}, bf16[128,1024]{1,0:T(8,128)(2,1)S(1)}, u32[]{:S(2)}, u32[]{:S(2)}) collective-permute-start(bf16[128,1024]{1,0:T(8,128)(2,1)S(1)} %copy-done.12), channel_id=1, source_target_pairs={{0,2},{2,0},{4,6},{6,4},{8,10},{10,8},{12,14},{14,12},{16,18},{18,... | collective-permute-start | bytes 786440 | tf_op jit(solution)/shard_map/ppermute | solution.py:358
  39.3 188.1 %reduce-scatter.2.cloned.1.call-start = ((), (), s32[]{:S(2)}) async-start(), calls=%async_computation.2 | async-start | bytes 4587520 | tf_op jit(solution)/shard_map/reduce_scatter | solution.py:488
  48.8 6.5 %collective-permute-start.12 = (bf16[512,1024]{1,0:T(8,128)(2,1)S(1)}, bf16[512,1024]{1,0:T(8,128)(2,1)S(1)}, u32[]{:S(2)}, u32[]{:S(2)}) collective-permute-start(bf16[512,1024]{1,0:T(8,128)(2,1)S(1)} %get-tuple-element.100), channel_id=1, source_target_pairs={{0,1},{1,0},{2,3},{3,2},{4,5},{5,4},{6,7},{7,6},{8,9},{9,8},{10,11... | collective-permute-start | bytes 3145736 | tf_op jit(solution)/shard_map/ppermute | solution.py:361
  50.4 20.1 %collective-permute-start.13 = (bf16[128,1024]{1,0:T(8,128)(2,1)S(1)}, bf16[128,1024]{1,0:T(8,128)(2,1)S(1)}, u32[]{:S(2)}, u32[]{:S(2)}) collective-permute-start(bf16[128,1024]{1,0:T(8,128)(2,1)S(1)} %copy-done.20), channel_id=1, source_target_pairs={{0,2},{2,0},{4,6},{6,4},{8,10},{10,8},{12,14},{14,12},{16,18},{18,... | collective-permute-start | bytes 786440 | tf_op jit(solution)/shard_map/ppermute | solution.py:358
  51.8 18.7 %collective-permute-start.14 = (bf16[128,1024]{1,0:T(8,128)(2,1)S(1)}, bf16[128,1024]{1,0:T(8,128)(2,1)S(1)}, u32[]{:S(2)}, u32[]{:S(2)}) collective-permute-start(bf16[128,1024]{1,0:T(8,128)(2,1)S(1)} %copy-done.20), channel_id=1, source_target_pairs={{0,4},{2,6},{4,0},{6,2},{8,12},{10,14},{12,8},{14,10},{16,20},{18,... | collective-permute-start | bytes 786440 | tf_op jit(solution)/shard_map/ppermute | solution.py:358
  52.7 17.8 %collective-permute-start.15 = (bf16[128,1024]{1,0:T(8,128)(2,1)S(1)}, bf16[128,1024]{1,0:T(8,128)(2,1)S(1)}, u32[]{:S(2)}, u32[]{:S(2)}) collective-permute-start(bf16[128,1024]{1,0:T(8,128)(2,1)S(1)} %copy-done.20), channel_id=1, source_target_pairs={{0,6},{2,4},{4,2},{6,0},{8,14},{10,12},{12,10},{14,8},{16,22},{18,... | collective-permute-start | bytes 786440 | tf_op jit(solution)/shard_map/ppermute | solution.py:358
  75.2 10.2 %collective-permute-start.19 = (bf16[128,1024]{1,0:T(8,128)(2,1)S(1)}, bf16[128,1024]{1,0:T(8,128)(2,1)S(1)}, u32[]{:S(2)}, u32[]{:S(2)}) collective-permute-start(bf16[128,1024]{1,0:T(8,128)(2,1)S(1)} %get-tuple-element.124), channel_id=1, source_target_pairs={{0,6},{2,4},{4,2},{6,0},{8,14},{10,12},{12,10},{14,8},{16,22},{18,... | collective-permute-start | bytes 786440 | tf_op jit(solution)/shard_map/ppermute | solution.py:358
  77.0 13.2 %collective-permute-start.18 = (bf16[128,1024]{1,0:T(8,128)(2,1)S(1)}, bf16[128,1024]{1,0:T(8,128)(2,1)S(1)}, u32[]{:S(2)}, u32[]{:S(2)}) collective-permute-start(bf16[128,1024]{1,0:T(8,128)(2,1)S(1)} %get-tuple-element.125), channel_id=1, source_target_pairs={{0,4},{2,6},{4,0},{6,2},{8,12},{10,14},{12,8},{14,10},{16,20},{18,... | collective-permute-start | bytes 786440 | tf_op jit(solution)/shard_map/ppermute | solution.py:358
  78.1 12.1 %collective-permute-start.17 = (bf16[128,1024]{1,0:T(8,128)(2,1)S(1)}, bf16[128,1024]{1,0:T(8,128)(2,1)S(1)}, u32[]{:S(2)}, u32[]{:S(2)}) collective-permute-start(bf16[128,1024]{1,0:T(8,128)(2,1)S(1)} %get-tuple-element.123), channel_id=1, source_target_pairs={{0,2},{2,0},{4,6},{6,4},{8,10},{10,8},{12,14},{14,12},{16,18},{18,... | collective-permute-start | bytes 786440 | tf_op jit(solution)/shard_map/ppermute | solution.py:358
  91.1 10.2 %collective-permute-start.22 = (bf16[128,1024]{1,0:T(8,128)(2,1)S(1)}, bf16[128,1024]{1,0:T(8,128)(2,1)S(1)}, u32[]{:S(2)}, u32[]{:S(2)}) collective-permute-start(bf16[128,1024]{1,0:T(8,128)(2,1)S(1)} %multiply_convert_fusion), channel_id=1, source_target_pairs={{0,6},{2,4},{4,2},{6,0},{8,14},{10,12},{12,10},{14,8},{16,22},{18,... | collective-permute-start | bytes 786440 | tf_op jit(solution)/shard_map/ppermute | solution.py:358
  92.8 13.2 %collective-permute-start.21 = (bf16[128,1024]{1,0:T(8,128)(2,1)S(1)}, bf16[128,1024]{1,0:T(8,128)(2,1)S(1)}, u32[]{:S(2)}, u32[]{:S(2)}) collective-permute-start(bf16[128,1024]{1,0:T(8,128)(2,1)S(1)} %multiply_convert_fusion), channel_id=1, source_target_pairs={{0,4},{2,6},{4,0},{6,2},{8,12},{10,14},{12,8},{14,10},{16,20},{18,... | collective-permute-start | bytes 786440 | tf_op jit(solution)/shard_map/ppermute | solution.py:358
  93.9 12.1 %collective-permute-start.20 = (bf16[128,1024]{1,0:T(8,128)(2,1)S(1)}, bf16[128,1024]{1,0:T(8,128)(2,1)S(1)}, u32[]{:S(2)}, u32[]{:S(2)}) collective-permute-start(bf16[128,1024]{1,0:T(8,128)(2,1)S(1)} %multiply_convert_fusion), channel_id=1, source_target_pairs={{0,2},{2,0},{4,6},{6,4},{8,10},{10,8},{12,14},{14,12},{16,18},{18,... | collective-permute-start | bytes 786440 | tf_op jit(solution)/shard_map/ppermute | solution.py:358
  94.6 21.0 %collective-permute-start.24 = (bf16[512,1024]{1,0:T(8,128)(2,1)S(1)}, bf16[512,1024]{1,0:T(8,128)(2,1)S(1)}, u32[]{:S(2)}, u32[]{:S(2)}) collective-permute-start(bf16[512,1024]{1,0:T(8,128)(2,1)S(1)} %constant_dynamic-update-slice_fusion.g_ref.g0_ref), channel_id=1, source_target_pairs={{0,1},{1,0},{2,3},{3,2},{4,5},{5,4},{6,7},{7,6},{8,9},{9,8},{10,11... | collective-permute-start | bytes 3145736 | tf_op jit(solution)/shard_map/ppermute | solution.py:361
  106.1 9.6 %collective-permute-start.23 = (bf16[512,1024]{1,0:T(8,128)(2,1)S(1)}, bf16[512,1024]{1,0:T(8,128)(2,1)}, u32[]{:S(2)}, u32[]{:S(2)}) collective-permute-start(bf16[512,1024]{1,0:T(8,128)(2,1)S(1)} %pad_maximum_fusion.1.n_ref.n0_ref), channel_id=1, source_target_pairs={{0,1},{1,0},{2,3},{3,2},{4,5},{5,4},{6,7},{7,6},{8,9},{9,8},{10,11... | collective-permute-start | bytes 3145736 | tf_op jit(solution)/shard_map/ppermute | solution.py:361
  124.9 8.1 %collective-permute-start.26 = (bf16[512,1024]{1,0:T(8,128)(2,1)S(1)}, bf16[512,1024]{1,0:T(8,128)(2,1)S(1)}, u32[]{:S(2)}, u32[]{:S(2)}) collective-permute-start(bf16[512,1024]{1,0:T(8,128)(2,1)S(1)} %get-tuple-element.60), channel_id=1, source_target_pairs={{0,1},{1,0},{2,3},{3,2},{4,5},{5,4},{6,7},{7,6},{8,9},{9,8},{10,11... | collective-permute-start | bytes 3145736 | tf_op jit(solution)/shard_map/ppermute | solution.py:361
  144.6 10.1 %collective-permute-start.29 = (bf16[128,1024]{1,0:T(8,128)(2,1)S(1)}, bf16[128,1024]{1,0:T(8,128)(2,1)S(1)}, u32[]{:S(2)}, u32[]{:S(2)}) collective-permute-start(bf16[128,1024]{1,0:T(8,128)(2,1)S(1)} %get-tuple-element.121), channel_id=1, source_target_pairs={{0,6},{2,4},{4,2},{6,0},{8,14},{10,12},{12,10},{14,8},{16,22},{18,... | collective-permute-start | bytes 786440 | tf_op jit(solution)/shard_map/ppermute | solution.py:358
  147.1 12.9 %collective-permute-start.28 = (bf16[128,1024]{1,0:T(8,128)(2,1)S(1)}, bf16[128,1024]{1,0:T(8,128)(2,1)S(1)}, u32[]{:S(2)}, u32[]{:S(2)}) collective-permute-start(bf16[128,1024]{1,0:T(8,128)(2,1)S(1)} %get-tuple-element.122), channel_id=1, source_target_pairs={{0,4},{2,6},{4,0},{6,2},{8,12},{10,14},{12,8},{14,10},{16,20},{18,... | collective-permute-start | bytes 786440 | tf_op jit(solution)/shard_map/ppermute | solution.py:358
  147.6 12.4 %collective-permute-start.27 = (bf16[128,1024]{1,0:T(8,128)(2,1)S(1)}, bf16[128,1024]{1,0:T(8,128)(2,1)S(1)}, u32[]{:S(2)}, u32[]{:S(2)}) collective-permute-start(bf16[128,1024]{1,0:T(8,128)(2,1)S(1)} %get-tuple-element.120), channel_id=1, source_target_pairs={{0,2},{2,0},{4,6},{6,4},{8,10},{10,8},{12,14},{14,12},{16,18},{18,... | collective-permute-start | bytes 786440 | tf_op jit(solution)/shard_map/ppermute | solution.py:358
  148.2 30.4 %collective-permute-start.25 = (bf16[512,1024]{1,0:T(8,128)(2,1)S(1)}, bf16[512,1024]{1,0:T(8,128)(2,1)}, u32[]{:S(2)}, u32[]{:S(2)}) collective-permute-start(bf16[512,1024]{1,0:T(8,128)(2,1)S(1)} %copy-done.5), channel_id=1, source_target_pairs={{0,1},{1,0},{2,3},{3,2},{4,5},{5,4},{6,7},{7,6},{8,9},{9,8},{10,11... | collective-permute-start | bytes 3145736 | tf_op jit(solution)/shard_map/ppermute | solution.py:361
  161.6 10.2 %collective-permute-start.32 = (bf16[128,1024]{1,0:T(8,128)(2,1)S(1)}, bf16[128,1024]{1,0:T(8,128)(2,1)S(1)}, u32[]{:S(2)}, u32[]{:S(2)}) collective-permute-start(bf16[128,1024]{1,0:T(8,128)(2,1)S(1)} %convert_element_type.215), channel_id=1, source_target_pairs={{0,6},{2,4},{4,2},{6,0},{8,14},{10,12},{12,10},{14,8},{16,22},{18,... | collective-permute-start | bytes 786440 | tf_op jit(solution)/shard_map/ppermute | solution.py:358
  163.3 13.1 %collective-permute-start.31 = (bf16[128,1024]{1,0:T(8,128)(2,1)S(1)}, bf16[128,1024]{1,0:T(8,128)(2,1)S(1)}, u32[]{:S(2)}, u32[]{:S(2)}) collective-permute-start(bf16[128,1024]{1,0:T(8,128)(2,1)S(1)} %convert_element_type.215), channel_id=1, source_target_pairs={{0,4},{2,6},{4,0},{6,2},{8,12},{10,14},{12,8},{14,10},{16,20},{18,... | collective-permute-start | bytes 786440 | tf_op jit(solution)/shard_map/ppermute | solution.py:358
  164.6 12.6 %collective-permute-start.30 = (bf16[128,1024]{1,0:T(8,128)(2,1)S(1)}, bf16[128,1024]{1,0:T(8,128)(2,1)}, u32[]{:S(2)}, u32[]{:S(2)}) collective-permute-start(bf16[128,1024]{1,0:T(8,128)(2,1)S(1)} %convert_element_type.215), channel_id=1, source_target_pairs={{0,2},{2,0},{4,6},{6,4},{8,10},{10,8},{12,14},{14,12},{16,18},{18,... | collective-permute-start | bytes 786440 | tf_op jit(solution)/shard_map/ppermute | solution.py:358
  178.4 18.3 %collective-permute-start.36 = (bf16[512,1024]{1,0:T(8,128)(2,1)S(1)}, bf16[512,1024]{1,0:T(8,128)(2,1)S(1)}, u32[]{:S(2)}, u32[]{:S(2)}) collective-permute-start(bf16[512,1024]{1,0:T(8,128)(2,1)S(1)} %pad_maximum_fusion.2), channel_id=1, source_target_pairs={{0,1},{1,0},{2,3},{3,2},{4,5},{5,4},{6,7},{7,6},{8,9},{9,8},{10,11... | collective-permute-start | bytes 3145736 | tf_op jit(solution)/shard_map/ppermute | solution.py:361
  180.5 10.1 %collective-permute-start.35 = (bf16[128,1024]{1,0:T(8,128)(2,1)S(1)}, bf16[128,1024]{1,0:T(8,128)(2,1)S(1)}, u32[]{:S(2)}, u32[]{:S(2)}) collective-permute-start(bf16[128,1024]{1,0:T(8,128)(2,1)S(1)} %get-tuple-element.118), channel_id=1, source_target_pairs={{0,6},{2,4},{4,2},{6,0},{8,14},{10,12},{12,10},{14,8},{16,22},{18,... | collective-permute-start | bytes 786440 | tf_op jit(solution)/shard_map/ppermute | solution.py:358
  181.8 13.9 %collective-permute-start.34 = (bf16[128,1024]{1,0:T(8,128)(2,1)S(1)}, bf16[128,1024]{1,0:T(8,128)(2,1)S(1)}, u32[]{:S(2)}, u32[]{:S(2)}) collective-permute-start(bf16[128,1024]{1,0:T(8,128)(2,1)S(1)} %get-tuple-element.119), channel_id=1, source_target_pairs={{0,4},{2,6},{4,0},{6,2},{8,12},{10,14},{12,8},{14,10},{16,20},{18,... | collective-permute-start | bytes 786440 | tf_op jit(solution)/shard_map/ppermute | solution.py:358
  183.5 12.2 %collective-permute-start.33 = (bf16[128,1024]{1,0:T(8,128)(2,1)S(1)}, bf16[128,1024]{1,0:T(8,128)(2,1)S(1)}, u32[]{:S(2)}, u32[]{:S(2)}) collective-permute-start(bf16[128,1024]{1,0:T(8,128)(2,1)S(1)} %get-tuple-element.117), channel_id=1, source_target_pairs={{0,2},{2,0},{4,6},{6,4},{8,10},{10,8},{12,14},{14,12},{16,18},{18,... | collective-permute-start | bytes 786440 | tf_op jit(solution)/shard_map/ppermute | solution.py:358
  222.4 38.6 %collective-permute-start.46 = (bf16[128,1024]{1,0:T(8,128)(2,1)}, bf16[128,1024]{1,0:T(8,128)(2,1)}, u32[]{:S(2)}, u32[]{:S(2)}) collective-permute-start(bf16[128,1024]{1,0:T(8,128)(2,1)} %get-tuple-element.115), channel_id=1, source_target_pairs={{0,6},{2,4},{4,2},{6,0},{8,14},{10,12},{12,10},{14,8},{16,22},{18,... | collective-permute-start | bytes 786440 | tf_op jit(solution)/shard_map/ppermute | solution.py:358
  223.8 38.0 %collective-permute-start.45 = (bf16[128,1024]{1,0:T(8,128)(2,1)}, bf16[128,1024]{1,0:T(8,128)(2,1)}, u32[]{:S(2)}, u32[]{:S(2)}) collective-permute-start(bf16[128,1024]{1,0:T(8,128)(2,1)} %get-tuple-element.116), channel_id=1, source_target_pairs={{0,4},{2,6},{4,0},{6,2},{8,12},{10,14},{12,8},{14,10},{16,20},{18,... | collective-permute-start | bytes 786440 | tf_op jit(solution)/shard_map/ppermute | solution.py:358
  227.4 10.1 %collective-permute-start.42 = (bf16[268,384]{1,0:T(8,128)(2,1)}, bf16[268,384]{1,0:T(8,128)(2,1)S(1)}, u32[]{:S(2)}, u32[]{:S(2)}) collective-permute-start(bf16[268,384]{1,0:T(8,128)(2,1)} %get-tuple-element.80), channel_id=1, source_target_pairs={{0,24},{2,26},{4,28},{6,30},{8,16},{10,18},{12,20},{14,22},{16,8},... | collective-permute-start | bytes 617480 | tf_op jit(solution)/shard_map/ppermute | solution.py:358
  229.7 22.5 %collective-permute-start.39 = (bf16[64,1728]{1,0:T(8,128)(2,1)S(1)}, bf16[64,1728]{1,0:T(8,128)(2,1)S(1)}, u32[]{:S(2)}, u32[]{:S(2)}) collective-permute-start(bf16[64,1728]{1,0:T(8,128)(2,1)S(1)} %get-tuple-element.128), channel_id=1, source_target_pairs={{0,6},{2,4},{4,2},{6,0},{8,14},{10,12},{12,10},{14,8},{16,22},{18,... | collective-permute-start | bytes 663560 | tf_op jit(solution)/shard_map/ppermute | solution.py:358
  231.1 18.7 %collective-permute-start.40 = (bf16[268,384]{1,0:T(8,128)(2,1)}, bf16[268,384]{1,0:T(8,128)(2,1)S(1)}, u32[]{:S(2)}, u32[]{:S(2)}) collective-permute-start(bf16[268,384]{1,0:T(8,128)(2,1)} %get-tuple-element.78), channel_id=1, source_target_pairs={{0,8},{2,10},{4,12},{6,14},{8,0},{10,2},{12,4},{14,6},{16,24},{18,... | collective-permute-start | bytes 617480 | tf_op jit(solution)/shard_map/ppermute | solution.py:358
  237.5 11.7 %collective-permute-start.41 = (bf16[268,384]{1,0:T(8,128)(2,1)}, bf16[268,384]{1,0:T(8,128)(2,1)S(1)}, u32[]{:S(2)}, u32[]{:S(2)}) collective-permute-start(bf16[268,384]{1,0:T(8,128)(2,1)} %get-tuple-element.79), channel_id=1, source_target_pairs={{0,16},{2,18},{4,20},{6,22},{8,24},{10,26},{12,28},{14,30},{16,0},... | collective-permute-start | bytes 617480 | tf_op jit(solution)/shard_map/ppermute | solution.py:358
  249.9 8.5 %collective-permute-start.44 = (bf16[64,1728]{1,0:T(8,128)(2,1)S(1)}, bf16[64,1728]{1,0:T(8,128)(2,1)S(1)}, u32[]{:S(2)}, u32[]{:S(2)}) collective-permute-start(bf16[64,1728]{1,0:T(8,128)(2,1)S(1)} %get-tuple-element.126), channel_id=1, source_target_pairs={{0,2},{2,0},{4,6},{6,4},{8,10},{10,8},{12,14},{14,12},{16,18},{18,... | collective-permute-start | bytes 663560 | tf_op jit(solution)/shard_map/ppermute | solution.py:358
  252.2 10.6 %collective-permute-start.38 = (bf16[128,1024]{1,0:T(8,128)(2,1)S(1)}, bf16[128,1024]{1,0:T(8,128)(2,1)S(1)}, u32[]{:S(2)}, u32[]{:S(2)}) collective-permute-start(bf16[128,1024]{1,0:T(8,128)(2,1)S(1)} %copy-done.31), channel_id=1, source_target_pairs={{0,2},{2,0},{4,6},{6,4},{8,10},{10,8},{12,14},{14,12},{16,18},{18,... | collective-permute-start | bytes 786440 | tf_op jit(solution)/shard_map/ppermute | solution.py:358
  255.7 15.8 %collective-permute-start.49 = (bf16[76,384]{1,0:T(8,128)(2,1)}, bf16[76,384]{1,0:T(8,128)(2,1)S(1)}, u32[]{:S(2)}, u32[]{:S(2)}) collective-permute-start(bf16[76,384]{1,0:T(8,128)(2,1)} %get-tuple-element.166), channel_id=1, source_target_pairs={{0,6},{2,4},{4,2},{6,0},{8,14},{10,12},{12,10},{14,8},{16,22},{18,... | collective-permute-start | bytes 175112 | tf_op jit(solution)/shard_map/ppermute | solution.py:358
  258.4 13.1 %collective-permute-start.48 = (bf16[76,384]{1,0:T(8,128)(2,1)}, bf16[76,384]{1,0:T(8,128)(2,1)S(1)}, u32[]{:S(2)}, u32[]{:S(2)}) collective-permute-start(bf16[76,384]{1,0:T(8,128)(2,1)} %get-tuple-element.165), channel_id=1, source_target_pairs={{0,4},{2,6},{4,0},{6,2},{8,12},{10,14},{12,8},{14,10},{16,20},{18,... | collective-permute-start | bytes 175112 | tf_op jit(solution)/shard_map/ppermute | solution.py:358
  261.0 10.6 %collective-permute-start.47 = (bf16[76,384]{1,0:T(8,128)(2,1)}, bf16[76,384]{1,0:T(8,128)(2,1)}, u32[]{:S(2)}, u32[]{:S(2)}) collective-permute-start(bf16[76,384]{1,0:T(8,128)(2,1)} %get-tuple-element.164), channel_id=1, source_target_pairs={{0,2},{2,0},{4,6},{6,4},{8,10},{10,8},{12,14},{14,12},{16,18},{18,... | collective-permute-start | bytes 175112 | tf_op jit(solution)/shard_map/ppermute | solution.py:358
  (51 other events, 403.9 us)
Sparse Core Ops, SparseCore 0:
  39.4 70.3 all-gather.1
  143.5 67.1 reduce-scatter.1

commit v2 on v1

--- a/solution.py
+++ b/solution.py
@@ -8,6 +8,7 @@
 
 HD = 64
 PLANE = 4
+STEP = 2
 
 epsilon = 1e-05
 rope_base = 1000000.0
@@ -71,34 +72,39 @@
     half = length // 2
     own_rows = pl.ds(pl.multiple_of(core_ref[0] * half, half), half)
     other_rows = pl.ds(pl.multiple_of((1 - core_ref[0]) * half, half), half)
-    qkv_ref[own_rows, :] = own_ref[0]
-    qkv_ref[other_rows, :] = other_ref[0]
-    qkv = qkv_ref[...]
-    cosine, sine = cos_ref[0], sin_ref[0]
-    row = lax.broadcasted_iota(jnp.int32, (length, length), 0)
-    col = lax.broadcasted_iota(jnp.int32, (length, length), 1)
-    allowed = (col <= row) & (seg_col_ref[0] == seg_row_ref[0])
-
-    def rotated(lo, gain):
-        raw = qkv[:, lo : lo + HD]
-        normed = raw * inverse_rms(raw) * gain
-        return (normed * cosine + swap_halves(normed) * sine).astype(bf16)
-
-    key = rotated(2 * HD, gain_ref[1:2, :])
-    value = qkv[:, 3 * HD : 4 * HD].astype(bf16)
-    outs = []
-    for head in range(2):
-        query = rotated(head * HD, gain_ref[0:1, :])
-        scores = jnp.where(allowed, dot_nt(query, key) * HD**-0.5, masked_score)
-        row_max = jnp.max(scores, axis=-1, keepdims=True)
-        raised = jnp.exp(scores - row_max)
-        total = jnp.sum(raised, axis=-1, keepdims=True)
-        weights = (raised * (1.0 / total)).astype(bf16)
-        p_ref[0, head] = weights
-        outs.append(dot_nn(weights, value))
-    o_ref[...] = jnp.concatenate(outs, axis=-1)
-    o_own_ref[0] = o_ref[own_rows, :].astype(bf16)
-    o_other_ref[0] = o_ref[other_rows, :].astype(bf16)
+
+    def forward_one(seq):
+        qkv_ref[seq, own_rows, :] = own_ref[seq]
+        qkv_ref[seq, other_rows, :] = other_ref[seq]
+        qkv = qkv_ref[seq]
+        cosine, sine = cos_ref[seq], sin_ref[seq]
+        row = lax.broadcasted_iota(jnp.int32, (length, length), 0)
+        col = lax.broadcasted_iota(jnp.int32, (length, length), 1)
+        allowed = (col <= row) & (seg_col_ref[seq] == seg_row_ref[seq])
+
+        def rotated(lo, gain):
+            raw = qkv[:, lo : lo + HD]
+            normed = raw * inverse_rms(raw) * gain
+            return (normed * cosine + swap_halves(normed) * sine).astype(bf16)
+
+        key = rotated(2 * HD, gain_ref[1:2, :])
+        value = qkv[:, 3 * HD : 4 * HD].astype(bf16)
+        outs = []
+        for head in range(2):
+            query = rotated(head * HD, gain_ref[0:1, :])
+            scores = jnp.where(allowed, dot_nt(query, key) * HD**-0.5, masked_score)
+            row_max = jnp.max(scores, axis=-1, keepdims=True)
+            raised = jnp.exp(scores - row_max)
+            total = jnp.sum(raised, axis=-1, keepdims=True)
+            weights = (raised * (1.0 / total)).astype(bf16)
+            p_ref[seq, head] = weights
+            outs.append(dot_nn(weights, value))
+        o_ref[seq] = jnp.concatenate(outs, axis=-1)
+        o_own_ref[seq] = o_ref[seq, own_rows, :].astype(bf16)
+        o_other_ref[seq] = o_ref[seq, other_rows, :].astype(bf16)
+
+    for seq in range(cos_ref.shape[0]):
+        forward_one(seq)
 
 
 def attention_backward_kernel(
@@ -121,58 +127,63 @@
     half = length // 2
     own_rows = pl.ds(pl.multiple_of(core_ref[0] * half, half), half)
     other_rows = pl.ds(pl.multiple_of((1 - core_ref[0]) * half, half), half)
-    qkv_ref[own_rows, :] = own_ref[0]
-    qkv_ref[other_rows, :] = other_ref[0]
-    do_ref[own_rows, :] = do_own_ref[0].astype(f32)
-    do_ref[other_rows, :] = do_other_ref[0].astype(f32)
-    qkv = qkv_ref[...]
-    cosine, sine = cos_ref[0], sin_ref[0]
-    grad_o = do_ref[...].astype(bf16)
-
-    def forward(lo, gain):
-        raw = qkv[:, lo : lo + HD]
-        scale = inverse_rms(raw)
-        unit = raw * scale
-        normed = unit * gain
-        return unit, scale, (normed * cosine + swap_halves(normed) * sine).astype(bf16)
-
-    def backward(grad_rot, unit, scale, gain):
-        grad_normed = grad_rot * cosine - swap_halves(grad_rot) * sine
-        gain_part = jnp.sum(unit * grad_normed, axis=0, keepdims=True)
-        weighted = grad_normed * gain
-        mean = jnp.mean(weighted * unit, axis=-1, keepdims=True)
-        return scale * (weighted - unit * mean), gain_part
-
-    query_gain, key_gain = gain_ref[0:1, :], gain_ref[1:2, :]
-    key_unit, key_scale, key = forward(2 * HD, key_gain)
-    value = qkv[:, 3 * HD : 4 * HD].astype(bf16)
-    grad_key = jnp.zeros((length, HD), f32)
-    grad_value = jnp.zeros((length, HD), f32)
-    query_gain_part = jnp.zeros((1, HD), f32)
-    parts = []
-    for head in range(2):
-        query_unit, query_scale, query = forward(head * HD, query_gain)
-        low = p_ref[0, head]
-        wide = low.astype(f32)
-        grad_head = grad_o[:, head * HD : (head + 1) * HD]
-        grad_weights = dot_nt(grad_head, value)
-        delta = jnp.sum(wide * grad_weights, axis=-1, keepdims=True)
-        grad_scores = (wide * (grad_weights - delta) * HD**-0.5).astype(bf16)
-        grad_value += dot_tn(low, grad_head)
-        grad_key += dot_tn(grad_scores, query)
-        part, gain_part = backward(dot_nn(grad_scores, key), query_unit, query_scale, query_gain)
-        query_gain_part += gain_part
-        parts.append(part)
-    part, key_gain_part = backward(grad_key, key_unit, key_scale, key_gain)
-    parts += [part, grad_value]
-    qkv_ref[...] = jnp.concatenate(parts, axis=-1)
-    d_own_ref[0] = qkv_ref[own_rows, :].astype(bf16)
-    d_other_ref[0] = qkv_ref[other_rows, :].astype(bf16)
-    dgain_ref[0] = jnp.concatenate([query_gain_part, key_gain_part], axis=-1)
+
+    def backward_one(seq):
+        qkv_ref[seq, own_rows, :] = own_ref[seq]
+        qkv_ref[seq, other_rows, :] = other_ref[seq]
+        do_ref[seq, own_rows, :] = do_own_ref[seq].astype(f32)
+        do_ref[seq, other_rows, :] = do_other_ref[seq].astype(f32)
+        qkv = qkv_ref[seq]
+        cosine, sine = cos_ref[seq], sin_ref[seq]
+        grad_o = do_ref[seq].astype(bf16)
+
+        def forward(lo, gain):
+            raw = qkv[:, lo : lo + HD]
+            scale = inverse_rms(raw)
+            unit = raw * scale
+            normed = unit * gain
+            return unit, scale, (normed * cosine + swap_halves(normed) * sine).astype(bf16)
+
+        def backward(grad_rot, unit, scale, gain):
+            grad_normed = grad_rot * cosine - swap_halves(grad_rot) * sine
+            gain_part = jnp.sum(unit * grad_normed, axis=0, keepdims=True)
+            weighted = grad_normed * gain
+            mean = jnp.mean(weighted * unit, axis=-1, keepdims=True)
+            return scale * (weighted - unit * mean), gain_part
+
+        query_gain, key_gain = gain_ref[0:1, :], gain_ref[1:2, :]
+        key_unit, key_scale, key = forward(2 * HD, key_gain)
+        value = qkv[:, 3 * HD : 4 * HD].astype(bf16)
+        grad_key = jnp.zeros((length, HD), f32)
+        grad_value = jnp.zeros((length, HD), f32)
+        query_gain_part = jnp.zeros((1, HD), f32)
+        parts = []
+        for head in range(2):
+            query_unit, query_scale, query = forward(head * HD, query_gain)
+            low = p_ref[seq, head]
+            wide = low.astype(f32)
+            grad_head = grad_o[:, head * HD : (head + 1) * HD]
+            grad_weights = dot_nt(grad_head, value)
+            delta = jnp.sum(wide * grad_weights, axis=-1, keepdims=True)
+            grad_scores = (wide * (grad_weights - delta) * HD**-0.5).astype(bf16)
+            grad_value += dot_tn(low, grad_head)
+            grad_key += dot_tn(grad_scores, query)
+            part, gain_part = backward(dot_nn(grad_scores, key), query_unit, query_scale, query_gain)
+            query_gain_part += gain_part
+            parts.append(part)
+        part, key_gain_part = backward(grad_key, key_unit, key_scale, key_gain)
+        parts += [part, grad_value]
+        qkv_ref[seq] = jnp.concatenate(parts, axis=-1)
+        d_own_ref[seq] = qkv_ref[seq, own_rows, :].astype(bf16)
+        d_other_ref[seq] = qkv_ref[seq, other_rows, :].astype(bf16)
+        dgain_ref[seq] = jnp.concatenate([query_gain_part, key_gain_part], axis=-1)
+
+    for seq in range(cos_ref.shape[0]):
+        backward_one(seq)
 
 
 def seq_block(*shape):
-    return pl.BlockSpec((1,) + shape, lambda s, c: (s,) + (0,) * len(shape))
+    return pl.BlockSpec((STEP,) + shape, lambda s, c: (s,) + (0,) * len(shape))
 
 
 def attention_forward(core, own, other, cosine, sine, seg_col, seg_row, gains):
@@ -182,7 +193,7 @@
         attention_forward_kernel,
         grid_spec=pltpu.PrefetchScalarGridSpec(
             num_scalar_prefetch=1,
-            grid=(seqs,),
+            grid=(seqs // STEP,),
             in_specs=[
                 seq_block(half, width),
                 seq_block(half, width),
@@ -198,8 +209,8 @@
                 seq_block(2, length, length),
             ],
             scratch_shapes=[
-                pltpu.VMEM((length, width), f32),
-                pltpu.VMEM((length, 2 * HD), f32),
+                pltpu.VMEM((STEP, length, width), f32),
+                pltpu.VMEM((STEP, length, 2 * HD), f32),
             ],
         ),
         out_shape=[
@@ -207,6 +218,7 @@
             jax.ShapeDtypeStruct((seqs, half, 2 * HD), bf16),
             jax.ShapeDtypeStruct((seqs, 2, length, length), bf16),
         ],
+        compiler_params=pltpu.CompilerParams(vmem_limit_bytes=48 << 20),
         cost_estimate=SMALL_COST,
         name="attention_forward",
     )(core, own, other, cosine, sine, seg_col, seg_row, gains)
@@ -219,7 +231,7 @@
         attention_backward_kernel,
         grid_spec=pltpu.PrefetchScalarGridSpec(
             num_scalar_prefetch=1,
-            grid=(seqs,),
+            grid=(seqs // STEP,),
             in_specs=[
                 seq_block(half, width),
                 seq_block(half, width),
@@ -236,8 +248,8 @@
                 seq_block(1, 2 * HD),
             ],
             scratch_shapes=[
-                pltpu.VMEM((length, width), f32),
-                pltpu.VMEM((length, 2 * HD), f32),
+                pltpu.VMEM((STEP, length, width), f32),
+                pltpu.VMEM((STEP, length, 2 * HD), f32),
             ],
         ),
         out_shape=[
@@ -245,6 +257,7 @@
             jax.ShapeDtypeStruct((seqs, half, width), bf16),
             jax.ShapeDtypeStruct((seqs, 1, 2 * HD), f32),
         ],
+        compiler_params=pltpu.CompilerParams(vmem_limit_bytes=48 << 20),
         cost_estimate=SMALL_COST,
         name="attention_backward",
     )(core, own, other, do_own, do_other, cosine, sine, gains, weights)
@@ -429,14 +442,16 @@
         ffn_stack = after(quarters(w_gate, w_up, w_down.T), attn_stack)
         ffn_stack = with_layout_constraint(ffn_stack, Layout(major_to_minor=(0, 1, 2)))
         ffn_band = plane_exchange(ffn_stack).reshape(band, 3 * units)
+        ffn_band = with_layout_constraint(ffn_band, Layout(major_to_minor=(0, 1)))
         ffn_weights = lax.all_gather(ffn_band, "dp", axis_index_groups=lines)
+        ffn_weights = with_layout_constraint(ffn_weights, Layout(major_to_minor=(0, 1, 2)))
         ffn_weights = ffn_weights.reshape(width, 3 * units)
 
         bands = [attn_band]
         for k in range(1, depth):
             bands.append(dp_swap(attn_band, k * PLANE))
         attn_weights = jnp.concatenate(unxor(bands, level), axis=0)
-        own_x = gather_chips(after(block_input, ffn_band))
+        own_x = gather_chips(after(block_input, ffn_band, bands[1]))
         other_x = core_swap(own_x)
 
         w_qkv, w_out_t = attn_weights[:, : 4 * HD], attn_weights[:, 4 * HD :]
@@ -499,8 +514,6 @@
         other_dh = core_swap(own_dh)
 
         y_sum = after(y_own + core_swap(y_other).astype(f32), own_dh)
-        block_out = (hidden + reduce_chips(y_sum)).astype(bf16)
-
         do_pair = [
             dot_nn(dh, w_out_t).astype(bf16).reshape(PLANE, half, 2 * HD)
             for dh in (own_dh, other_dh)
@@ -508,6 +521,7 @@
         dqkv_own, dqkv_other, head_gain_parts = attention_backward(
             core_index, *qkv_pair, *do_pair, cosine, sine, head_gains, weights
         )
+        block_out = (hidden + reduce_chips(y_sum, dqkv_own)).astype(bf16)
         dqkv_own = after(dqkv_own, block_out).reshape(-1, 4 * HD)
         dqkv_other = dqkv_other.reshape(-1, 4 * HD)
 
@@ -553,7 +567,7 @@
         ffn_grads = jnp.moveaxis(ffn_grads, 0, 1).astype(f32)
 
 
-        grad_normed_one = reduce_chips(dn1_sum, ffn_grads)
+        grad_normed_one = reduce_chips(dn1_sum, messages[-1])
         total = total.astype(bf16).reshape(PLANE, rows, attn_width)
         extra = two_parts(gain_sum)
         received = [pick(total, place)]

time: 286 us -> 255 us (0.89)
  waiting for transfers between devices: 86.5 us -> 75.6 us
  Pallas kernels: 49.3 us -> 41.6 us
  local copies, waits for them, and re-layouts: 34.2 us -> 27.7 us
  matrix products: 14.6 us -> 9.6 us
    ppermute x42, waiting for transfers between devices: 80.2 us -> 71.2 us  [dp_swap(): return lax.ppermute(value, 'dp', [(i, i ^ mask) for i in range(devices)])]
    all_gather x1 -> x0, local copies, waits for them, and re-layouts: 5.84 us -> none  [body(): ffn_weights = lax.all_gather(ffn_band, 'dp', axis_index_groups=lines)]
    pallas_call x1, Pallas kernels: 12.9 us -> 7.21 us  [attention_forward(): pl.pallas_call(attention_forward_kernel, grid_spec=pltpu.PrefetchScalarGr...]
    all_gather x1, waiting for transfers between devices: 3.53 us -> 0.16 us  [body(): ffn_weights = lax.all_gather(ffn_band, 'dp', axis_index_groups=lines)]
    unnamed x97 -> x95, local copies, waits for them, and re-layouts: 5.95 us -> 8.92 us
    dot_general x4, matrix products: 4.78 us -> 1.87 us  [dot_nn(): lax.dot_general(a, b, (((1,), (0,)), ((), ())), preferred_element_type=f32)]
  transfers between devices with their start and end apart: 53 -> 53, of which waited for: 25 -> 23; matrix products, arithmetic and copies ran while one was open for 22% -> 20% of each run, Pallas kernels for 12% -> 10%
where the time goes in v2:
time: 255 us; the launch traced here: 253 us
  waiting for transfers between devices  75.6 us (30%)
  starting transfers between devices  54.3 us (21%)
  Pallas kernels  41.6 us (16%)
  other arithmetic  29.4 us (12%)
  local copies, waits for them, and re-layouts  27.7 us (11%)
  between operations  15.2 us (6%)
  matrix products  9.6 us (4%)
    ppermute x42, waiting for transfers between devices, dp_swap(): return lax.ppermute(value, 'dp', [(i, i ^ mask) for i in range(devices)])  71.2 us
    ppermute x42, starting transfers between devices, dp_swap(): return lax.ppermute(value, 'dp', [(i, i ^ mask) for i in range(devices)])  53.8 us
    pallas_call x2, Pallas kernels, ffn_half(): pl.pallas_call(ffn_kernel, grid=(tokens // tile,), in_specs=[rows_of(widt...  15.2 us
    pallas_call x1, Pallas kernels, attention_backward(): pl.pallas_call(attention_backward_kernel, grid_spec=pltpu.PrefetchScalarG...  11 us
    unnamed x95, local copies, waits for them, and re-layouts  8.92 us
    pallas_call x1, Pallas kernels, ffn_grads_call(): pl.pallas_call(ffn_grads_kernel, grid=(width // tile,), in_specs=[slab] *...  8.17 us
    pallas_call x1, Pallas kernels, attention_forward(): pl.pallas_call(attention_forward_kernel, grid_spec=pltpu.PrefetchScalarGr...  7.21 us
    reshape x7, local copies, waits for them, and re-layouts, columns(): return grads[:, :, lo:hi].reshape(rows, -1)  6.57 us
  transfers between devices with their start and end apart: 53, of which 23 were waited for; matrix products, arithmetic and copies ran while one was open for 20% of the time, Pallas kernels for 10%

profile of v2, /device:TPU:0, one launch (start us, length us, event | category | flops | bytes accessed | tf_op | source)
XLA Modules:
  0.0 253.4 jit_solution(12780569718869231462)
XLA Ops:
  11.6 3.0 %collective-permute-start.4 = (bf16[66,384]{1,0:T(8,128)(2,1)S(1)}, bf16[66,384]{1,0:T(8,128)(2,1)S(1)}, u32[]{:S(2)}, u32[]{:S(2)}) collective-permute-start(bf16[66,384]{1,0:T(8,128)(2,1)S(1)} %get-tuple-element.158), channel_id=1, source_target_pairs={{0,4},{2,6},{4,0},{6,2},{8,12},{10,14},{12,8},{14,10},{16,20},{18,... | collective-permute-start | bytes 152072 | tf_op jit(solution)/shard_map/ppermute | solution.py:371
  14.6 1.4 collective-permute-start.3
  19.0 2.9 %collective-permute-start = (bf16[64,1728]{1,0:T(8,128)(2,1)S(1)}, bf16[64,1728]{1,0:T(8,128)(2,1)S(1)}, u32[]{:S(2)}, u32[]{:S(2)}) collective-permute-start(bf16[64,1728]{1,0:T(8,128)(2,1)S(1)} %get-tuple-element.137), channel_id=1, source_target_pairs={{0,6},{2,4},{4,2},{6,0},{8,14},{10,12},{12,10},{14,8},{16,22},{18,... | collective-permute-start | bytes 663560 | tf_op jit(solution)/shard_map/ppermute | solution.py:371
  23.5 3.0 %collective-permute-start.11 = (bf16[256,384]{1,0:T(8,128)(2,1)}, bf16[256,384]{1,0:T(8,128)(2,1)S(1)}, u32[]{:S(2)}, u32[]{:S(2)}) collective-permute-start(bf16[256,384]{1,0:T(8,128)(2,1)} %pad_maximum_fusion.14), channel_id=1, source_target_pairs={{0,16},{2,18},{4,20},{6,22},{8,24},{10,26},{12,28},{14,30},{16,0},... | collective-permute-start | bytes 589832 | tf_op jit(solution)/shard_map/ppermute | solution.py:371
  28.6 2.0 collective-permute-start.6
  34.8 5.1 %collective-permute-done.6 = bf16[256,384]{1,0:T(8,128)(2,1)S(1)} collective-permute-done((bf16[256,384]{1,0:T(8,128)(2,1)}, bf16[256,384]{1,0:T(8,128)(2,1)S(1)}, u32[]{:S(2)}, u32[]{:S(2)}) %collective-permute-start.6) | collective-permute-done | bytes 196640 | tf_op jit(solution)/shard_map/ppermute | solution.py:371
  39.9 2.5 collective-permute-start.9
  43.4 1.9 fusion.58
  46.0 1.4 collective-permute-done.9
  47.4 2.7 %collective-permute-done.8 = bf16[128,1024]{1,0:T(8,128)(2,1)} collective-permute-done((bf16[128,1024]{1,0:T(8,128)(2,1)S(1)}, bf16[128,1024]{1,0:T(8,128)(2,1)}, u32[]{:S(2)}, u32[]{:S(2)}) %collective-permute-start.8) | collective-permute-done | bytes 262176 | tf_op jit(solution)/shard_map/ppermute | solution.py:371
  54.4 1.5 collective-permute-start.13
  59.3 7.2 %attention_forward.1 = (bf16[4,128,128]{2,1,0:T(8,128)(2,1)S(1)}, bf16[4,128,128]{2,1,0:T(8,128)(2,1)S(1)}, bf16[4,2,256,256]{3,2,1,0:T(8,128)(2,1)S(1)}) custom-call(s32[1]{0:T(128)} %bitcast.core_ref, f32[4,128,256]{2,1,0:T(8,128)S(1)} %bitcast.188, f32[4,128,256]{2,1,0:T(8,128)S(1)} %bitcast.190, f32[4,256,64]{2,1,0:T(8,128)S(1)} %pad_maximum_fusion.5.cos_ref, ...), custom_call_target="tpu_custom_call" | custom-call | flops 1000000 | bytes 100000 | tf_op jit(solution)/shard_map/attention_forward/pallas_call | solution.py:192
  66.6 3.1 %collective-permute-done.14 = bf16[128,1024]{1,0:T(8,128)(2,1)S(1)} collective-permute-done((bf16[128,1024]{1,0:T(8,128)(2,1)S(1)}, bf16[128,1024]{1,0:T(8,128)(2,1)S(1)}, u32[]{:S(2)}, u32[]{:S(2)}) %collective-permute-start.14) | collective-permute-done | bytes 262176 | tf_op jit(solution)/shard_map/ppermute | solution.py:371
  70.3 2.6 %collective-permute-done.16 = bf16[512,1024]{1,0:T(8,128)(2,1)S(1)} collective-permute-done((bf16[512,1024]{1,0:T(8,128)(2,1)S(1)}, bf16[512,1024]{1,0:T(8,128)(2,1)S(1)}, u32[]{:S(2)}, u32[]{:S(2)}) %collective-permute-start.16) | collective-permute-done | bytes 1048608 | tf_op jit(solution)/shard_map/ppermute | solution.py:374
  73.5 1.5 collective-permute-start.19
  77.0 6.6 %collective-permute-done.19 = bf16[128,1024]{1,0:T(8,128)(2,1)S(1)} collective-permute-done((bf16[128,1024]{1,0:T(8,128)(2,1)S(1)}, bf16[128,1024]{1,0:T(8,128)(2,1)S(1)}, u32[]{:S(2)}, u32[]{:S(2)}) %collective-permute-start.19) | collective-permute-done | bytes 262176 | tf_op jit(solution)/shard_map/ppermute | solution.py:371
  83.6 4.8 %collective-permute-done.18 = bf16[128,1024]{1,0:T(8,128)(2,1)S(1)} collective-permute-done((bf16[128,1024]{1,0:T(8,128)(2,1)S(1)}, bf16[128,1024]{1,0:T(8,128)(2,1)S(1)}, u32[]{:S(2)}, u32[]{:S(2)}) %collective-permute-start.18) | collective-permute-done | bytes 262176 | tf_op jit(solution)/shard_map/ppermute | solution.py:371
  88.8 1.5 collective-permute-start.22
  92.4 6.6 %collective-permute-done.22 = bf16[128,1024]{1,0:T(8,128)(2,1)S(1)} collective-permute-done((bf16[128,1024]{1,0:T(8,128)(2,1)S(1)}, bf16[128,1024]{1,0:T(8,128)(2,1)S(1)}, u32[]{:S(2)}, u32[]{:S(2)}) %collective-permute-start.22) | collective-permute-done | bytes 262176 | tf_op jit(solution)/shard_map/ppermute | solution.py:371
  99.0 4.8 %collective-permute-done.21 = bf16[128,1024]{1,0:T(8,128)(2,1)S(1)} collective-permute-done((bf16[128,1024]{1,0:T(8,128)(2,1)S(1)}, bf16[128,1024]{1,0:T(8,128)(2,1)S(1)}, u32[]{:S(2)}, u32[]{:S(2)}) %collective-permute-start.21) | collective-permute-done | bytes 262176 | tf_op jit(solution)/shard_map/ppermute | solution.py:371
  105.0 1.6 collective-permute-done.23.n_ref.n1_ref
  110.1 7.1 %ffn_half.2 = (bf16[512,1024]{1,0:T(8,128)(2,1)S(1)}, bf16[512,1024]{1,0:T(8,128)(2,1)S(1)}, bf16[512,576]{1,0:T(8,128)(2,1)S(1)}, bf16[512,1152]{1,0:T(8,128)(2,1)S(1)}) custom-call(bf16[512,1024]{1,0:T(8,128)(2,1)S(1)} %copy-done.9, bf16[512,1024]{1,0:T(8,128)(2,1)S(1)} %copy-done.7, bf16[1024,1728]{1,0:T(8,128)(2,1)} %all-gather.3.cloned.1.call-done.w_ref), custom_call_target="tpu_custom_call" | custom-call | flops 1000000 | bytes 100000 | tf_op jit(solution)/shard_map/ffn_half/pallas_call | solution.py:291
  119.3 8.0 %ffn_half.3 = (f32[512,1024]{1,0:T(8,128)S(1)}, f32[512,1024]{1,0:T(8,128)}, bf16[512,576]{1,0:T(8,128)(2,1)S(1)}, bf16[512,1152]{1,0:T(8,128)(2,1)S(1)}) custom-call(bf16[512,1024]{1,0:T(8,128)(2,1)S(1)} %pad_maximum_fusion.1.n_ref.n0_ref, bf16[512,1024]{1,0:T(8,128)(2,1)S(1)} %copy-done.3, bf16[1024,1728]{1,0:T(8,128)(2,1)} %all-gather.3.cloned.1.call-done.w_ref), custom_call_target="tpu_custom_call" | custom-call | flops 1000000 | bytes 100000 | tf_op jit(solution)/shard_map/ffn_half/pallas_call | solution.py:291
  127.4 2.3 fusion.69
  129.7 8.2 %ffn_grads.1 = bf16[1024,1728]{1,0:T(8,128)(2,1)} custom-call(bf16[512,1024]{1,0:T(8,128)(2,1)S(1)} %pad_maximum_fusion.1.n_ref.n0_ref, bf16[512,1024]{1,0:T(8,128)(2,1)S(1)} %copy-done.9, bf16[512,1024]{1,0:T(8,128)(2,1)S(1)} %copy-done.3, bf16[512,1024]{1,0:T(8,128)(2,1)S(1)} %copy-done.7, bf16[512,1152]{1,0:T(8,128)(2,1)} %copy-done.11, ...), custom_call_target="tpu_custom_call" | custom-call | flops 3623878656 | bytes 11272192 | tf_op jit(solution)/shard_map/ffn_grads/pallas_call | solution.py:330
  139.2 2.5 collective-permute-start.29
  142.8 6.5 %collective-permute-done.29 = bf16[128,1024]{1,0:T(8,128)(2,1)S(1)} collective-permute-done((bf16[128,1024]{1,0:T(8,128)(2,1)S(1)}, bf16[128,1024]{1,0:T(8,128)(2,1)S(1)}, u32[]{:S(2)}, u32[]{:S(2)}) %collective-permute-start.29) | collective-permute-done | bytes 262176 | tf_op jit(solution)/shard_map/ppermute | solution.py:371
  149.3 5.2 %collective-permute-done.28 = bf16[128,1024]{1,0:T(8,128)(2,1)S(1)} collective-permute-done((bf16[128,1024]{1,0:T(8,128)(2,1)S(1)}, bf16[128,1024]{1,0:T(8,128)(2,1)S(1)}, u32[]{:S(2)}, u32[]{:S(2)}) %collective-permute-start.28) | collective-permute-done | bytes 262176 | tf_op jit(solution)/shard_map/ppermute | solution.py:371
  154.6 1.5 multiply_reduce_fusion
  157.9 1.7 collective-permute-start.32
  161.4 6.9 %collective-permute-done.32 = bf16[128,1024]{1,0:T(8,128)(2,1)} collective-permute-done((bf16[128,1024]{1,0:T(8,128)(2,1)}, bf16[128,1024]{1,0:T(8,128)(2,1)}, u32[]{:S(2)}, u32[]{:S(2)}) %collective-permute-start.32) | collective-permute-done | bytes 262176 | tf_op jit(solution)/shard_map/ppermute | solution.py:371
  168.3 4.7 %collective-permute-done.31 = bf16[128,1024]{1,0:T(8,128)(2,1)} collective-permute-done((bf16[128,1024]{1,0:T(8,128)(2,1)}, bf16[128,1024]{1,0:T(8,128)(2,1)}, u32[]{:S(2)}, u32[]{:S(2)}) %collective-permute-start.31) | collective-permute-done | bytes 262176 | tf_op jit(solution)/shard_map/ppermute | solution.py:371
  174.5 1.9 convert_add_fusion.2
  176.7 1.5 collective-permute-start.36
  178.2 1.4 collective-permute-start.35
  181.1 11.0 %attention_backward.1 = (bf16[4,128,256]{2,1,0:T(8,128)(2,1)S(1)}, bf16[4,128,256]{2,1,0:T(8,128)(2,1)S(1)}, f32[4,1,128]{2,1,0:T(1,128)S(1)}) custom-call(s32[1]{0:T(128)} %bitcast.core_ref, f32[4,128,256]{2,1,0:T(8,128)S(1)} %bitcast.189, f32[4,128,256]{2,1,0:T(8,128)S(1)} %bitcast.191, bf16[4,128,128]{2,1,0:T(8,128)(2,1)S(1)} %bitcast.200, ...), custom_call_target="tpu_custom_call" | custom-call | flops 1000000 | bytes 100000 | tf_op jit(solution)/shard_map/attention_backward/pallas_call | solution.py:230
  192.2 1.5 convolution_convert_fusion.1
  195.5 1.9 fusion.35
  199.1 1.9 fusion.3
  201.9 1.4 collective-permute-start.41
  203.4 1.5 collective-permute-start.40
  205.5 2.1 pad_maximum_fusion.8
  207.6 2.8 %collective-permute-start.39 = (bf16[268,384]{1,0:T(8,128)(2,1)}, bf16[268,384]{1,0:T(8,128)(2,1)S(1)}, u32[]{:S(2)}, u32[]{:S(2)}) collective-permute-start(bf16[268,384]{1,0:T(8,128)(2,1)} %get-tuple-element.84), channel_id=1, source_target_pairs={{0,24},{2,26},{4,28},{6,30},{8,16},{10,18},{12,20},{14,22},{16,8},... | collective-permute-start | bytes 617480 | tf_op jit(solution)/shard_map/ppermute | solution.py:371
  213.3 4.5 %collective-permute-done.39 = bf16[268,384]{1,0:T(8,128)(2,1)S(1)} collective-permute-done((bf16[268,384]{1,0:T(8,128)(2,1)}, bf16[268,384]{1,0:T(8,128)(2,1)S(1)}, u32[]{:S(2)}, u32[]{:S(2)}) %collective-permute-start.39) | collective-permute-done | bytes 205856 | tf_op jit(solution)/shard_map/ppermute | solution.py:371
  219.1 1.5 collective-permute-start.49
  222.5 5.6 %collective-permute-done.43 = bf16[268,384]{1,0:T(8,128)(2,1)S(1)} collective-permute-done((bf16[268,384]{1,0:T(8,128)(2,1)}, bf16[268,384]{1,0:T(8,128)(2,1)S(1)}, u32[]{:S(2)}, u32[]{:S(2)}) %collective-permute-start.43) | collective-permute-done | bytes 205856 | tf_op jit(solution)/shard_map/ppermute | solution.py:371
  229.0 2.1 collective-permute-start.46
  231.7 2.1 fusion.14
  (281 shorter events, 71.1 us)
Async XLA Ops:
  7.2 100.5 %all-gather.3.cloned.1.call-start = ((), (), s32[]{:S(2)}) async-start(), calls=%async_computation.2 | async-start | bytes 4587520 | tf_op jit(solution)/shard_map/all_gather | solution.py:446
  11.6 11.0 %collective-permute-start.4 = (bf16[66,384]{1,0:T(8,128)(2,1)S(1)}, bf16[66,384]{1,0:T(8,128)(2,1)S(1)}, u32[]{:S(2)}, u32[]{:S(2)}) collective-permute-start(bf16[66,384]{1,0:T(8,128)(2,1)S(1)} %get-tuple-element.158), channel_id=1, source_target_pairs={{0,4},{2,6},{4,0},{6,2},{8,12},{10,14},{12,8},{14,10},{16,20},{18,... | collective-permute-start | bytes 152072 | tf_op jit(solution)/shard_map/ppermute | solution.py:371
  14.6 8.2 %collective-permute-start.3 = (bf16[66,384]{1,0:T(8,128)(2,1)S(1)}, bf16[66,384]{1,0:T(8,128)(2,1)S(1)}, u32[]{:S(2)}, u32[]{:S(2)}) collective-permute-start(bf16[66,384]{1,0:T(8,128)(2,1)S(1)} %get-tuple-element.159), channel_id=1, source_target_pairs={{0,6},{2,4},{4,2},{6,0},{8,14},{10,12},{12,10},{14,8},{16,22},{18,... | collective-permute-start | bytes 152072 | tf_op jit(solution)/shard_map/ppermute | solution.py:371
  16.1 6.7 %collective-permute-start.5 = (bf16[66,384]{1,0:T(8,128)(2,1)S(1)}, bf16[66,384]{1,0:T(8,128)(2,1)S(1)}, u32[]{:S(2)}, u32[]{:S(2)}) collective-permute-start(bf16[66,384]{1,0:T(8,128)(2,1)S(1)} %get-tuple-element.157), channel_id=1, source_target_pairs={{0,2},{2,0},{4,6},{6,4},{8,10},{10,8},{12,14},{14,12},{16,18},{18,... | collective-permute-start | bytes 152072 | tf_op jit(solution)/shard_map/ppermute | solution.py:371
  19.0 9.5 %collective-permute-start = (bf16[64,1728]{1,0:T(8,128)(2,1)S(1)}, bf16[64,1728]{1,0:T(8,128)(2,1)S(1)}, u32[]{:S(2)}, u32[]{:S(2)}) collective-permute-start(bf16[64,1728]{1,0:T(8,128)(2,1)S(1)} %get-tuple-element.137), channel_id=1, source_target_pairs={{0,6},{2,4},{4,2},{6,0},{8,14},{10,12},{12,10},{14,8},{16,22},{18,... | collective-permute-start | bytes 663560 | tf_op jit(solution)/shard_map/ppermute | solution.py:371
  22.0 9.7 %collective-permute-start.1 = (bf16[64,1728]{1,0:T(8,128)(2,1)S(1)}, bf16[64,1728]{1,0:T(8,128)(2,1)S(1)}, u32[]{:S(2)}, u32[]{:S(2)}) collective-permute-start(bf16[64,1728]{1,0:T(8,128)(2,1)S(1)} %get-tuple-element.136), channel_id=1, source_target_pairs={{0,4},{2,6},{4,0},{6,2},{8,12},{10,14},{12,8},{14,10},{16,20},{18,... | collective-permute-start | bytes 663560 | tf_op jit(solution)/shard_map/ppermute | solution.py:371
  22.6 9.8 %collective-permute-start.2 = (bf16[64,1728]{1,0:T(8,128)(2,1)S(1)}, bf16[64,1728]{1,0:T(8,128)(2,1)}, u32[]{:S(2)}, u32[]{:S(2)}) collective-permute-start(bf16[64,1728]{1,0:T(8,128)(2,1)S(1)} %get-tuple-element.135), channel_id=1, source_target_pairs={{0,2},{2,0},{4,6},{6,4},{8,10},{10,8},{12,14},{14,12},{16,18},{18,... | collective-permute-start | bytes 663560 | tf_op jit(solution)/shard_map/ppermute | solution.py:371
  23.5 28.3 %collective-permute-start.11 = (bf16[256,384]{1,0:T(8,128)(2,1)}, bf16[256,384]{1,0:T(8,128)(2,1)S(1)}, u32[]{:S(2)}, u32[]{:S(2)}) collective-permute-start(bf16[256,384]{1,0:T(8,128)(2,1)} %pad_maximum_fusion.14), channel_id=1, source_target_pairs={{0,16},{2,18},{4,20},{6,22},{8,24},{10,26},{12,28},{14,30},{16,0},... | collective-permute-start | bytes 589832 | tf_op jit(solution)/shard_map/ppermute | solution.py:371
  26.5 25.3 %collective-permute-start.10 = (bf16[256,384]{1,0:T(8,128)(2,1)}, bf16[256,384]{1,0:T(8,128)(2,1)}, u32[]{:S(2)}, u32[]{:S(2)}) collective-permute-start(bf16[256,384]{1,0:T(8,128)(2,1)} %pad_maximum_fusion.14), channel_id=1, source_target_pairs={{0,24},{2,26},{4,28},{6,30},{8,16},{10,18},{12,20},{14,22},{16,8},... | collective-permute-start | bytes 589832 | tf_op jit(solution)/shard_map/ppermute | solution.py:371
  28.6 11.4 %collective-permute-start.6 = (bf16[256,384]{1,0:T(8,128)(2,1)}, bf16[256,384]{1,0:T(8,128)(2,1)S(1)}, u32[]{:S(2)}, u32[]{:S(2)}) collective-permute-start(bf16[256,384]{1,0:T(8,128)(2,1)} %pad_maximum_fusion.14), channel_id=1, source_target_pairs={{0,8},{2,10},{4,12},{6,14},{8,0},{10,2},{12,4},{14,6},{16,24},{18,... | collective-permute-start | bytes 589832 | tf_op jit(solution)/shard_map/ppermute | solution.py:371
  34.7 172.9 %reduce-scatter.2.cloned.1.call-start = ((), (), s32[]{:S(2)}) async-start(), calls=%async_computation.1 | async-start | bytes 4587520 | tf_op jit(solution)/shard_map/reduce_scatter | solution.py:503
  39.9 7.5 %collective-permute-start.9 = (bf16[128,1024]{1,0:T(8,128)(2,1)S(1)}, bf16[128,1024]{1,0:T(8,128)(2,1)}, u32[]{:S(2)}, u32[]{:S(2)}) collective-permute-start(bf16[128,1024]{1,0:T(8,128)(2,1)S(1)} %copy-done.26), channel_id=1, source_target_pairs={{0,6},{2,4},{4,2},{6,0},{8,14},{10,12},{12,10},{14,8},{16,22},{18,... | collective-permute-start | bytes 786440 | tf_op jit(solution)/shard_map/ppermute | solution.py:371
  42.5 7.7 %collective-permute-start.8 = (bf16[128,1024]{1,0:T(8,128)(2,1)S(1)}, bf16[128,1024]{1,0:T(8,128)(2,1)}, u32[]{:S(2)}, u32[]{:S(2)}) collective-permute-start(bf16[128,1024]{1,0:T(8,128)(2,1)S(1)} %copy-done.26), channel_id=1, source_target_pairs={{0,4},{2,6},{4,0},{6,2},{8,12},{10,14},{12,8},{14,10},{16,20},{18,... | collective-permute-start | bytes 786440 | tf_op jit(solution)/shard_map/ppermute | solution.py:371
  43.0 7.3 %collective-permute-start.7 = (bf16[128,1024]{1,0:T(8,128)(2,1)S(1)}, bf16[128,1024]{1,0:T(8,128)(2,1)}, u32[]{:S(2)}, u32[]{:S(2)}) collective-permute-start(bf16[128,1024]{1,0:T(8,128)(2,1)S(1)} %copy-done.26), channel_id=1, source_target_pairs={{0,2},{2,0},{4,6},{6,4},{8,10},{10,8},{12,14},{14,12},{16,18},{18,... | collective-permute-start | bytes 786440 | tf_op jit(solution)/shard_map/ppermute | solution.py:371
  51.7 6.8 %collective-permute-start.12 = (bf16[512,1024]{1,0:T(8,128)(2,1)S(1)}, bf16[512,1024]{1,0:T(8,128)(2,1)S(1)}, u32[]{:S(2)}, u32[]{:S(2)}) collective-permute-start(bf16[512,1024]{1,0:T(8,128)(2,1)S(1)} %get-tuple-element.106), channel_id=1, source_target_pairs={{0,1},{1,0},{2,3},{3,2},{4,5},{5,4},{6,7},{7,6},{8,9},{9,8},{10,11... | collective-permute-start | bytes 3145736 | tf_op jit(solution)/shard_map/ppermute | solution.py:374
  54.4 12.2 %collective-permute-start.13 = (bf16[128,1024]{1,0:T(8,128)(2,1)S(1)}, bf16[128,1024]{1,0:T(8,128)(2,1)S(1)}, u32[]{:S(2)}, u32[]{:S(2)}) collective-permute-start(bf16[128,1024]{1,0:T(8,128)(2,1)S(1)} %copy-done.31), channel_id=1, source_target_pairs={{0,2},{2,0},{4,6},{6,4},{8,10},{10,8},{12,14},{14,12},{16,18},{18,... | collective-permute-start | bytes 786440 | tf_op jit(solution)/shard_map/ppermute | solution.py:371
  56.0 13.7 %collective-permute-start.14 = (bf16[128,1024]{1,0:T(8,128)(2,1)S(1)}, bf16[128,1024]{1,0:T(8,128)(2,1)S(1)}, u32[]{:S(2)}, u32[]{:S(2)}) collective-permute-start(bf16[128,1024]{1,0:T(8,128)(2,1)S(1)} %copy-done.31), channel_id=1, source_target_pairs={{0,4},{2,6},{4,0},{6,2},{8,12},{10,14},{12,8},{14,10},{16,20},{18,... | collective-permute-start | bytes 786440 | tf_op jit(solution)/shard_map/ppermute | solution.py:371
  56.9 12.8 %collective-permute-start.15 = (bf16[128,1024]{1,0:T(8,128)(2,1)S(1)}, bf16[128,1024]{1,0:T(8,128)(2,1)S(1)}, u32[]{:S(2)}, u32[]{:S(2)}) collective-permute-start(bf16[128,1024]{1,0:T(8,128)(2,1)S(1)} %copy-done.31), channel_id=1, source_target_pairs={{0,6},{2,4},{4,2},{6,0},{8,14},{10,12},{12,10},{14,8},{16,22},{18,... | collective-permute-start | bytes 786440 | tf_op jit(solution)/shard_map/ppermute | solution.py:371
  73.5 10.2 %collective-permute-start.19 = (bf16[128,1024]{1,0:T(8,128)(2,1)S(1)}, bf16[128,1024]{1,0:T(8,128)(2,1)S(1)}, u32[]{:S(2)}, u32[]{:S(2)}) collective-permute-start(bf16[128,1024]{1,0:T(8,128)(2,1)S(1)} %get-tuple-element.130), channel_id=1, source_target_pairs={{0,6},{2,4},{4,2},{6,0},{8,14},{10,12},{12,10},{14,8},{16,22},{18,... | collective-permute-start | bytes 786440 | tf_op jit(solution)/shard_map/ppermute | solution.py:371
  74.9 13.5 %collective-permute-start.18 = (bf16[128,1024]{1,0:T(8,128)(2,1)S(1)}, bf16[128,1024]{1,0:T(8,128)(2,1)S(1)}, u32[]{:S(2)}, u32[]{:S(2)}) collective-permute-start(bf16[128,1024]{1,0:T(8,128)(2,1)S(1)} %get-tuple-element.131), channel_id=1, source_target_pairs={{0,4},{2,6},{4,0},{6,2},{8,12},{10,14},{12,8},{14,10},{16,20},{18,... | collective-permute-start | bytes 786440 | tf_op jit(solution)/shard_map/ppermute | solution.py:371
  75.6 12.8 %collective-permute-start.17 = (bf16[128,1024]{1,0:T(8,128)(2,1)S(1)}, bf16[128,1024]{1,0:T(8,128)(2,1)S(1)}, u32[]{:S(2)}, u32[]{:S(2)}) collective-permute-start(bf16[128,1024]{1,0:T(8,128)(2,1)S(1)} %get-tuple-element.129), channel_id=1, source_target_pairs={{0,2},{2,0},{4,6},{6,4},{8,10},{10,8},{12,14},{14,12},{16,18},{18,... | collective-permute-start | bytes 786440 | tf_op jit(solution)/shard_map/ppermute | solution.py:371
  88.8 10.2 %collective-permute-start.22 = (bf16[128,1024]{1,0:T(8,128)(2,1)S(1)}, bf16[128,1024]{1,0:T(8,128)(2,1)S(1)}, u32[]{:S(2)}, u32[]{:S(2)}) collective-permute-start(bf16[128,1024]{1,0:T(8,128)(2,1)S(1)} %multiply_convert_fusion), channel_id=1, source_target_pairs={{0,6},{2,4},{4,2},{6,0},{8,14},{10,12},{12,10},{14,8},{16,22},{18,... | collective-permute-start | bytes 786440 | tf_op jit(solution)/shard_map/ppermute | solution.py:371
  90.3 13.4 %collective-permute-start.21 = (bf16[128,1024]{1,0:T(8,128)(2,1)S(1)}, bf16[128,1024]{1,0:T(8,128)(2,1)S(1)}, u32[]{:S(2)}, u32[]{:S(2)}) collective-permute-start(bf16[128,1024]{1,0:T(8,128)(2,1)S(1)} %multiply_convert_fusion), channel_id=1, source_target_pairs={{0,4},{2,6},{4,0},{6,2},{8,12},{10,14},{12,8},{14,10},{16,20},{18,... | collective-permute-start | bytes 786440 | tf_op jit(solution)/shard_map/ppermute | solution.py:371
  91.0 12.8 %collective-permute-start.20 = (bf16[128,1024]{1,0:T(8,128)(2,1)S(1)}, bf16[128,1024]{1,0:T(8,128)(2,1)S(1)}, u32[]{:S(2)}, u32[]{:S(2)}) collective-permute-start(bf16[128,1024]{1,0:T(8,128)(2,1)S(1)} %multiply_convert_fusion), channel_id=1, source_target_pairs={{0,2},{2,0},{4,6},{6,4},{8,10},{10,8},{12,14},{14,12},{16,18},{18,... | collective-permute-start | bytes 786440 | tf_op jit(solution)/shard_map/ppermute | solution.py:371
  92.4 11.6 %collective-permute-start.24 = (bf16[512,1024]{1,0:T(8,128)(2,1)S(1)}, bf16[512,1024]{1,0:T(8,128)(2,1)S(1)}, u32[]{:S(2)}, u32[]{:S(2)}) collective-permute-start(bf16[512,1024]{1,0:T(8,128)(2,1)S(1)} %constant_dynamic-update-slice_fusion.g_ref.g0_ref), channel_id=1, source_target_pairs={{0,1},{1,0},{2,3},{3,2},{4,5},{5,4},{6,7},{7,6},{8,9},{9,8},{10,11... | collective-permute-start | bytes 3145736 | tf_op jit(solution)/shard_map/ppermute | solution.py:374
  119.3 8.0 %collective-permute-start.26 = (bf16[512,1024]{1,0:T(8,128)(2,1)S(1)}, bf16[512,1024]{1,0:T(8,128)(2,1)S(1)}, u32[]{:S(2)}, u32[]{:S(2)}) collective-permute-start(bf16[512,1024]{1,0:T(8,128)(2,1)S(1)} %get-tuple-element.63), channel_id=1, source_target_pairs={{0,1},{1,0},{2,3},{3,2},{4,5},{5,4},{6,7},{7,6},{8,9},{9,8},{10,11... | collective-permute-start | bytes 3145736 | tf_op jit(solution)/shard_map/ppermute | solution.py:374
  139.2 10.1 %collective-permute-start.29 = (bf16[128,1024]{1,0:T(8,128)(2,1)S(1)}, bf16[128,1024]{1,0:T(8,128)(2,1)S(1)}, u32[]{:S(2)}, u32[]{:S(2)}) collective-permute-start(bf16[128,1024]{1,0:T(8,128)(2,1)S(1)} %get-tuple-element.127), channel_id=1, source_target_pairs={{0,6},{2,4},{4,2},{6,0},{8,14},{10,12},{12,10},{14,8},{16,22},{18,... | collective-permute-start | bytes 786440 | tf_op jit(solution)/shard_map/ppermute | solution.py:371
  141.7 12.8 %collective-permute-start.28 = (bf16[128,1024]{1,0:T(8,128)(2,1)S(1)}, bf16[128,1024]{1,0:T(8,128)(2,1)S(1)}, u32[]{:S(2)}, u32[]{:S(2)}) collective-permute-start(bf16[128,1024]{1,0:T(8,128)(2,1)S(1)} %get-tuple-element.128), channel_id=1, source_target_pairs={{0,4},{2,6},{4,0},{6,2},{8,12},{10,14},{12,8},{14,10},{16,20},{18,... | collective-permute-start | bytes 786440 | tf_op jit(solution)/shard_map/ppermute | solution.py:371
  142.3 12.4 %collective-permute-start.27 = (bf16[128,1024]{1,0:T(8,128)(2,1)S(1)}, bf16[128,1024]{1,0:T(8,128)(2,1)S(1)}, u32[]{:S(2)}, u32[]{:S(2)}) collective-permute-start(bf16[128,1024]{1,0:T(8,128)(2,1)S(1)} %get-tuple-element.126), channel_id=1, source_target_pairs={{0,2},{2,0},{4,6},{6,4},{8,10},{10,8},{12,14},{14,12},{16,18},{18,... | collective-permute-start | bytes 786440 | tf_op jit(solution)/shard_map/ppermute | solution.py:371
  142.8 31.7 %collective-permute-start.25 = (bf16[512,1024]{1,0:T(8,128)(2,1)S(1)}, bf16[512,1024]{1,0:T(8,128)(2,1)}, u32[]{:S(2)}, u32[]{:S(2)}) collective-permute-start(bf16[512,1024]{1,0:T(8,128)(2,1)S(1)} %copy-done.13), channel_id=1, source_target_pairs={{0,1},{1,0},{2,3},{3,2},{4,5},{5,4},{6,7},{7,6},{8,9},{9,8},{10,11... | collective-permute-start | bytes 3145736 | tf_op jit(solution)/shard_map/ppermute | solution.py:374
  157.9 10.4 %collective-permute-start.32 = (bf16[128,1024]{1,0:T(8,128)(2,1)}, bf16[128,1024]{1,0:T(8,128)(2,1)}, u32[]{:S(2)}, u32[]{:S(2)}) collective-permute-start(bf16[128,1024]{1,0:T(8,128)(2,1)} %convert_element_type.215), channel_id=1, source_target_pairs={{0,6},{2,4},{4,2},{6,0},{8,14},{10,12},{12,10},{14,8},{16,22},{18,... | collective-permute-start | bytes 786440 | tf_op jit(solution)/shard_map/ppermute | solution.py:371
  159.5 13.4 %collective-permute-start.31 = (bf16[128,1024]{1,0:T(8,128)(2,1)}, bf16[128,1024]{1,0:T(8,128)(2,1)}, u32[]{:S(2)}, u32[]{:S(2)}) collective-permute-start(bf16[128,1024]{1,0:T(8,128)(2,1)} %convert_element_type.215), channel_id=1, source_target_pairs={{0,4},{2,6},{4,0},{6,2},{8,12},{10,14},{12,8},{14,10},{16,20},{18,... | collective-permute-start | bytes 786440 | tf_op jit(solution)/shard_map/ppermute | solution.py:371
  160.8 12.3 %collective-permute-start.30 = (bf16[128,1024]{1,0:T(8,128)(2,1)}, bf16[128,1024]{1,0:T(8,128)(2,1)}, u32[]{:S(2)}, u32[]{:S(2)}) collective-permute-start(bf16[128,1024]{1,0:T(8,128)(2,1)} %convert_element_type.215), channel_id=1, source_target_pairs={{0,2},{2,0},{4,6},{6,4},{8,10},{10,8},{12,14},{14,12},{16,18},{18,... | collective-permute-start | bytes 786440 | tf_op jit(solution)/shard_map/ppermute | solution.py:371
  176.7 15.5 %collective-permute-start.36 = (bf16[128,1024]{1,0:T(8,128)(2,1)S(1)}, bf16[128,1024]{1,0:T(8,128)(2,1)S(1)}, u32[]{:S(2)}, u32[]{:S(2)}) collective-permute-start(bf16[128,1024]{1,0:T(8,128)(2,1)S(1)} %get-tuple-element.124), channel_id=1, source_target_pairs={{0,6},{2,4},{4,2},{6,0},{8,14},{10,12},{12,10},{14,8},{16,22},{18,... | collective-permute-start | bytes 786440 | tf_op jit(solution)/shard_map/ppermute | solution.py:371
  178.2 14.0 %collective-permute-start.35 = (bf16[128,1024]{1,0:T(8,128)(2,1)S(1)}, bf16[128,1024]{1,0:T(8,128)(2,1)S(1)}, u32[]{:S(2)}, u32[]{:S(2)}) collective-permute-start(bf16[128,1024]{1,0:T(8,128)(2,1)S(1)} %get-tuple-element.125), channel_id=1, source_target_pairs={{0,4},{2,6},{4,0},{6,2},{8,12},{10,14},{12,8},{14,10},{16,20},{18,... | collective-permute-start | bytes 786440 | tf_op jit(solution)/shard_map/ppermute | solution.py:371
  179.6 12.6 %collective-permute-start.33 = (bf16[128,1024]{1,0:T(8,128)(2,1)S(1)}, bf16[128,1024]{1,0:T(8,128)(2,1)S(1)}, u32[]{:S(2)}, u32[]{:S(2)}) collective-permute-start(bf16[128,1024]{1,0:T(8,128)(2,1)S(1)} %get-tuple-element.123), channel_id=1, source_target_pairs={{0,2},{2,0},{4,6},{6,4},{8,10},{10,8},{12,14},{14,12},{16,18},{18,... | collective-permute-start | bytes 786440 | tf_op jit(solution)/shard_map/ppermute | solution.py:371
  201.9 10.3 %collective-permute-start.41 = (bf16[128,1024]{1,0:T(8,128)(2,1)}, bf16[128,1024]{1,0:T(8,128)(2,1)S(1)}, u32[]{:S(2)}, u32[]{:S(2)}) collective-permute-start(bf16[128,1024]{1,0:T(8,128)(2,1)} %get-tuple-element.121), channel_id=1, source_target_pairs={{0,6},{2,4},{4,2},{6,0},{8,14},{10,12},{12,10},{14,8},{16,22},{18,... | collective-permute-start | bytes 786440 | tf_op jit(solution)/shard_map/ppermute | solution.py:371
  203.4 15.7 %collective-permute-start.40 = (bf16[128,1024]{1,0:T(8,128)(2,1)}, bf16[128,1024]{1,0:T(8,128)(2,1)}, u32[]{:S(2)}, u32[]{:S(2)}) collective-permute-start(bf16[128,1024]{1,0:T(8,128)(2,1)} %get-tuple-element.122), channel_id=1, source_target_pairs={{0,4},{2,6},{4,0},{6,2},{8,12},{10,14},{12,8},{14,10},{16,20},{18,... | collective-permute-start | bytes 786440 | tf_op jit(solution)/shard_map/ppermute | solution.py:371
  204.9 15.7 %collective-permute-start.38 = (bf16[128,1024]{1,0:T(8,128)(2,1)}, bf16[128,1024]{1,0:T(8,128)(2,1)}, u32[]{:S(2)}, u32[]{:S(2)}) collective-permute-start(bf16[128,1024]{1,0:T(8,128)(2,1)} %get-tuple-element.120), channel_id=1, source_target_pairs={{0,2},{2,0},{4,6},{6,4},{8,10},{10,8},{12,14},{14,12},{16,18},{18,... | collective-permute-start | bytes 786440 | tf_op jit(solution)/shard_map/ppermute | solution.py:371
  207.6 10.1 %collective-permute-start.39 = (bf16[268,384]{1,0:T(8,128)(2,1)}, bf16[268,384]{1,0:T(8,128)(2,1)S(1)}, u32[]{:S(2)}, u32[]{:S(2)}) collective-permute-start(bf16[268,384]{1,0:T(8,128)(2,1)} %get-tuple-element.84), channel_id=1, source_target_pairs={{0,24},{2,26},{4,28},{6,30},{8,16},{10,18},{12,20},{14,22},{16,8},... | collective-permute-start | bytes 617480 | tf_op jit(solution)/shard_map/ppermute | solution.py:371
  210.4 17.7 %collective-permute-start.43 = (bf16[268,384]{1,0:T(8,128)(2,1)}, bf16[268,384]{1,0:T(8,128)(2,1)S(1)}, u32[]{:S(2)}, u32[]{:S(2)}) collective-permute-start(bf16[268,384]{1,0:T(8,128)(2,1)} %get-tuple-element.89), channel_id=1, source_target_pairs={{0,16},{2,18},{4,20},{6,22},{8,24},{10,26},{12,28},{14,30},{16,0},... | collective-permute-start | bytes 617480 | tf_op jit(solution)/shard_map/ppermute | solution.py:371
  212.2 15.9 %collective-permute-start.42 = (bf16[268,384]{1,0:T(8,128)(2,1)}, bf16[268,384]{1,0:T(8,128)(2,1)S(1)}, u32[]{:S(2)}, u32[]{:S(2)}) collective-permute-start(bf16[268,384]{1,0:T(8,128)(2,1)} %get-tuple-element.88), channel_id=1, source_target_pairs={{0,8},{2,10},{4,12},{6,14},{8,0},{10,2},{12,4},{14,6},{16,24},{18,... | collective-permute-start | bytes 617480 | tf_op jit(solution)/shard_map/ppermute | solution.py:371
  217.7 16.1 %collective-permute-start.48 = (bf16[64,1728]{1,0:T(8,128)(2,1)S(1)}, bf16[64,1728]{1,0:T(8,128)(2,1)S(1)}, u32[]{:S(2)}, u32[]{:S(2)}) collective-permute-start(bf16[64,1728]{1,0:T(8,128)(2,1)S(1)} %get-tuple-element.134), channel_id=1, source_target_pairs={{0,6},{2,4},{4,2},{6,0},{8,14},{10,12},{12,10},{14,8},{16,22},{18,... | collective-permute-start | bytes 663560 | tf_op jit(solution)/shard_map/ppermute | solution.py:371
  219.1 15.6 %collective-permute-start.49 = (bf16[64,1728]{1,0:T(8,128)(2,1)S(1)}, bf16[64,1728]{1,0:T(8,128)(2,1)S(1)}, u32[]{:S(2)}, u32[]{:S(2)}) collective-permute-start(bf16[64,1728]{1,0:T(8,128)(2,1)S(1)} %get-tuple-element.133), channel_id=1, source_target_pairs={{0,4},{2,6},{4,0},{6,2},{8,12},{10,14},{12,8},{14,10},{16,20},{18,... | collective-permute-start | bytes 663560 | tf_op jit(solution)/shard_map/ppermute | solution.py:371
  220.6 14.1 %collective-permute-start.50 = (bf16[64,1728]{1,0:T(8,128)(2,1)S(1)}, bf16[64,1728]{1,0:T(8,128)(2,1)S(1)}, u32[]{:S(2)}, u32[]{:S(2)}) collective-permute-start(bf16[64,1728]{1,0:T(8,128)(2,1)S(1)} %get-tuple-element.132), channel_id=1, source_target_pairs={{0,2},{2,0},{4,6},{6,4},{8,10},{10,8},{12,14},{14,12},{16,18},{18,... | collective-permute-start | bytes 663560 | tf_op jit(solution)/shard_map/ppermute | solution.py:371
  229.0 12.1 %collective-permute-start.46 = (bf16[76,384]{1,0:T(8,128)(2,1)S(1)}, bf16[76,384]{1,0:T(8,128)(2,1)S(1)}, u32[]{:S(2)}, u32[]{:S(2)}) collective-permute-start(bf16[76,384]{1,0:T(8,128)(2,1)S(1)} %get-tuple-element.172), channel_id=1, source_target_pairs={{0,6},{2,4},{4,2},{6,0},{8,14},{10,12},{12,10},{14,8},{16,22},{18,... | collective-permute-start | bytes 175112 | tf_op jit(solution)/shard_map/ppermute | solution.py:371
  231.2 10.0 %collective-permute-start.45 = (bf16[76,384]{1,0:T(8,128)(2,1)S(1)}, bf16[76,384]{1,0:T(8,128)(2,1)S(1)}, u32[]{:S(2)}, u32[]{:S(2)}) collective-permute-start(bf16[76,384]{1,0:T(8,128)(2,1)S(1)} %get-tuple-element.171), channel_id=1, source_target_pairs={{0,4},{2,6},{4,0},{6,2},{8,12},{10,14},{12,8},{14,10},{16,20},{18,... | collective-permute-start | bytes 175112 | tf_op jit(solution)/shard_map/ppermute | solution.py:371
  233.8 7.4 %collective-permute-start.44 = (bf16[76,384]{1,0:T(8,128)(2,1)S(1)}, bf16[76,384]{1,0:T(8,128)(2,1)S(1)}, u32[]{:S(2)}, u32[]{:S(2)}) collective-permute-start(bf16[76,384]{1,0:T(8,128)(2,1)S(1)} %get-tuple-element.170), channel_id=1, source_target_pairs={{0,2},{2,0},{4,6},{6,4},{8,10},{10,8},{12,14},{14,12},{16,18},{18,... | collective-permute-start | bytes 175112 | tf_op jit(solution)/shard_map/ppermute | solution.py:371
  (50 other events, 334.4 us)
Sparse Core Ops, SparseCore 0:
  34.8 72.7 all-gather.2
  138.0 68.0 reduce-scatter.1

commit v3 on v2

--- a/solution.py
+++ b/solution.py
@@ -492,7 +492,6 @@
         dn_own, y_own, z_own, d_own = ffn_half(after(own_n2, dn_other), own_go, ffn_weights, f32)
         dn_sum = dn_own + sent.astype(f32)
         grad_normed_two = reduce_chips(dn_sum)
-        d_own = after(d_own, dn_sum)
 
         ffn_partial = ffn_grads_call(
             (own_n2, other_n2),

time: 255 us -> 279 us (1.094)
  waiting for transfers between devices: 75.6 us -> 93.7 us
  other arithmetic: 29.4 us -> 25 us
  starting transfers between devices: 54.3 us -> 58 us
  matrix products: 9.6 us -> 12.9 us
    ppermute x42, waiting for transfers between devices: 71.2 us -> 86.4 us  [dp_swap(): return lax.ppermute(value, 'dp', [(i, i ^ mask) for i in range(devices)])]
    ppermute x42, starting transfers between devices: 53.8 us -> 57.4 us  [dp_swap(): return lax.ppermute(value, 'dp', [(i, i ^ mask) for i in range(devices)])]
    reduce_scatter x1, waiting for transfers between devices: 0.01 us -> 2.98 us  [body(): lax.psum_scatter(ffn_partial.reshape(depth, band, 3 * units), 'dp', axis_...]
    unnamed x95 -> x87, local copies, waits for them, and re-layouts: 8.92 us -> 9.7 us
  transfers between devices with their start and end apart: 53 -> 53, of which waited for: 23 -> 21; matrix products, arithmetic and copies ran while one was open for 20% -> 17% of each run, Pallas kernels for 10% -> 13%
where the time goes in v3:
time: 279 us; the launch traced here: 275 us
  waiting for transfers between devices  93.7 us (34%)
  starting transfers between devices  58 us (21%)
  Pallas kernels  42.3 us (15%)
  local copies, waits for them, and re-layouts  28.3 us (10%)
  other arithmetic  25 us (9%)
  between operations  15.2 us (5%)
  matrix products  12.9 us (5%)
    ppermute x42, waiting for transfers between devices, dp_swap(): return lax.ppermute(value, 'dp', [(i, i ^ mask) for i in range(devices)])  86.4 us
    ppermute x42, starting transfers between devices, dp_swap(): return lax.ppermute(value, 'dp', [(i, i ^ mask) for i in range(devices)])  57.4 us
    pallas_call x2, Pallas kernels, ffn_half(): pl.pallas_call(ffn_kernel, grid=(tokens // tile,), in_specs=[rows_of(widt...  15.9 us
    pallas_call x1, Pallas kernels, attention_backward(): pl.pallas_call(attention_backward_kernel, grid_spec=pltpu.PrefetchScalarG...  11 us
    unnamed x87, local copies, waits for them, and re-layouts  9.7 us
    pallas_call x1, Pallas kernels, ffn_grads_call(): pl.pallas_call(ffn_grads_kernel, grid=(width // tile,), in_specs=[slab] *...  8.17 us
    pallas_call x1, Pallas kernels, attention_forward(): pl.pallas_call(attention_forward_kernel, grid_spec=pltpu.PrefetchScalarGr...  7.21 us
    reshape x7, local copies, waits for them, and re-layouts, columns(): return grads[:, :, lo:hi].reshape(rows, -1)  6.57 us
  transfers between devices with their start and end apart: 53, of which 21 were waited for; matrix products, arithmetic and copies ran while one was open for 17% of the time, Pallas kernels for 13%

profile of v3, /device:TPU:0, one launch (start us, length us, event | category | flops | bytes accessed | tf_op | source)
XLA Modules:
  0.0 275.4 jit_solution(3110765925367935575)
XLA Ops:
  15.4 4.0 %collective-permute-start = (bf16[64,1728]{1,0:T(8,128)(2,1)S(1)}, bf16[64,1728]{1,0:T(8,128)(2,1)S(1)}, u32[]{:S(2)}, u32[]{:S(2)}) collective-permute-start(bf16[64,1728]{1,0:T(8,128)(2,1)S(1)} %get-tuple-element.135), channel_id=1, source_target_pairs={{0,6},{2,4},{4,2},{6,0},{8,14},{10,12},{12,10},{14,8},{16,22},{18,... | collective-permute-start | bytes 663560 | tf_op jit(solution)/shard_map/ppermute | solution.py:371
  20.1 1.9 collective-permute-start.4
  23.6 3.5 %collective-permute-done.5 = bf16[66,384]{1,0:T(8,128)(2,1)S(1)} collective-permute-done((bf16[66,384]{1,0:T(8,128)(2,1)S(1)}, bf16[66,384]{1,0:T(8,128)(2,1)S(1)}, u32[]{:S(2)}, u32[]{:S(2)}) %collective-permute-start.5) | collective-permute-done | bytes 50720 | tf_op jit(solution)/shard_map/ppermute | solution.py:371
  28.5 3.7 %collective-permute-done.4 = bf16[66,384]{1,0:T(8,128)(2,1)S(1)} collective-permute-done((bf16[66,384]{1,0:T(8,128)(2,1)S(1)}, bf16[66,384]{1,0:T(8,128)(2,1)S(1)}, u32[]{:S(2)}, u32[]{:S(2)}) %collective-permute-start.4) | collective-permute-done | bytes 50720 | tf_op jit(solution)/shard_map/ppermute | solution.py:371
  33.0 1.8 collective-permute-start.6
  34.8 2.5 collective-permute-start.10
  38.8 1.6 collective-permute-done.6
  43.9 1.9 fusion.58
  46.4 3.2 %collective-permute-done.7 = bf16[128,1024]{1,0:T(8,128)(2,1)S(1)} collective-permute-done((bf16[128,1024]{1,0:T(8,128)(2,1)S(1)}, bf16[128,1024]{1,0:T(8,128)(2,1)S(1)}, u32[]{:S(2)}, u32[]{:S(2)}) %collective-permute-start.7) | collective-permute-done | bytes 262176 | tf_op jit(solution)/shard_map/ppermute | solution.py:371
  49.6 4.9 %collective-permute-done.8 = bf16[128,1024]{1,0:T(8,128)(2,1)} collective-permute-done((bf16[128,1024]{1,0:T(8,128)(2,1)S(1)}, bf16[128,1024]{1,0:T(8,128)(2,1)}, u32[]{:S(2)}, u32[]{:S(2)}) %collective-permute-start.8) | collective-permute-done | bytes 262176 | tf_op jit(solution)/shard_map/ppermute | solution.py:371
  56.0 14.0 %collective-permute-done.11 = bf16[256,384]{1,0:T(8,128)(2,1)} collective-permute-done((bf16[256,384]{1,0:T(8,128)(2,1)}, bf16[256,384]{1,0:T(8,128)(2,1)}, u32[]{:S(2)}, u32[]{:S(2)}) %collective-permute-start.11) | collective-permute-done | bytes 196640 | tf_op jit(solution)/shard_map/ppermute | solution.py:371
  72.4 3.0 %collective-permute-start.14 = (bf16[128,1024]{1,0:T(8,128)(2,1)S(1)}, bf16[128,1024]{1,0:T(8,128)(2,1)S(1)}, u32[]{:S(2)}, u32[]{:S(2)}) collective-permute-start(bf16[128,1024]{1,0:T(8,128)(2,1)S(1)} %copy-done.30), channel_id=1, source_target_pairs={{0,4},{2,6},{4,0},{6,2},{8,12},{10,14},{12,8},{14,10},{16,20},{18,... | collective-permute-start | bytes 786440 | tf_op jit(solution)/shard_map/ppermute | solution.py:371
  77.3 7.2 %attention_forward.1 = (bf16[4,128,128]{2,1,0:T(8,128)(2,1)S(1)}, bf16[4,128,128]{2,1,0:T(8,128)(2,1)S(1)}, bf16[4,2,256,256]{3,2,1,0:T(8,128)(2,1)S(1)}) custom-call(s32[1]{0:T(128)} %bitcast.core_ref, f32[4,128,256]{2,1,0:T(8,128)S(1)} %bitcast.188, f32[4,128,256]{2,1,0:T(8,128)S(1)} %bitcast.190, f32[4,256,64]{2,1,0:T(8,128)S(1)} %pad_maximum_fusion.5.cos_ref, ...), custom_call_target="tpu_custom_call" | custom-call | flops 1000000 | bytes 100000 | tf_op jit(solution)/shard_map/attention_forward/pallas_call | solution.py:192
  85.2 2.6 collective-permute-done.16
  88.3 1.6 collective-permute-start.17
  90.1 1.8 collective-permute-start.19
  91.9 5.7 %collective-permute-done.17 = bf16[128,1024]{1,0:T(8,128)(2,1)S(1)} collective-permute-done((bf16[128,1024]{1,0:T(8,128)(2,1)S(1)}, bf16[128,1024]{1,0:T(8,128)(2,1)S(1)}, u32[]{:S(2)}, u32[]{:S(2)}) %collective-permute-start.17) | collective-permute-done | bytes 262176 | tf_op jit(solution)/shard_map/ppermute | solution.py:371
  97.6 6.0 %collective-permute-done.18 = bf16[128,1024]{1,0:T(8,128)(2,1)S(1)} collective-permute-done((bf16[128,1024]{1,0:T(8,128)(2,1)S(1)}, bf16[128,1024]{1,0:T(8,128)(2,1)S(1)}, u32[]{:S(2)}, u32[]{:S(2)}) %collective-permute-start.18) | collective-permute-done | bytes 262176 | tf_op jit(solution)/shard_map/ppermute | solution.py:371
  104.6 1.6 collective-permute-start.21
  107.6 5.8 %collective-permute-done.20 = bf16[128,1024]{1,0:T(8,128)(2,1)S(1)} collective-permute-done((bf16[128,1024]{1,0:T(8,128)(2,1)S(1)}, bf16[128,1024]{1,0:T(8,128)(2,1)S(1)}, u32[]{:S(2)}, u32[]{:S(2)}) %collective-permute-start.20) | collective-permute-done | bytes 262176 | tf_op jit(solution)/shard_map/ppermute | solution.py:371
  113.3 4.1 %collective-permute-done.21 = bf16[128,1024]{1,0:T(8,128)(2,1)S(1)} collective-permute-done((bf16[128,1024]{1,0:T(8,128)(2,1)S(1)}, bf16[128,1024]{1,0:T(8,128)(2,1)S(1)}, u32[]{:S(2)}, u32[]{:S(2)}) %collective-permute-start.21) | collective-permute-done | bytes 262176 | tf_op jit(solution)/shard_map/ppermute | solution.py:371
  118.6 1.6 collective-permute-done.23.n_ref.n1_ref
  123.8 7.9 %ffn_half.2 = (bf16[512,1024]{1,0:T(8,128)(2,1)}, bf16[512,1024]{1,0:T(8,128)(2,1)}, bf16[512,576]{1,0:T(8,128)(2,1)S(1)}, bf16[512,1152]{1,0:T(8,128)(2,1)S(1)}) custom-call(bf16[512,1024]{1,0:T(8,128)(2,1)S(1)} %copy-done.13, bf16[512,1024]{1,0:T(8,128)(2,1)S(1)} %copy-done.11, bf16[1024,1728]{1,0:T(8,128)(2,1)} %all-gather.3.cloned.1.call-done.w_ref), custom_call_target="tpu_custom_call" | custom-call | flops 1000000 | bytes 100000 | tf_op jit(solution)/shard_map/ffn_half/pallas_call | solution.py:291
  132.8 8.0 %ffn_half.3 = (f32[512,1024]{1,0:T(8,128)S(1)}, f32[512,1024]{1,0:T(8,128)}, bf16[512,576]{1,0:T(8,128)(2,1)S(1)}, bf16[512,1152]{1,0:T(8,128)(2,1)S(1)}) custom-call(bf16[512,1024]{1,0:T(8,128)(2,1)S(1)} %pad_maximum_fusion.1.n_ref.n0_ref, bf16[512,1024]{1,0:T(8,128)(2,1)S(1)} %constant_dynamic-update-slice_fusion.g_ref.g0_ref, ...), custom_call_target="tpu_custom_call" | custom-call | flops 1000000 | bytes 100000 | tf_op jit(solution)/shard_map/ffn_half/pallas_call | solution.py:291
  143.3 8.2 %ffn_grads.1 = bf16[1024,1728]{1,0:T(8,128)(2,1)} custom-call(bf16[512,1024]{1,0:T(8,128)(2,1)S(1)} %pad_maximum_fusion.1.n_ref.n0_ref, bf16[512,1024]{1,0:T(8,128)(2,1)S(1)} %copy-done.13, bf16[512,1024]{1,0:T(8,128)(2,1)S(1)} %constant_dynamic-update-slice_fusion.g_ref.g0_ref, bf16[512,1024]{1,0:T(8,128)(2,1)S(1)} %copy-done.11, ...), custom_call_target="tpu_custom_call" | custom-call | flops 3623878656 | bytes 11272192 | tf_op jit(solution)/shard_map/ffn_grads/pallas_call | solution.py:330
  151.5 1.6 copy-done.3
  153.0 1.7 fusion.69
  156.7 1.6 collective-permute-start.29
  158.4 5.6 %collective-permute-done.27 = bf16[128,1024]{1,0:T(8,128)(2,1)S(1)} collective-permute-done((bf16[128,1024]{1,0:T(8,128)(2,1)S(1)}, bf16[128,1024]{1,0:T(8,128)(2,1)S(1)}, u32[]{:S(2)}, u32[]{:S(2)}) %collective-permute-start.27) | collective-permute-done | bytes 262176 | tf_op jit(solution)/shard_map/ppermute | solution.py:371
  164.0 6.2 %collective-permute-done.28 = bf16[128,1024]{1,0:T(8,128)(2,1)S(1)} collective-permute-done((bf16[128,1024]{1,0:T(8,128)(2,1)S(1)}, bf16[128,1024]{1,0:T(8,128)(2,1)S(1)}, u32[]{:S(2)}, u32[]{:S(2)}) %collective-permute-start.28) | collective-permute-done | bytes 262176 | tf_op jit(solution)/shard_map/ppermute | solution.py:371
  174.4 5.8 %collective-permute-done.30 = bf16[128,1024]{1,0:T(8,128)(2,1)S(1)} collective-permute-done((bf16[128,1024]{1,0:T(8,128)(2,1)S(1)}, bf16[128,1024]{1,0:T(8,128)(2,1)S(1)}, u32[]{:S(2)}, u32[]{:S(2)}) %collective-permute-start.30) | collective-permute-done | bytes 262176 | tf_op jit(solution)/shard_map/ppermute | solution.py:371
  180.1 4.1 %collective-permute-done.31 = bf16[128,1024]{1,0:T(8,128)(2,1)S(1)} collective-permute-done((bf16[128,1024]{1,0:T(8,128)(2,1)S(1)}, bf16[128,1024]{1,0:T(8,128)(2,1)S(1)}, u32[]{:S(2)}, u32[]{:S(2)}) %collective-permute-start.31) | collective-permute-done | bytes 262176 | tf_op jit(solution)/shard_map/ppermute | solution.py:371
  184.4 1.9 convert_add_fusion.2
  186.6 1.6 collective-permute-start.33
  191.1 11.0 %attention_backward.1 = (bf16[4,128,256]{2,1,0:T(8,128)(2,1)S(1)}, bf16[4,128,256]{2,1,0:T(8,128)(2,1)S(1)}, f32[4,1,128]{2,1,0:T(1,128)S(1)}) custom-call(s32[1]{0:T(128)} %bitcast.core_ref, f32[4,128,256]{2,1,0:T(8,128)S(1)} %bitcast.189, f32[4,128,256]{2,1,0:T(8,128)S(1)} %bitcast.191, bf16[4,128,128]{2,1,0:T(8,128)(2,1)S(1)} %bitcast.200, ...), custom_call_target="tpu_custom_call" | custom-call | flops 1000000 | bytes 100000 | tf_op jit(solution)/shard_map/attention_backward/pallas_call | solution.py:230
  205.8 1.6 fusion.8
  207.5 1.8 fusion.35
  211.0 3.2 %fusion.3 = (f32[1024]{0:T(1024)S(1)}, bf16[512,1024]{1,0:T(8,128)(2,1)S(1)}, f32[512,1024]{1,0:T(8,128)}) fusion(bf16[512,1024]{1,0:T(8,128)(2,1)S(1)} %copy-done.23, f32[512]{0:T(512)S(1)} %add_rsqrt_fusion.1, bf16[512,1024]{1,0:T(8,128)(2,1)} %collective-permute-done.37, bf16[512,256]{1,0:T(8,128)(2,1)S(1)} %bitcast.197, bf16[1024,384]{1,0:T(8,128)(2,1)S(1)} %copy-done.20), kind=kOutput, calls=%fused_computation.7 | convolution fusion | flops 272104448 | bytes 6035456 | tf_op jit(solution)/shard_map/dot_general | solution.py:32
  218.6 1.9 pad_maximum_fusion.8
  220.5 3.0 %reduce-scatter.2.cloned.1.call-done = bf16[1,256,1728]{2,1,0:T(8,128)(2,1)} async-done(((bf16[4,256,1728]{2,1,0:T(8,128)(2,1)}), bf16[1,256,1728]{2,1,0:T(8,128)(2,1)}) %reduce-scatter.2.cloned.1.call-update) | async-done | bytes 884752 | tf_op jit(solution)/shard_map/reduce_scatter | solution.py:502
  224.9 3.3 %collective-permute-start.43 = (bf16[268,384]{1,0:T(8,128)(2,1)}, bf16[268,384]{1,0:T(8,128)(2,1)S(1)}, u32[]{:S(2)}, u32[]{:S(2)}) collective-permute-start(bf16[268,384]{1,0:T(8,128)(2,1)} %get-tuple-element.87), channel_id=1, source_target_pairs={{0,16},{2,18},{4,20},{6,22},{8,24},{10,26},{12,28},{14,30},{16,0},... | collective-permute-start | bytes 617480 | tf_op jit(solution)/shard_map/ppermute | solution.py:371
  229.4 5.4 %collective-permute-done.42 = bf16[268,384]{1,0:T(8,128)(2,1)S(1)} collective-permute-done((bf16[268,384]{1,0:T(8,128)(2,1)}, bf16[268,384]{1,0:T(8,128)(2,1)S(1)}, u32[]{:S(2)}, u32[]{:S(2)}) %collective-permute-start.42) | collective-permute-done | bytes 205856 | tf_op jit(solution)/shard_map/ppermute | solution.py:371
  234.8 1.6 collective-permute-start.50
  237.7 2.4 collective-permute-start.39
  240.1 5.5 %collective-permute-done.39 = bf16[268,384]{1,0:T(8,128)(2,1)S(1)} collective-permute-done((bf16[268,384]{1,0:T(8,128)(2,1)}, bf16[268,384]{1,0:T(8,128)(2,1)S(1)}, u32[]{:S(2)}, u32[]{:S(2)}) %collective-permute-start.39) | collective-permute-done | bytes 205856 | tf_op jit(solution)/shard_map/ppermute | solution.py:371
  245.6 1.5 collective-permute-start.49
  250.3 1.5 collective-permute-start.45
  253.2 2.1 fusion.14
  (273 shorter events, 76.2 us)
Async XLA Ops:
  7.2 114.1 %all-gather.3.cloned.1.call-start = ((), (), s32[]{:S(2)}) async-start(), calls=%async_computation.2 | async-start | bytes 4587520 | tf_op jit(solution)/shard_map/all_gather | solution.py:446
  15.4 21.9 %collective-permute-start = (bf16[64,1728]{1,0:T(8,128)(2,1)S(1)}, bf16[64,1728]{1,0:T(8,128)(2,1)S(1)}, u32[]{:S(2)}, u32[]{:S(2)}) collective-permute-start(bf16[64,1728]{1,0:T(8,128)(2,1)S(1)} %get-tuple-element.135), channel_id=1, source_target_pairs={{0,6},{2,4},{4,2},{6,0},{8,14},{10,12},{12,10},{14,8},{16,22},{18,... | collective-permute-start | bytes 663560 | tf_op jit(solution)/shard_map/ppermute | solution.py:371
  19.4 18.2 %collective-permute-start.1 = (bf16[64,1728]{1,0:T(8,128)(2,1)S(1)}, bf16[64,1728]{1,0:T(8,128)(2,1)S(1)}, u32[]{:S(2)}, u32[]{:S(2)}) collective-permute-start(bf16[64,1728]{1,0:T(8,128)(2,1)S(1)} %get-tuple-element.134), channel_id=1, source_target_pairs={{0,4},{2,6},{4,0},{6,2},{8,12},{10,14},{12,8},{14,10},{16,20},{18,... | collective-permute-start | bytes 663560 | tf_op jit(solution)/shard_map/ppermute | solution.py:371
  20.1 12.2 %collective-permute-start.4 = (bf16[66,384]{1,0:T(8,128)(2,1)S(1)}, bf16[66,384]{1,0:T(8,128)(2,1)S(1)}, u32[]{:S(2)}, u32[]{:S(2)}) collective-permute-start(bf16[66,384]{1,0:T(8,128)(2,1)S(1)} %get-tuple-element.156), channel_id=1, source_target_pairs={{0,4},{2,6},{4,0},{6,2},{8,12},{10,14},{12,8},{14,10},{16,20},{18,... | collective-permute-start | bytes 152072 | tf_op jit(solution)/shard_map/ppermute | solution.py:371
  22.0 10.2 %collective-permute-start.3 = (bf16[66,384]{1,0:T(8,128)(2,1)S(1)}, bf16[66,384]{1,0:T(8,128)(2,1)S(1)}, u32[]{:S(2)}, u32[]{:S(2)}) collective-permute-start(bf16[66,384]{1,0:T(8,128)(2,1)S(1)} %get-tuple-element.157), channel_id=1, source_target_pairs={{0,6},{2,4},{4,2},{6,0},{8,14},{10,12},{12,10},{14,8},{16,22},{18,... | collective-permute-start | bytes 152072 | tf_op jit(solution)/shard_map/ppermute | solution.py:371
  27.1 10.5 %collective-permute-start.2 = (bf16[64,1728]{1,0:T(8,128)(2,1)S(1)}, bf16[64,1728]{1,0:T(8,128)(2,1)S(1)}, u32[]{:S(2)}, u32[]{:S(2)}) collective-permute-start(bf16[64,1728]{1,0:T(8,128)(2,1)S(1)} %get-tuple-element.133), channel_id=1, source_target_pairs={{0,2},{2,0},{4,6},{6,4},{8,10},{10,8},{12,14},{14,12},{16,18},{18,... | collective-permute-start | bytes 663560 | tf_op jit(solution)/shard_map/ppermute | solution.py:371
  33.0 7.4 %collective-permute-start.6 = (bf16[256,384]{1,0:T(8,128)(2,1)}, bf16[256,384]{1,0:T(8,128)(2,1)S(1)}, u32[]{:S(2)}, u32[]{:S(2)}) collective-permute-start(bf16[256,384]{1,0:T(8,128)(2,1)} %pad_maximum_fusion.14), channel_id=1, source_target_pairs={{0,8},{2,10},{4,12},{6,14},{8,0},{10,2},{12,4},{14,6},{16,24},{18,... | collective-permute-start | bytes 589832 | tf_op jit(solution)/shard_map/ppermute | solution.py:371
  34.8 21.2 %collective-permute-start.10 = (bf16[256,384]{1,0:T(8,128)(2,1)}, bf16[256,384]{1,0:T(8,128)(2,1)}, u32[]{:S(2)}, u32[]{:S(2)}) collective-permute-start(bf16[256,384]{1,0:T(8,128)(2,1)} %pad_maximum_fusion.14), channel_id=1, source_target_pairs={{0,24},{2,26},{4,28},{6,30},{8,16},{10,18},{12,20},{14,22},{16,8},... | collective-permute-start | bytes 589832 | tf_op jit(solution)/shard_map/ppermute | solution.py:371
  37.4 32.6 %collective-permute-start.11 = (bf16[256,384]{1,0:T(8,128)(2,1)}, bf16[256,384]{1,0:T(8,128)(2,1)}, u32[]{:S(2)}, u32[]{:S(2)}) collective-permute-start(bf16[256,384]{1,0:T(8,128)(2,1)} %pad_maximum_fusion.14), channel_id=1, source_target_pairs={{0,16},{2,18},{4,20},{6,22},{8,24},{10,26},{12,28},{14,30},{16,0},... | collective-permute-start | bytes 589832 | tf_op jit(solution)/shard_map/ppermute | solution.py:371
  38.7 184.8 %reduce-scatter.2.cloned.1.call-start = ((), (), s32[]{:S(2)}) async-start(), calls=%async_computation.1 | async-start | bytes 4587520 | tf_op jit(solution)/shard_map/reduce_scatter | solution.py:502
  40.4 9.2 %collective-permute-start.7 = (bf16[128,1024]{1,0:T(8,128)(2,1)S(1)}, bf16[128,1024]{1,0:T(8,128)(2,1)S(1)}, u32[]{:S(2)}, u32[]{:S(2)}) collective-permute-start(bf16[128,1024]{1,0:T(8,128)(2,1)S(1)} %copy-done.26), channel_id=1, source_target_pairs={{0,2},{2,0},{4,6},{6,4},{8,10},{10,8},{12,14},{14,12},{16,18},{18,... | collective-permute-start | bytes 786440 | tf_op jit(solution)/shard_map/ppermute | solution.py:371
  41.9 12.7 %collective-permute-start.8 = (bf16[128,1024]{1,0:T(8,128)(2,1)S(1)}, bf16[128,1024]{1,0:T(8,128)(2,1)}, u32[]{:S(2)}, u32[]{:S(2)}) collective-permute-start(bf16[128,1024]{1,0:T(8,128)(2,1)S(1)} %copy-done.26), channel_id=1, source_target_pairs={{0,4},{2,6},{4,0},{6,2},{8,12},{10,14},{12,8},{14,10},{16,20},{18,... | collective-permute-start | bytes 786440 | tf_op jit(solution)/shard_map/ppermute | solution.py:371
  42.8 11.8 %collective-permute-start.9 = (bf16[128,1024]{1,0:T(8,128)(2,1)S(1)}, bf16[128,1024]{1,0:T(8,128)(2,1)}, u32[]{:S(2)}, u32[]{:S(2)}) collective-permute-start(bf16[128,1024]{1,0:T(8,128)(2,1)S(1)} %copy-done.26), channel_id=1, source_target_pairs={{0,6},{2,4},{4,2},{6,0},{8,14},{10,12},{12,10},{14,8},{16,22},{18,... | collective-permute-start | bytes 786440 | tf_op jit(solution)/shard_map/ppermute | solution.py:371
  55.9 20.6 %collective-permute-start.12 = (bf16[512,1024]{1,0:T(8,128)(2,1)S(1)}, bf16[512,1024]{1,0:T(8,128)(2,1)S(1)}, u32[]{:S(2)}, u32[]{:S(2)}) collective-permute-start(bf16[512,1024]{1,0:T(8,128)(2,1)S(1)} %get-tuple-element.104), channel_id=1, source_target_pairs={{0,1},{1,0},{2,3},{3,2},{4,5},{5,4},{6,7},{7,6},{8,9},{9,8},{10,11... | collective-permute-start | bytes 3145736 | tf_op jit(solution)/shard_map/ppermute | solution.py:374
  72.3 12.2 %collective-permute-start.15 = (bf16[128,1024]{1,0:T(8,128)(2,1)S(1)}, bf16[128,1024]{1,0:T(8,128)(2,1)S(1)}, u32[]{:S(2)}, u32[]{:S(2)}) collective-permute-start(bf16[128,1024]{1,0:T(8,128)(2,1)S(1)} %copy-done.30), channel_id=1, source_target_pairs={{0,6},{2,4},{4,2},{6,0},{8,14},{10,12},{12,10},{14,8},{16,22},{18,... | collective-permute-start | bytes 786440 | tf_op jit(solution)/shard_map/ppermute | solution.py:371
  72.4 12.1 %collective-permute-start.14 = (bf16[128,1024]{1,0:T(8,128)(2,1)S(1)}, bf16[128,1024]{1,0:T(8,128)(2,1)S(1)}, u32[]{:S(2)}, u32[]{:S(2)}) collective-permute-start(bf16[128,1024]{1,0:T(8,128)(2,1)S(1)} %copy-done.30), channel_id=1, source_target_pairs={{0,4},{2,6},{4,0},{6,2},{8,12},{10,14},{12,8},{14,10},{16,20},{18,... | collective-permute-start | bytes 786440 | tf_op jit(solution)/shard_map/ppermute | solution.py:371
  75.4 9.2 %collective-permute-start.13 = (bf16[128,1024]{1,0:T(8,128)(2,1)S(1)}, bf16[128,1024]{1,0:T(8,128)(2,1)S(1)}, u32[]{:S(2)}, u32[]{:S(2)}) collective-permute-start(bf16[128,1024]{1,0:T(8,128)(2,1)S(1)} %copy-done.30), channel_id=1, source_target_pairs={{0,2},{2,0},{4,6},{6,4},{8,10},{10,8},{12,14},{14,12},{16,18},{18,... | collective-permute-start | bytes 786440 | tf_op jit(solution)/shard_map/ppermute | solution.py:371
  88.3 9.2 %collective-permute-start.17 = (bf16[128,1024]{1,0:T(8,128)(2,1)S(1)}, bf16[128,1024]{1,0:T(8,128)(2,1)S(1)}, u32[]{:S(2)}, u32[]{:S(2)}) collective-permute-start(bf16[128,1024]{1,0:T(8,128)(2,1)S(1)} %get-tuple-element.127), channel_id=1, source_target_pairs={{0,2},{2,0},{4,6},{6,4},{8,10},{10,8},{12,14},{14,12},{16,18},{18,... | collective-permute-start | bytes 786440 | tf_op jit(solution)/shard_map/ppermute | solution.py:371
  89.9 13.7 %collective-permute-start.18 = (bf16[128,1024]{1,0:T(8,128)(2,1)S(1)}, bf16[128,1024]{1,0:T(8,128)(2,1)S(1)}, u32[]{:S(2)}, u32[]{:S(2)}) collective-permute-start(bf16[128,1024]{1,0:T(8,128)(2,1)S(1)} %get-tuple-element.129), channel_id=1, source_target_pairs={{0,4},{2,6},{4,0},{6,2},{8,12},{10,14},{12,8},{14,10},{16,20},{18,... | collective-permute-start | bytes 786440 | tf_op jit(solution)/shard_map/ppermute | solution.py:371
  90.1 13.6 %collective-permute-start.19 = (bf16[128,1024]{1,0:T(8,128)(2,1)S(1)}, bf16[128,1024]{1,0:T(8,128)(2,1)S(1)}, u32[]{:S(2)}, u32[]{:S(2)}) collective-permute-start(bf16[128,1024]{1,0:T(8,128)(2,1)S(1)} %get-tuple-element.128), channel_id=1, source_target_pairs={{0,6},{2,4},{4,2},{6,0},{8,14},{10,12},{12,10},{14,8},{16,22},{18,... | collective-permute-start | bytes 786440 | tf_op jit(solution)/shard_map/ppermute | solution.py:371
  104.0 9.3 %collective-permute-start.20 = (bf16[128,1024]{1,0:T(8,128)(2,1)S(1)}, bf16[128,1024]{1,0:T(8,128)(2,1)S(1)}, u32[]{:S(2)}, u32[]{:S(2)}) collective-permute-start(bf16[128,1024]{1,0:T(8,128)(2,1)S(1)} %multiply_convert_fusion), channel_id=1, source_target_pairs={{0,2},{2,0},{4,6},{6,4},{8,10},{10,8},{12,14},{14,12},{16,18},{18,... | collective-permute-start | bytes 786440 | tf_op jit(solution)/shard_map/ppermute | solution.py:371
  104.6 12.9 %collective-permute-start.21 = (bf16[128,1024]{1,0:T(8,128)(2,1)S(1)}, bf16[128,1024]{1,0:T(8,128)(2,1)S(1)}, u32[]{:S(2)}, u32[]{:S(2)}) collective-permute-start(bf16[128,1024]{1,0:T(8,128)(2,1)S(1)} %multiply_convert_fusion), channel_id=1, source_target_pairs={{0,4},{2,6},{4,0},{6,2},{8,12},{10,14},{12,8},{14,10},{16,20},{18,... | collective-permute-start | bytes 786440 | tf_op jit(solution)/shard_map/ppermute | solution.py:371
  106.2 11.3 %collective-permute-start.22 = (bf16[128,1024]{1,0:T(8,128)(2,1)S(1)}, bf16[128,1024]{1,0:T(8,128)(2,1)S(1)}, u32[]{:S(2)}, u32[]{:S(2)}) collective-permute-start(bf16[128,1024]{1,0:T(8,128)(2,1)S(1)} %multiply_convert_fusion), channel_id=1, source_target_pairs={{0,6},{2,4},{4,2},{6,0},{8,14},{10,12},{12,10},{14,8},{16,22},{18,... | collective-permute-start | bytes 786440 | tf_op jit(solution)/shard_map/ppermute | solution.py:371
  107.6 10.1 %collective-permute-start.24 = (bf16[512,1024]{1,0:T(8,128)(2,1)S(1)}, bf16[512,1024]{1,0:T(8,128)(2,1)S(1)}, u32[]{:S(2)}, u32[]{:S(2)}) collective-permute-start(bf16[512,1024]{1,0:T(8,128)(2,1)S(1)} %constant_dynamic-update-slice_fusion.g_ref.g0_ref), channel_id=1, source_target_pairs={{0,1},{1,0},{2,3},{3,2},{4,5},{5,4},{6,7},{7,6},{8,9},{9,8},{10,11... | collective-permute-start | bytes 3145736 | tf_op jit(solution)/shard_map/ppermute | solution.py:374
  132.6 18.8 %collective-permute-start.26 = (bf16[512,1024]{1,0:T(8,128)(2,1)}, bf16[512,1024]{1,0:T(8,128)(2,1)}, u32[]{:S(2)}, u32[]{:S(2)}) collective-permute-start(bf16[512,1024]{1,0:T(8,128)(2,1)} %get-tuple-element.62), channel_id=1, source_target_pairs={{0,1},{1,0},{2,3},{3,2},{4,5},{5,4},{6,7},{7,6},{8,9},{9,8},{10,11... | collective-permute-start | bytes 3145736 | tf_op jit(solution)/shard_map/ppermute | solution.py:374
  154.8 9.2 %collective-permute-start.27 = (bf16[128,1024]{1,0:T(8,128)(2,1)S(1)}, bf16[128,1024]{1,0:T(8,128)(2,1)S(1)}, u32[]{:S(2)}, u32[]{:S(2)}) collective-permute-start(bf16[128,1024]{1,0:T(8,128)(2,1)S(1)} %get-tuple-element.124), channel_id=1, source_target_pairs={{0,2},{2,0},{4,6},{6,4},{8,10},{10,8},{12,14},{14,12},{16,18},{18,... | collective-permute-start | bytes 786440 | tf_op jit(solution)/shard_map/ppermute | solution.py:371
  156.3 13.9 %collective-permute-start.28 = (bf16[128,1024]{1,0:T(8,128)(2,1)S(1)}, bf16[128,1024]{1,0:T(8,128)(2,1)S(1)}, u32[]{:S(2)}, u32[]{:S(2)}) collective-permute-start(bf16[128,1024]{1,0:T(8,128)(2,1)S(1)} %get-tuple-element.126), channel_id=1, source_target_pairs={{0,4},{2,6},{4,0},{6,2},{8,12},{10,14},{12,8},{14,10},{16,20},{18,... | collective-permute-start | bytes 786440 | tf_op jit(solution)/shard_map/ppermute | solution.py:371
  156.7 13.5 %collective-permute-start.29 = (bf16[128,1024]{1,0:T(8,128)(2,1)S(1)}, bf16[128,1024]{1,0:T(8,128)(2,1)S(1)}, u32[]{:S(2)}, u32[]{:S(2)}) collective-permute-start(bf16[128,1024]{1,0:T(8,128)(2,1)S(1)} %get-tuple-element.125), channel_id=1, source_target_pairs={{0,6},{2,4},{4,2},{6,0},{8,14},{10,12},{12,10},{14,8},{16,22},{18,... | collective-permute-start | bytes 786440 | tf_op jit(solution)/shard_map/ppermute | solution.py:371
  158.4 26.0 %collective-permute-start.25 = (bf16[512,1024]{1,0:T(8,128)(2,1)}, bf16[512,1024]{1,0:T(8,128)(2,1)}, u32[]{:S(2)}, u32[]{:S(2)}) collective-permute-start(bf16[512,1024]{1,0:T(8,128)(2,1)} %get-tuple-element.65), channel_id=1, source_target_pairs={{0,1},{1,0},{2,3},{3,2},{4,5},{5,4},{6,7},{7,6},{8,9},{9,8},{10,11... | collective-permute-start | bytes 3145736 | tf_op jit(solution)/shard_map/ppermute | solution.py:374
  170.8 9.3 %collective-permute-start.30 = (bf16[128,1024]{1,0:T(8,128)(2,1)S(1)}, bf16[128,1024]{1,0:T(8,128)(2,1)S(1)}, u32[]{:S(2)}, u32[]{:S(2)}) collective-permute-start(bf16[128,1024]{1,0:T(8,128)(2,1)S(1)} %convert_element_type.215), channel_id=1, source_target_pairs={{0,2},{2,0},{4,6},{6,4},{8,10},{10,8},{12,14},{14,12},{16,18},{18,... | collective-permute-start | bytes 786440 | tf_op jit(solution)/shard_map/ppermute | solution.py:371
  171.5 12.7 %collective-permute-start.31 = (bf16[128,1024]{1,0:T(8,128)(2,1)S(1)}, bf16[128,1024]{1,0:T(8,128)(2,1)S(1)}, u32[]{:S(2)}, u32[]{:S(2)}) collective-permute-start(bf16[128,1024]{1,0:T(8,128)(2,1)S(1)} %convert_element_type.215), channel_id=1, source_target_pairs={{0,4},{2,6},{4,0},{6,2},{8,12},{10,14},{12,8},{14,10},{16,20},{18,... | collective-permute-start | bytes 786440 | tf_op jit(solution)/shard_map/ppermute | solution.py:371
  172.8 11.3 %collective-permute-start.32 = (bf16[128,1024]{1,0:T(8,128)(2,1)S(1)}, bf16[128,1024]{1,0:T(8,128)(2,1)S(1)}, u32[]{:S(2)}, u32[]{:S(2)}) collective-permute-start(bf16[128,1024]{1,0:T(8,128)(2,1)S(1)} %convert_element_type.215), channel_id=1, source_target_pairs={{0,6},{2,4},{4,2},{6,0},{8,14},{10,12},{12,10},{14,8},{16,22},{18,... | collective-permute-start | bytes 786440 | tf_op jit(solution)/shard_map/ppermute | solution.py:371
  186.6 15.5 %collective-permute-start.33 = (bf16[128,1024]{1,0:T(8,128)(2,1)S(1)}, bf16[128,1024]{1,0:T(8,128)(2,1)S(1)}, u32[]{:S(2)}, u32[]{:S(2)}) collective-permute-start(bf16[128,1024]{1,0:T(8,128)(2,1)S(1)} %get-tuple-element.121), channel_id=1, source_target_pairs={{0,2},{2,0},{4,6},{6,4},{8,10},{10,8},{12,14},{14,12},{16,18},{18,... | collective-permute-start | bytes 786440 | tf_op jit(solution)/shard_map/ppermute | solution.py:371
  188.2 14.0 %collective-permute-start.35 = (bf16[128,1024]{1,0:T(8,128)(2,1)S(1)}, bf16[128,1024]{1,0:T(8,128)(2,1)S(1)}, u32[]{:S(2)}, u32[]{:S(2)}) collective-permute-start(bf16[128,1024]{1,0:T(8,128)(2,1)S(1)} %get-tuple-element.123), channel_id=1, source_target_pairs={{0,4},{2,6},{4,0},{6,2},{8,12},{10,14},{12,8},{14,10},{16,20},{18,... | collective-permute-start | bytes 786440 | tf_op jit(solution)/shard_map/ppermute | solution.py:371
  188.8 13.3 %collective-permute-start.36 = (bf16[128,1024]{1,0:T(8,128)(2,1)S(1)}, bf16[128,1024]{1,0:T(8,128)(2,1)S(1)}, u32[]{:S(2)}, u32[]{:S(2)}) collective-permute-start(bf16[128,1024]{1,0:T(8,128)(2,1)S(1)} %get-tuple-element.122), channel_id=1, source_target_pairs={{0,6},{2,4},{4,2},{6,0},{8,14},{10,12},{12,10},{14,8},{16,22},{18,... | collective-permute-start | bytes 786440 | tf_op jit(solution)/shard_map/ppermute | solution.py:371
  203.6 7.3 %collective-permute-start.37 = (bf16[512,1024]{1,0:T(8,128)(2,1)}, bf16[512,1024]{1,0:T(8,128)(2,1)}, u32[]{:S(2)}, u32[]{:S(2)}) collective-permute-start(bf16[512,1024]{1,0:T(8,128)(2,1)} %convolution_convert_fusion.1), channel_id=1, source_target_pairs={{0,1},{1,0},{2,3},{3,2},{4,5},{5,4},{6,7},{7,6},{8,9},{9,8},{10,11... | collective-permute-start | bytes 3145736 | tf_op jit(solution)/shard_map/ppermute | solution.py:374
  215.1 33.1 %collective-permute-start.38 = (bf16[128,1024]{1,0:T(8,128)(2,1)}, bf16[128,1024]{1,0:T(8,128)(2,1)S(1)}, u32[]{:S(2)}, u32[]{:S(2)}) collective-permute-start(bf16[128,1024]{1,0:T(8,128)(2,1)} %get-tuple-element.118), channel_id=1, source_target_pairs={{0,2},{2,0},{4,6},{6,4},{8,10},{10,8},{12,14},{14,12},{16,18},{18,... | collective-permute-start | bytes 786440 | tf_op jit(solution)/shard_map/ppermute | solution.py:371
  216.6 33.0 %collective-permute-start.40 = (bf16[128,1024]{1,0:T(8,128)(2,1)}, bf16[128,1024]{1,0:T(8,128)(2,1)}, u32[]{:S(2)}, u32[]{:S(2)}) collective-permute-start(bf16[128,1024]{1,0:T(8,128)(2,1)} %get-tuple-element.120), channel_id=1, source_target_pairs={{0,4},{2,6},{4,0},{6,2},{8,12},{10,14},{12,8},{14,10},{16,20},{18,... | collective-permute-start | bytes 786440 | tf_op jit(solution)/shard_map/ppermute | solution.py:371
  217.3 33.1 %collective-permute-start.41 = (bf16[128,1024]{1,0:T(8,128)(2,1)}, bf16[128,1024]{1,0:T(8,128)(2,1)}, u32[]{:S(2)}, u32[]{:S(2)}) collective-permute-start(bf16[128,1024]{1,0:T(8,128)(2,1)} %get-tuple-element.119), channel_id=1, source_target_pairs={{0,6},{2,4},{4,2},{6,0},{8,14},{10,12},{12,10},{14,8},{16,22},{18,... | collective-permute-start | bytes 786440 | tf_op jit(solution)/shard_map/ppermute | solution.py:371
  223.5 11.3 %collective-permute-start.42 = (bf16[268,384]{1,0:T(8,128)(2,1)}, bf16[268,384]{1,0:T(8,128)(2,1)S(1)}, u32[]{:S(2)}, u32[]{:S(2)}) collective-permute-start(bf16[268,384]{1,0:T(8,128)(2,1)} %get-tuple-element.86), channel_id=1, source_target_pairs={{0,8},{2,10},{4,12},{6,14},{8,0},{10,2},{12,4},{14,6},{16,24},{18,... | collective-permute-start | bytes 617480 | tf_op jit(solution)/shard_map/ppermute | solution.py:371
  224.9 12.8 %collective-permute-start.43 = (bf16[268,384]{1,0:T(8,128)(2,1)}, bf16[268,384]{1,0:T(8,128)(2,1)S(1)}, u32[]{:S(2)}, u32[]{:S(2)}) collective-permute-start(bf16[268,384]{1,0:T(8,128)(2,1)} %get-tuple-element.87), channel_id=1, source_target_pairs={{0,16},{2,18},{4,20},{6,22},{8,24},{10,26},{12,28},{14,30},{16,0},... | collective-permute-start | bytes 617480 | tf_op jit(solution)/shard_map/ppermute | solution.py:371
  234.8 20.5 %collective-permute-start.50 = (bf16[64,1728]{1,0:T(8,128)(2,1)S(1)}, bf16[64,1728]{1,0:T(8,128)(2,1)S(1)}, u32[]{:S(2)}, u32[]{:S(2)}) collective-permute-start(bf16[64,1728]{1,0:T(8,128)(2,1)S(1)} %get-tuple-element.130), channel_id=1, source_target_pairs={{0,2},{2,0},{4,6},{6,4},{8,10},{10,8},{12,14},{14,12},{16,18},{18,... | collective-permute-start | bytes 663560 | tf_op jit(solution)/shard_map/ppermute | solution.py:371
  237.7 7.9 %collective-permute-start.39 = (bf16[268,384]{1,0:T(8,128)(2,1)}, bf16[268,384]{1,0:T(8,128)(2,1)S(1)}, u32[]{:S(2)}, u32[]{:S(2)}) collective-permute-start(bf16[268,384]{1,0:T(8,128)(2,1)} %get-tuple-element.82), channel_id=1, source_target_pairs={{0,24},{2,26},{4,28},{6,30},{8,16},{10,18},{12,20},{14,22},{16,8},... | collective-permute-start | bytes 617480 | tf_op jit(solution)/shard_map/ppermute | solution.py:371
  245.6 11.1 %collective-permute-start.49 = (bf16[64,1728]{1,0:T(8,128)(2,1)S(1)}, bf16[64,1728]{1,0:T(8,128)(2,1)S(1)}, u32[]{:S(2)}, u32[]{:S(2)}) collective-permute-start(bf16[64,1728]{1,0:T(8,128)(2,1)S(1)} %get-tuple-element.131), channel_id=1, source_target_pairs={{0,4},{2,6},{4,0},{6,2},{8,12},{10,14},{12,8},{14,10},{16,20},{18,... | collective-permute-start | bytes 663560 | tf_op jit(solution)/shard_map/ppermute | solution.py:371
  248.2 8.5 %collective-permute-start.48 = (bf16[64,1728]{1,0:T(8,128)(2,1)S(1)}, bf16[64,1728]{1,0:T(8,128)(2,1)S(1)}, u32[]{:S(2)}, u32[]{:S(2)}) collective-permute-start(bf16[64,1728]{1,0:T(8,128)(2,1)S(1)} %get-tuple-element.132), channel_id=1, source_target_pairs={{0,6},{2,4},{4,2},{6,0},{8,14},{10,12},{12,10},{14,8},{16,22},{18,... | collective-permute-start | bytes 663560 | tf_op jit(solution)/shard_map/ppermute | solution.py:371
  249.6 13.5 %collective-permute-start.44 = (bf16[76,384]{1,0:T(8,128)(2,1)S(1)}, bf16[76,384]{1,0:T(8,128)(2,1)S(1)}, u32[]{:S(2)}, u32[]{:S(2)}) collective-permute-start(bf16[76,384]{1,0:T(8,128)(2,1)S(1)} %get-tuple-element.168), channel_id=1, source_target_pairs={{0,2},{2,0},{4,6},{6,4},{8,10},{10,8},{12,14},{14,12},{16,18},{18,... | collective-permute-start | bytes 175112 | tf_op jit(solution)/shard_map/ppermute | solution.py:371
  250.3 12.8 %collective-permute-start.45 = (bf16[76,384]{1,0:T(8,128)(2,1)S(1)}, bf16[76,384]{1,0:T(8,128)(2,1)S(1)}, u32[]{:S(2)}, u32[]{:S(2)}) collective-permute-start(bf16[76,384]{1,0:T(8,128)(2,1)S(1)} %get-tuple-element.169), channel_id=1, source_target_pairs={{0,4},{2,6},{4,0},{6,2},{8,12},{10,14},{12,8},{14,10},{16,20},{18,... | collective-permute-start | bytes 175112 | tf_op jit(solution)/shard_map/ppermute | solution.py:371
  255.3 7.9 %collective-permute-start.46 = (bf16[76,384]{1,0:T(8,128)(2,1)S(1)}, bf16[76,384]{1,0:T(8,128)(2,1)S(1)}, u32[]{:S(2)}, u32[]{:S(2)}) collective-permute-start(bf16[76,384]{1,0:T(8,128)(2,1)S(1)} %get-tuple-element.170), channel_id=1, source_target_pairs={{0,6},{2,4},{4,2},{6,0},{8,14},{10,12},{12,10},{14,8},{16,22},{18,... | collective-permute-start | bytes 175112 | tf_op jit(solution)/shard_map/ppermute | solution.py:371
  (46 other events, 362.0 us)
Sparse Core Ops, SparseCore 0:
  38.9 75.9 all-gather.2
  151.6 71.9 reduce-scatter.1
